TPU v7x, 32 devices: a whole 2x2x4 slice. The times are simulated.
32 devices in a mesh: gx: 8 (over y, x, core), gy: 4 (over z).
Axes of the slice: x: 2, y: 2, z: 4, core: 2. Of those that a mesh axis runs over, the one named last changes fastest.
Arguments:
- basis_vec: float32 [16, 128, 1024], P(None, 'gx', 'gy'), may hold values from -6 to 6
- conductivity: float32 [16, 128, 1024], P(None, 'gx', 'gy'), may hold values from 0.2 to 5
- sign_vals: int32 [128, 1024], P('gx', 'gy'), may hold values from -1 to 1, as said below
- sample_cols: int32 [64], P('gy'), may hold values from 0 to 255, as said below
Outputs:
- precond: float32 [16, 128, 1024], P(None, 'gx', 'gy')
- image_vec: float32 [16, 128, 1024], P(None, 'gx', 'gy')
- sketch: float32 [16, 128, 16], P(None, 'gx')
Inputs may be any that keep to these rules, and one draw needn't show every extreme that they name: `sign_vals`: each entry is -1 or 1. `sample_cols`: the entries of each aligned block of 16 are distinct column offsets within one block of 256 columns.
All inputs are finite; a program needn't handle non-finite values.
Results may differ from a plain program's by a relative error of at most 0.0002.
Values sent between devices are 32-bit elements; how exact they have to be, the bound alone decides.
No kernel may reach another device: no remote copies, remote signals or barrier semaphores. Data moves between devices by JAX's collectives and lax.ppermute only.
A program may use at most 64 MiB of HBM per device.

v0:
```python
import jax
import jax.numpy as jnp
from jax import lax
from jax.sharding import PartitionSpec as P

SWEEPS = 8


reaction = 0.5
lowest = 0.5
highest = 62.0
half_root = 0.7071067811865476


def extended(array, sides, width):
    for axis, dim in sides:
        devices, length = (lax.axis_size(axis), array.shape[dim])
        up = [(i, (i + 1) % devices) for i in range(devices - 1)]
        down = [(j, i) for i, j in up]
        last = lax.slice_in_dim(array, length - width, length, axis=dim)
        leading = lax.slice_in_dim(array, 0, width, axis=dim)
        before = lax.ppermute(last, axis, up)
        after = lax.ppermute(leading, axis, down)
        array = jnp.concatenate([before, array, after], axis=dim)
    return array


def partner_2(array, axis, stride):
    return lax.ppermute(array, axis, [(i, i ^ 1 << stride) for i in range(lax.axis_size(axis))])


def operate(values, conduct):
    padded = jnp.pad(values, ((1, 1), (0, 0), (0, 0)))
    centre_val = padded[1:-1, 1:-1, 1:-1]
    kappa_mid = conduct[1:-1, 1:-1, 1:-1]
    neighbours = (
        (padded[2:, 1:-1, 1:-1], conduct[2:, 1:-1, 1:-1]),
        (padded[:-2, 1:-1, 1:-1], conduct[:-2, 1:-1, 1:-1]),
        (padded[1:-1, 2:, 1:-1], conduct[1:-1, 2:, 1:-1]),
        (padded[1:-1, :-2, 1:-1], conduct[1:-1, :-2, 1:-1]),
        (padded[1:-1, 1:-1, 2:], conduct[1:-1, 1:-1, 2:]),
        (padded[1:-1, 1:-1, :-2], conduct[1:-1, 1:-1, :-2]),
    )
    summed = reaction * centre_val
    for near_value, near_kappa in neighbours:
        summed = summed + 0.5 * (kappa_mid + near_kappa) * (centre_val - near_value)
    return summed


def hartley_table(length):
    row_ids = jnp.arange(length, dtype=jnp.int32)[:, None]
    col_ids = jnp.arange(length, dtype=jnp.int32)[None, :]
    angles = (row_ids * col_ids % length).astype(jnp.float32) * (2.0 * jnp.pi / length)
    return (jnp.cos(angles) + jnp.sin(angles)) / jnp.sqrt(jnp.float32(length))


def shrink(values, margin_from, margin_to):
    offset = margin_from - margin_to
    return values[:, offset : values.shape[1] - offset, offset : values.shape[2] - offset]


def per_device(basis_vec, conductivity, sign_vals, sample_cols):
    depth_cells, row_cells, col_cells = basis_vec.shape
    margin = 4
    conduct = extended(conductivity, (("gx", 1), ("gy", 2)), margin)
    conduct = jnp.pad(conduct, ((1, 1), (0, 0), (0, 0)))
    conduct_one = shrink(conduct, margin, 1)
    middle = (highest + lowest) / 2.0
    spread = (highest - lowest) / 2.0
    sig_ratio = middle / spread
    rho_now = 1.0 / sig_ratio
    direction = basis_vec * (1.0 / middle)
    precond = jnp.zeros_like(basis_vec)
    gx_index = lax.axis_index("gx")
    gy_index = lax.axis_index("gy")
    rows_total = row_cells * lax.axis_size("gx")
    cols_total = col_cells * lax.axis_size("gy")
    direction_pad = direction
    residual_pad = basis_vec
    margin_now = 0
    for sweep_no in range(SWEEPS):
        if sweep_no % 4 == 0 and sweep_no < SWEEPS - 1:
            direction_pad, residual_pad = (
                extended(direction_pad, (("gx", 1), ("gy", 2)), 4),
                extended(residual_pad, (("gx", 1), ("gy", 2)), 4),
            )
            margin_now = 4
        precond = precond + shrink(direction_pad, margin_now, 0)
        if sweep_no < SWEEPS - 1:
            applied = operate(direction_pad, shrink(conduct, 4, margin_now))
            margin_now = margin_now - 1
            row_pos = (
                jnp.arange(row_cells + 2 * margin_now, dtype=jnp.int32)
                + gx_index * row_cells
                - margin_now
            )
            col_pos = (
                jnp.arange(col_cells + 2 * margin_now, dtype=jnp.int32)
                + gy_index * col_cells
                - margin_now
            )
            row_ok = (row_pos >= 0) & (row_pos < rows_total)
            col_ok = (col_pos >= 0) & (col_pos < cols_total)
            residual_pad = (shrink(residual_pad, margin_now + 1, margin_now) - applied) * (
                row_ok[:, None] & col_ok[None, :]
            ).astype(jnp.float32)[None]
            rho_next = 1.0 / (2.0 * sig_ratio - rho_now)
            direction_pad = (
                rho_next * rho_now * shrink(direction_pad, margin_now + 1, margin_now)
                + 2.0 * rho_next / spread * residual_pad
            )
            rho_now = rho_next
    padded = extended(precond, (("gx", 1), ("gy", 2)), 1)
    image_vec = operate(padded, conduct_one)
    flipped = image_vec * sign_vals.astype(jnp.float32)[None]
    hartley_mat = hartley_table(row_cells)
    current = jnp.einsum("jk,dkc->djc", hartley_mat, flipped, precision=lax.Precision.HIGHEST)
    for section_bit in range(lax.axis_size("gx").bit_length() - 1):
        partner = partner_2(current, "gx", section_bit)
        upper_half = lax.axis_index("gx") >> section_bit & 1 == 1
        current = jnp.where(upper_half, partner - current, current + partner) * half_root
    picked = jnp.take(current, sample_cols, axis=2)
    sketch = lax.psum(picked, "gy")
    return (precond, image_vec, sketch)


def solution(mesh):
    in_specs = (P(None, "gx", "gy"), P(None, "gx", "gy"), P("gx", "gy"), P("gy"))
    out_specs = (P(None, "gx", "gy"), P(None, "gx", "gy"), P(None, "gx", None))
    return jax.shard_map(
        per_device, mesh=mesh, in_specs=in_specs, out_specs=out_specs, check_vma=False
    )
```

profile of v0, /device:TPU:0, one launch (start us, length us, event | category | flops | bytes accessed | tf_op | source)
XLA Modules:
  0.0 155.3 jit_solution(9285129976066306890)
XLA Ops:
  1.6 2.4 %collective-permute-start.8 = (f32[16,4,256]{2,1,0:T(4,128)S(1)}, f32[16,4,256]{2,1,0:T(4,128)S(1)}, u32[]{:S(2)}, u32[]{:S(2)}) collective-permute-start(f32[16,4,256]{2,1,0:T(4,128)S(1)} %get-tuple-element.45), channel_id=1, source_target_pairs={{0,4},{4,8},{8,12},{12,16},{16,20},{20,24},{24,28},{1,5},{5,9},{9,... | collective-permute-start | bytes 196616 | tf_op jit(solution)/shard_map/ppermute | solution.py:22
  4.0 1.4 collective-permute-start.9
  6.5 5.1 %collective-permute-start = (f32[16,4,256]{2,1,0:T(4,128)S(1)}, f32[16,4,256]{2,1,0:T(4,128)S(1)}, u32[]{:S(2)}, u32[]{:S(2)}) collective-permute-start(f32[16,4,256]{2,1,0:T(4,128)S(1)} %get-tuple-element.47), channel_id=1, source_target_pairs={{0,4},{4,8},{8,12},{12,16},{16,20},{20,24},{24,28},{1,5},{5,9},{9,... | collective-permute-start | bytes 196616 | tf_op jit(solution)/shard_map/ppermute | solution.py:22
  13.9 4.3 %collective-permute-start.4 = (f32[16,4,256]{2,1,0:T(4,128)S(1)}, f32[16,4,256]{2,1,0:T(4,128)S(1)}, u32[]{:S(2)}, u32[]{:S(2)}) collective-permute-start(f32[16,4,256]{2,1,0:T(4,128)S(1)} %get-tuple-element.43), channel_id=1, source_target_pairs={{0,4},{4,8},{8,12},{12,16},{16,20},{20,24},{24,28},{1,5},{5,9},{9,... | collective-permute-start | bytes 196616 | tf_op jit(solution)/shard_map/ppermute | solution.py:22
  21.2 3.5 %collective-permute-start.10 = (f32[16,24,4]{2,1,0:T(8,128)S(1)}, f32[16,24,4]{2,1,0:T(8,128)S(1)}, u32[]{:S(2)}, u32[]{:S(2)}) collective-permute-start(f32[16,24,4]{2,1,0:T(8,128)S(1)} %get-tuple-element.33), channel_id=1, source_target_pairs={{0,1},{1,2},{2,3},{4,5},{5,6},{6,7},{8,9},{9,10},{10,11},{12,13},{... | collective-permute-start | bytes 18440 | tf_op jit(solution)/shard_map/ppermute | solution.py:22
  26.2 4.6 %collective-permute-start.2 = (f32[16,24,4]{2,1,0:T(8,128)S(1)}, f32[16,24,4]{2,1,0:T(8,128)S(1)}, u32[]{:S(2)}, u32[]{:S(2)}) collective-permute-start(f32[16,24,4]{2,1,0:T(8,128)S(1)} %get-tuple-element.35), channel_id=1, source_target_pairs={{0,1},{1,2},{2,3},{4,5},{5,6},{6,7},{8,9},{9,10},{10,11},{12,13},{... | collective-permute-start | bytes 18440 | tf_op jit(solution)/shard_map/ppermute | solution.py:22
  32.2 4.6 %collective-permute-start.6 = (f32[16,24,4]{2,1,0:T(8,128)S(1)}, f32[16,24,4]{2,1,0:T(8,128)S(1)}, u32[]{:S(2)}, u32[]{:S(2)}) collective-permute-start(f32[16,24,4]{2,1,0:T(8,128)S(1)} %get-tuple-element.31), channel_id=1, source_target_pairs={{0,1},{1,2},{2,3},{4,5},{5,6},{6,7},{8,9},{9,10},{10,11},{12,13},{... | collective-permute-start | bytes 18440 | tf_op jit(solution)/shard_map/ppermute | solution.py:22
  40.2 1.5 collective-permute-done.6
  41.8 4.7 %collective-permute-done.7 = f32[16,24,4]{2,1,0:T(8,128)S(1)} collective-permute-done((f32[16,24,4]{2,1,0:T(8,128)S(1)}, f32[16,24,4]{2,1,0:T(8,128)S(1)}, u32[]{:S(2)}, u32[]{:S(2)}) %collective-permute-start.7) | collective-permute-done | bytes 6176 | tf_op jit(solution)/shard_map/ppermute | solution.py:23
  46.5 2.3 %multiply_add_fusion.4 = (f32[16,22,262]{2,1,0:T(8,128)S(1)}, f32[16,22,262]{2,1,0:T(8,128)S(1)}) fusion(f32[16,24,264]{2,1,0:T(8,128)S(1)} %pad_maximum_fusion.8, f32[22,262]{1,0:T(8,128)S(1)} %and_convert_fusion.2, f32[16,24,264]{2,1,0:T(8,128)S(1)} %pad_maximum_fusion.9, f32[16,24,4]{2,1,0:T(8,128)S(1)} %collective-permute-done.7, ...), kind=kLoop, calls=%fused_computation.199 | loop fusion | flops 3688960 | bytes 8638976 | tf_op jit(solution)/shard_map/add | solution.py:109
  48.8 2.2 %multiply_add_fusion.3 = (f32[16,20,260]{2,1,0:T(8,128)S(1)}, f32[16,20,260]{2,1,0:T(8,128)S(1)}) fusion(f32[16,22,262]{2,1,0:T(8,128)S(1)} %get-tuple-element.17, f32[20,260]{1,0:T(8,128)S(1)} %and_convert_fusion.1, f32[16,24,264]{2,1,0:T(8,128)S(1)} %pad_maximum_fusion.9, f32[16,22,262]{2,1,0:T(8,128)S(1)} %get-tuple-element.18), kind=kLoop, calls=%fused_computation.198 | loop fusion | flops 2995200 | bytes 8370176 | tf_op jit(solution)/shard_map/add | solution.py:109
  51.4 2.1 %multiply_add_fusion.2 = (f32[16,18,258]{2,1,0:T(8,128)S(1)}, f32[16,18,258]{2,1,0:T(8,128)S(1)}, f32[16,18,258]{2,1,0:T(8,128)S(1)}) fusion(f32[16,20,260]{2,1,0:T(8,128)S(1)} %get-tuple-element.15, f32[18,258]{1,0:T(8,128)S(1)} %and_convert_fusion, f32[16,24,260]{2,1,0:T(8,128)S(1)} %get-tuple-element.30, f32[16,24,264]{2,1,0:T(8,128)S(1)} %pad_maximum_fusion.9, ...), kind=kLoop, calls=%fused_computation.197 | loop fusion | flops 2674944 | bytes 8596224 | tf_op jit(solution)/shard_map/add | solution.py:109
  54.5 2.0 %collective-permute-start.12 = (f32[16,4,256]{2,1,0:T(4,128)S(1)}, f32[16,4,256]{2,1,0:T(4,128)S(1)}, u32[]{:S(2)}, u32[]{:S(2)}) collective-permute-start(f32[16,4,256]{2,1,0:T(4,128)S(1)} %get-tuple-element.41), channel_id=1, source_target_pairs={{0,4},{4,8},{8,12},{12,16},{16,20},{20,24},{24,28},{1,5},{5,9},{9,... | collective-permute-start | bytes 196616 | tf_op jit(solution)/shard_map/ppermute | solution.py:22
  57.9 5.8 %collective-permute-start.16 = (f32[16,4,256]{2,1,0:T(4,128)S(1)}, f32[16,4,256]{2,1,0:T(4,128)S(1)}, u32[]{:S(2)}, u32[]{:S(2)}) collective-permute-start(f32[16,4,256]{2,1,0:T(4,128)S(1)} %get-tuple-element.39), channel_id=1, source_target_pairs={{0,4},{4,8},{8,12},{12,16},{16,20},{20,24},{24,28},{1,5},{5,9},{9,... | collective-permute-start | bytes 196616 | tf_op jit(solution)/shard_map/ppermute | solution.py:22
  65.2 3.5 %collective-permute-start.14 = (f32[16,24,4]{2,1,0:T(8,128)S(1)}, f32[16,24,4]{2,1,0:T(8,128)S(1)}, u32[]{:S(2)}, u32[]{:S(2)}) collective-permute-start(f32[16,24,4]{2,1,0:T(8,128)S(1)} %get-tuple-element.27), channel_id=1, source_target_pairs={{0,1},{1,2},{2,3},{4,5},{5,6},{6,7},{8,9},{9,10},{10,11},{12,13},{... | collective-permute-start | bytes 18440 | tf_op jit(solution)/shard_map/ppermute | solution.py:22
  70.2 4.6 %collective-permute-start.18 = (f32[16,24,4]{2,1,0:T(8,128)S(1)}, f32[16,24,4]{2,1,0:T(8,128)S(1)}, u32[]{:S(2)}, u32[]{:S(2)}) collective-permute-start(f32[16,24,4]{2,1,0:T(8,128)S(1)} %get-tuple-element.25), channel_id=1, source_target_pairs={{0,1},{1,2},{2,3},{4,5},{5,6},{6,7},{8,9},{9,10},{10,11},{12,13},{... | collective-permute-start | bytes 18440 | tf_op jit(solution)/shard_map/ppermute | solution.py:22
  74.8 1.5 collective-permute-start.19
  77.6 1.5 collective-permute-done.18
  79.2 4.7 %collective-permute-done.19 = f32[16,24,4]{2,1,0:T(8,128)S(1)} collective-permute-done((f32[16,24,4]{2,1,0:T(8,128)S(1)}, f32[16,24,4]{2,1,0:T(8,128)S(1)}, u32[]{:S(2)}, u32[]{:S(2)}) %collective-permute-start.19) | collective-permute-done | bytes 6176 | tf_op jit(solution)/shard_map/ppermute | solution.py:23
  83.9 2.3 %multiply_add_fusion.1 = (f32[16,22,262]{2,1,0:T(8,128)S(1)}, f32[16,22,262]{2,1,0:T(8,128)S(1)}) fusion(f32[16,24,264]{2,1,0:T(8,128)S(1)} %pad_maximum_fusion.11, f32[22,262]{1,0:T(8,128)S(1)} %and_convert_fusion.2, f32[16,24,264]{2,1,0:T(8,128)S(1)} %pad_maximum_fusion.9, f32[16,24,4]{2,1,0:T(8,128)S(1)} %collective-permute-done.19, ...), kind=kLoop, calls=%fused_computation.196 | loop fusion | flops 3688960 | bytes 8638976 | tf_op jit(solution)/shard_map/add | solution.py:109
  86.2 2.2 %multiply_add_fusion = (f32[16,20,260]{2,1,0:T(8,128)S(1)}, f32[16,20,260]{2,1,0:T(8,128)S(1)}) fusion(f32[16,22,262]{2,1,0:T(8,128)S(1)} %get-tuple-element.8, f32[20,260]{1,0:T(8,128)S(1)} %and_convert_fusion.1, f32[16,24,264]{2,1,0:T(8,128)S(1)} %pad_maximum_fusion.9, f32[16,22,262]{2,1,0:T(8,128)S(1)} %get-tuple-element.9), kind=kLoop, calls=%fused_computation.195 | loop fusion | flops 2995200 | bytes 8370176 | tf_op jit(solution)/shard_map/add | solution.py:109
  88.4 1.8 %fusion.78 = (f32[16,18,258]{2,1,0:T(8,128)S(1)}, f32[16,18,258]{2,1,0:T(8,128)S(1)}, f32[16,18,258]{2,1,0:T(8,128)S(1)}, f32[16,18,258]{2,1,0:T(8,128)S(1)}) fusion(f32[16,20,260]{2,1,0:T(8,128)S(1)} %get-tuple-element.6, f32[16,24,264]{2,1,0:T(8,128)S(1)} %pad_maximum_fusion.9, f32[16,24,260]{2,1,0:T(8,128)S(1)} %get-tuple-element.30), kind=kLoop, calls=%fused_computation.108 | loop fusion | flops 1931904 | bytes 7676928 | tf_op jit(solution)/shard_map/add | solution.py:46
  91.4 2.3 %collective-permute-start.20 = (f32[16,1,256]{2,1,0:T(1,128)S(1)}, f32[16,1,256]{2,1,0:T(1,128)S(1)}, u32[]{:S(2)}, u32[]{:S(2)}) collective-permute-start(f32[16,1,256]{2,1,0:T(1,128)S(1)} %get-tuple-element.37), channel_id=1, source_target_pairs={{0,4},{4,8},{8,12},{12,16},{16,20},{20,24},{24,28},{1,5},{5,9},{9,... | collective-permute-start | bytes 49160 | tf_op jit(solution)/shard_map/ppermute | solution.py:22
  95.0 5.3 %collective-permute-done.21 = f32[16,1,256]{2,1,0:T(1,128)S(1)} collective-permute-done((f32[16,1,256]{2,1,0:T(1,128)S(1)}, f32[16,1,256]{2,1,0:T(1,128)S(1)}, u32[]{:S(2)}, u32[]{:S(2)}) %collective-permute-start.21) | collective-permute-done | bytes 16416 | tf_op jit(solution)/shard_map/ppermute | solution.py:23
  100.5 3.5 %collective-permute-start.22 = (f32[16,18,1]{2,1,0:T(8,128)S(1)}, f32[16,18,1]{2,1,0:T(8,128)S(1)}, u32[]{:S(2)}, u32[]{:S(2)}) collective-permute-start(f32[16,18,1]{2,1,0:T(8,128)S(1)} %get-tuple-element.24), channel_id=1, source_target_pairs={{0,1},{1,2},{2,3},{4,5},{5,6},{6,7},{8,9},{9,10},{10,11},{12,13},{... | collective-permute-start | bytes 3464 | tf_op jit(solution)/shard_map/ppermute | solution.py:22
  105.3 2.4 %collective-permute-done.22 = f32[16,18,1]{2,1,0:T(8,128)S(1)} collective-permute-done((f32[16,18,1]{2,1,0:T(8,128)S(1)}, f32[16,18,1]{2,1,0:T(8,128)S(1)}, u32[]{:S(2)}, u32[]{:S(2)}) %collective-permute-start.22) | collective-permute-done | bytes 1184 | tf_op jit(solution)/shard_map/ppermute | solution.py:22
  107.7 4.7 %collective-permute-done.23 = f32[16,18,1]{2,1,0:T(8,128)S(1)} collective-permute-done((f32[16,18,1]{2,1,0:T(8,128)S(1)}, f32[16,18,1]{2,1,0:T(8,128)S(1)}, u32[]{:S(2)}, u32[]{:S(2)}) %collective-permute-start.23) | collective-permute-done | bytes 1184 | tf_op jit(solution)/shard_map/ppermute | solution.py:23
  116.5 2.8 %collective-permute-start.25 = (f32[16,16,256]{2,1,0:T(8,128)S(1)}, f32[16,16,256]{2,1,0:T(8,128)S(1)}, u32[]{:S(2)}, u32[]{:S(2)}) collective-permute-start(f32[16,16,256]{2,1,0:T(8,128)S(1)} %select_multiply_fusion.2), channel_id=1, source_target_pairs={{0,8},{4,12},{8,0},{12,4},{16,24},{20,28},{24,16},{28,20},{1,9},{5... | collective-permute-start | bytes 786440 | tf_op jit(solution)/shard_map/ppermute | solution.py:29
  119.3 6.8 %collective-permute-done.25 = f32[16,16,256]{2,1,0:T(8,128)S(1)} collective-permute-done((f32[16,16,256]{2,1,0:T(8,128)S(1)}, f32[16,16,256]{2,1,0:T(8,128)S(1)}, u32[]{:S(2)}, u32[]{:S(2)}) %collective-permute-start.25) | collective-permute-done | bytes 262176 | tf_op jit(solution)/shard_map/ppermute | solution.py:29
  126.2 1.8 %collective-permute-start.26 = (f32[16,16,256]{2,1,0:T(8,128)S(1)}, f32[16,16,256]{2,1,0:T(8,128)S(1)}, u32[]{:S(2)}, u32[]{:S(2)}) collective-permute-start(f32[16,16,256]{2,1,0:T(8,128)S(1)} %select_multiply_fusion.1), channel_id=1, source_target_pairs={{0,16},{4,20},{8,24},{12,28},{16,0},{20,4},{24,8},{28,12},{1,17},{... | collective-permute-start | bytes 786440 | tf_op jit(solution)/shard_map/ppermute | solution.py:29
  128.0 6.2 %collective-permute-done.26 = f32[16,16,256]{2,1,0:T(8,128)S(1)} collective-permute-done((f32[16,16,256]{2,1,0:T(8,128)S(1)}, f32[16,16,256]{2,1,0:T(8,128)S(1)}, u32[]{:S(2)}, u32[]{:S(2)}) %collective-permute-start.26) | collective-permute-done | bytes 262176 | tf_op jit(solution)/shard_map/ppermute | solution.py:29
  136.3 18.2 %psum.7 = f32[16,16,16]{1,0,2:T(8,128)S(1)} all-reduce(f32[16,16,16]{1,0,2:T(8,128)S(1)} %select_bitcast_fusion), channel_id=1, replica_groups=mesh['gx'=8,'gy'=4] {'gy'}, use_global_device_ids=true, to_apply=%region_0.1 | all-reduce | flops 4096 | bytes 32768 | tf_op jit(solution)/shard_map/psum | solution.py:123
  (94 shorter events, 31.2 us)
Async XLA Ops:
  1.6 17.1 %collective-permute-start.8 = (f32[16,4,256]{2,1,0:T(4,128)S(1)}, f32[16,4,256]{2,1,0:T(4,128)S(1)}, u32[]{:S(2)}, u32[]{:S(2)}) collective-permute-start(f32[16,4,256]{2,1,0:T(4,128)S(1)} %get-tuple-element.45), channel_id=1, source_target_pairs={{0,4},{4,8},{8,12},{12,16},{16,20},{20,24},{24,28},{1,5},{5,9},{9,... | collective-permute-start | bytes 196616 | tf_op jit(solution)/shard_map/ppermute | solution.py:22
  4.0 28.0 %copy-start.1 = (f32[16,16,256]{2,1,0:T(8,128)S(1)}, f32[16,16,256]{2,1,0:T(8,128)}, u32[]{:S(2)}) copy-start(f32[16,16,256]{2,1,0:T(8,128)} %param.4) | copy-start | bytes 786436
  4.0 16.0 %collective-permute-start.9 = (f32[16,4,256]{2,1,0:T(4,128)S(1)}, f32[16,4,256]{2,1,0:T(4,128)S(1)}, u32[]{:S(2)}, u32[]{:S(2)}) collective-permute-start(f32[16,4,256]{2,1,0:T(4,128)S(1)} %get-tuple-element.46), channel_id=1, source_target_pairs={{4,0},{8,4},{12,8},{16,12},{20,16},{24,20},{28,24},{5,1},{9,5},{13... | collective-permute-start | bytes 196616 | tf_op jit(solution)/shard_map/ppermute | solution.py:23
  6.5 18.2 %collective-permute-start = (f32[16,4,256]{2,1,0:T(4,128)S(1)}, f32[16,4,256]{2,1,0:T(4,128)S(1)}, u32[]{:S(2)}, u32[]{:S(2)}) collective-permute-start(f32[16,4,256]{2,1,0:T(4,128)S(1)} %get-tuple-element.47), channel_id=1, source_target_pairs={{0,4},{4,8},{8,12},{12,16},{16,20},{20,24},{24,28},{1,5},{5,9},{9,... | collective-permute-start | bytes 196616 | tf_op jit(solution)/shard_map/ppermute | solution.py:22
  11.6 14.3 %collective-permute-start.1 = (f32[16,4,256]{2,1,0:T(4,128)S(1)}, f32[16,4,256]{2,1,0:T(4,128)S(1)}, u32[]{:S(2)}, u32[]{:S(2)}) collective-permute-start(f32[16,4,256]{2,1,0:T(4,128)S(1)} %get-tuple-element.48), channel_id=1, source_target_pairs={{4,0},{8,4},{12,8},{16,12},{20,16},{24,20},{28,24},{5,1},{9,5},{13... | collective-permute-start | bytes 196616 | tf_op jit(solution)/shard_map/ppermute | solution.py:23
  13.9 16.8 %collective-permute-start.4 = (f32[16,4,256]{2,1,0:T(4,128)S(1)}, f32[16,4,256]{2,1,0:T(4,128)S(1)}, u32[]{:S(2)}, u32[]{:S(2)}) collective-permute-start(f32[16,4,256]{2,1,0:T(4,128)S(1)} %get-tuple-element.43), channel_id=1, source_target_pairs={{0,4},{4,8},{8,12},{12,16},{16,20},{20,24},{24,28},{1,5},{5,9},{9,... | collective-permute-start | bytes 196616 | tf_op jit(solution)/shard_map/ppermute | solution.py:22
  18.7 13.3 %collective-permute-start.5 = (f32[16,4,256]{2,1,0:T(4,128)S(1)}, f32[16,4,256]{2,1,0:T(4,128)S(1)}, u32[]{:S(2)}, u32[]{:S(2)}) collective-permute-start(f32[16,4,256]{2,1,0:T(4,128)S(1)} %get-tuple-element.44), channel_id=1, source_target_pairs={{4,0},{8,4},{12,8},{16,12},{20,16},{24,20},{28,24},{5,1},{9,5},{13... | collective-permute-start | bytes 196616 | tf_op jit(solution)/shard_map/ppermute | solution.py:23
  21.0 17.1 %copy-start = (f32[16,16,256]{2,1,0:T(8,128)S(1)}, f32[16,16,256]{2,1,0:T(8,128)}, u32[]{:S(2)}) copy-start(f32[16,16,256]{2,1,0:T(8,128)} %param.5) | copy-start | bytes 786436
  21.2 15.6 %collective-permute-start.10 = (f32[16,24,4]{2,1,0:T(8,128)S(1)}, f32[16,24,4]{2,1,0:T(8,128)S(1)}, u32[]{:S(2)}, u32[]{:S(2)}) collective-permute-start(f32[16,24,4]{2,1,0:T(8,128)S(1)} %get-tuple-element.33), channel_id=1, source_target_pairs={{0,1},{1,2},{2,3},{4,5},{5,6},{6,7},{8,9},{9,10},{10,11},{12,13},{... | collective-permute-start | bytes 18440 | tf_op jit(solution)/shard_map/ppermute | solution.py:22
  24.7 13.4 %collective-permute-start.11 = (f32[16,24,4]{2,1,0:T(8,128)S(1)}, f32[16,24,4]{2,1,0:T(8,128)S(1)}, u32[]{:S(2)}, u32[]{:S(2)}) collective-permute-start(f32[16,24,4]{2,1,0:T(8,128)S(1)} %get-tuple-element.34), channel_id=1, source_target_pairs={{1,0},{2,1},{3,2},{5,4},{6,5},{7,6},{9,8},{10,9},{11,10},{13,12},{... | collective-permute-start | bytes 18440 | tf_op jit(solution)/shard_map/ppermute | solution.py:23
  26.2 12.4 %collective-permute-start.2 = (f32[16,24,4]{2,1,0:T(8,128)S(1)}, f32[16,24,4]{2,1,0:T(8,128)S(1)}, u32[]{:S(2)}, u32[]{:S(2)}) collective-permute-start(f32[16,24,4]{2,1,0:T(8,128)S(1)} %get-tuple-element.35), channel_id=1, source_target_pairs={{0,1},{1,2},{2,3},{4,5},{5,6},{6,7},{8,9},{9,10},{10,11},{12,13},{... | collective-permute-start | bytes 18440 | tf_op jit(solution)/shard_map/ppermute | solution.py:22
  30.7 9.1 %collective-permute-start.3 = (f32[16,24,4]{2,1,0:T(8,128)S(1)}, f32[16,24,4]{2,1,0:T(8,128)S(1)}, u32[]{:S(2)}, u32[]{:S(2)}) collective-permute-start(f32[16,24,4]{2,1,0:T(8,128)S(1)} %get-tuple-element.36), channel_id=1, source_target_pairs={{1,0},{2,1},{3,2},{5,4},{6,5},{7,6},{9,8},{10,9},{11,10},{13,12},{... | collective-permute-start | bytes 18440 | tf_op jit(solution)/shard_map/ppermute | solution.py:23
  32.2 9.6 %collective-permute-start.6 = (f32[16,24,4]{2,1,0:T(8,128)S(1)}, f32[16,24,4]{2,1,0:T(8,128)S(1)}, u32[]{:S(2)}, u32[]{:S(2)}) collective-permute-start(f32[16,24,4]{2,1,0:T(8,128)S(1)} %get-tuple-element.31), channel_id=1, source_target_pairs={{0,1},{1,2},{2,3},{4,5},{5,6},{6,7},{8,9},{9,10},{10,11},{12,13},{... | collective-permute-start | bytes 18440 | tf_op jit(solution)/shard_map/ppermute | solution.py:22
  36.8 9.7 %collective-permute-start.7 = (f32[16,24,4]{2,1,0:T(8,128)S(1)}, f32[16,24,4]{2,1,0:T(8,128)S(1)}, u32[]{:S(2)}, u32[]{:S(2)}) collective-permute-start(f32[16,24,4]{2,1,0:T(8,128)S(1)} %get-tuple-element.32), channel_id=1, source_target_pairs={{1,0},{2,1},{3,2},{5,4},{6,5},{7,6},{9,8},{10,9},{11,10},{13,12},{... | collective-permute-start | bytes 18440 | tf_op jit(solution)/shard_map/ppermute | solution.py:23
  54.5 10.5 %collective-permute-start.12 = (f32[16,4,256]{2,1,0:T(4,128)S(1)}, f32[16,4,256]{2,1,0:T(4,128)S(1)}, u32[]{:S(2)}, u32[]{:S(2)}) collective-permute-start(f32[16,4,256]{2,1,0:T(4,128)S(1)} %get-tuple-element.41), channel_id=1, source_target_pairs={{0,4},{4,8},{8,12},{12,16},{16,20},{20,24},{24,28},{1,5},{5,9},{9,... | collective-permute-start | bytes 196616 | tf_op jit(solution)/shard_map/ppermute | solution.py:22
  56.5 8.5 %collective-permute-start.13 = (f32[16,4,256]{2,1,0:T(4,128)S(1)}, f32[16,4,256]{2,1,0:T(4,128)S(1)}, u32[]{:S(2)}, u32[]{:S(2)}) collective-permute-start(f32[16,4,256]{2,1,0:T(4,128)S(1)} %get-tuple-element.42), channel_id=1, source_target_pairs={{4,0},{8,4},{12,8},{16,12},{20,16},{24,20},{28,24},{5,1},{9,5},{13... | collective-permute-start | bytes 196616 | tf_op jit(solution)/shard_map/ppermute | solution.py:23
  57.9 12.1 %collective-permute-start.16 = (f32[16,4,256]{2,1,0:T(4,128)S(1)}, f32[16,4,256]{2,1,0:T(4,128)S(1)}, u32[]{:S(2)}, u32[]{:S(2)}) collective-permute-start(f32[16,4,256]{2,1,0:T(4,128)S(1)} %get-tuple-element.39), channel_id=1, source_target_pairs={{0,4},{4,8},{8,12},{12,16},{16,20},{20,24},{24,28},{1,5},{5,9},{9,... | collective-permute-start | bytes 196616 | tf_op jit(solution)/shard_map/ppermute | solution.py:22
  63.7 6.3 %collective-permute-start.17 = (f32[16,4,256]{2,1,0:T(4,128)S(1)}, f32[16,4,256]{2,1,0:T(4,128)S(1)}, u32[]{:S(2)}, u32[]{:S(2)}) collective-permute-start(f32[16,4,256]{2,1,0:T(4,128)S(1)} %get-tuple-element.40), channel_id=1, source_target_pairs={{4,0},{8,4},{12,8},{16,12},{20,16},{24,20},{28,24},{5,1},{9,5},{13... | collective-permute-start | bytes 196616 | tf_op jit(solution)/shard_map/ppermute | solution.py:23
  65.2 11.0 %collective-permute-start.14 = (f32[16,24,4]{2,1,0:T(8,128)S(1)}, f32[16,24,4]{2,1,0:T(8,128)S(1)}, u32[]{:S(2)}, u32[]{:S(2)}) collective-permute-start(f32[16,24,4]{2,1,0:T(8,128)S(1)} %get-tuple-element.27), channel_id=1, source_target_pairs={{0,1},{1,2},{2,3},{4,5},{5,6},{6,7},{8,9},{9,10},{10,11},{12,13},{... | collective-permute-start | bytes 18440 | tf_op jit(solution)/shard_map/ppermute | solution.py:22
  68.7 8.6 %collective-permute-start.15 = (f32[16,24,4]{2,1,0:T(8,128)S(1)}, f32[16,24,4]{2,1,0:T(8,128)S(1)}, u32[]{:S(2)}, u32[]{:S(2)}) collective-permute-start(f32[16,24,4]{2,1,0:T(8,128)S(1)} %get-tuple-element.28), channel_id=1, source_target_pairs={{1,0},{2,1},{3,2},{5,4},{6,5},{7,6},{9,8},{10,9},{11,10},{13,12},{... | collective-permute-start | bytes 18440 | tf_op jit(solution)/shard_map/ppermute | solution.py:23
  70.2 9.0 %collective-permute-start.18 = (f32[16,24,4]{2,1,0:T(8,128)S(1)}, f32[16,24,4]{2,1,0:T(8,128)S(1)}, u32[]{:S(2)}, u32[]{:S(2)}) collective-permute-start(f32[16,24,4]{2,1,0:T(8,128)S(1)} %get-tuple-element.25), channel_id=1, source_target_pairs={{0,1},{1,2},{2,3},{4,5},{5,6},{6,7},{8,9},{9,10},{10,11},{12,13},{... | collective-permute-start | bytes 18440 | tf_op jit(solution)/shard_map/ppermute | solution.py:22
  74.8 9.1 %collective-permute-start.19 = (f32[16,24,4]{2,1,0:T(8,128)S(1)}, f32[16,24,4]{2,1,0:T(8,128)S(1)}, u32[]{:S(2)}, u32[]{:S(2)}) collective-permute-start(f32[16,24,4]{2,1,0:T(8,128)S(1)} %get-tuple-element.26), channel_id=1, source_target_pairs={{1,0},{2,1},{3,2},{5,4},{6,5},{7,6},{9,8},{10,9},{11,10},{13,12},{... | collective-permute-start | bytes 18440 | tf_op jit(solution)/shard_map/ppermute | solution.py:23
  90.4 14.8 %copy-start.4 = (s32[16,256]{1,0:T(8,128)S(1)}, s32[16,256]{1,0:T(8,128)}, u32[]{:S(2)}) copy-start(s32[16,256]{1,0:T(8,128)} %param.6) | copy-start | bytes 49156
  91.3 22.4 %copy-start.2 = (f32[16,16,256]{2,1,0:T(8,128)}, f32[16,16,256]{2,1,0:T(8,128)S(1)}, u32[]{:S(2)}) copy-start(f32[16,16,256]{2,1,0:T(8,128)S(1)} %fusion.149) | copy-start | bytes 786436
  91.4 3.6 %collective-permute-start.20 = (f32[16,1,256]{2,1,0:T(1,128)S(1)}, f32[16,1,256]{2,1,0:T(1,128)S(1)}, u32[]{:S(2)}, u32[]{:S(2)}) collective-permute-start(f32[16,1,256]{2,1,0:T(1,128)S(1)} %get-tuple-element.37), channel_id=1, source_target_pairs={{0,4},{4,8},{8,12},{12,16},{16,20},{20,24},{24,28},{1,5},{5,9},{9,... | collective-permute-start | bytes 49160 | tf_op jit(solution)/shard_map/ppermute | solution.py:22
  93.7 6.6 %collective-permute-start.21 = (f32[16,1,256]{2,1,0:T(1,128)S(1)}, f32[16,1,256]{2,1,0:T(1,128)S(1)}, u32[]{:S(2)}, u32[]{:S(2)}) collective-permute-start(f32[16,1,256]{2,1,0:T(1,128)S(1)} %get-tuple-element.38), channel_id=1, source_target_pairs={{4,0},{8,4},{12,8},{16,12},{20,16},{24,20},{28,24},{5,1},{9,5},{13... | collective-permute-start | bytes 49160 | tf_op jit(solution)/shard_map/ppermute | solution.py:23
  100.5 7.3 %collective-permute-start.22 = (f32[16,18,1]{2,1,0:T(8,128)S(1)}, f32[16,18,1]{2,1,0:T(8,128)S(1)}, u32[]{:S(2)}, u32[]{:S(2)}) collective-permute-start(f32[16,18,1]{2,1,0:T(8,128)S(1)} %get-tuple-element.24), channel_id=1, source_target_pairs={{0,1},{1,2},{2,3},{4,5},{5,6},{6,7},{8,9},{9,10},{10,11},{12,13},{... | collective-permute-start | bytes 3464 | tf_op jit(solution)/shard_map/ppermute | solution.py:22
  104.0 8.4 %collective-permute-start.23 = (f32[16,18,1]{2,1,0:T(8,128)S(1)}, f32[16,18,1]{2,1,0:T(8,128)S(1)}, u32[]{:S(2)}, u32[]{:S(2)}) collective-permute-start(f32[16,18,1]{2,1,0:T(8,128)S(1)} %get-tuple-element.23), channel_id=1, source_target_pairs={{1,0},{2,1},{3,2},{5,4},{6,5},{7,6},{9,8},{10,9},{11,10},{13,12},{... | collective-permute-start | bytes 3464 | tf_op jit(solution)/shard_map/ppermute | solution.py:23
  113.7 21.9 %copy-start.3 = (f32[16,16,256]{2,1,0:T(8,128)}, f32[16,16,256]{2,1,0:T(8,128)S(1)}, u32[]{:S(2)}) copy-start(f32[16,16,256]{2,1,0:T(8,128)S(1)} %fusion.134) | copy-start | bytes 786436
  114.2 2.3 %collective-permute-start.24 = (f32[16,16,256]{2,1,0:T(8,128)S(1)}, f32[16,16,256]{2,1,0:T(8,128)S(1)}, u32[]{:S(2)}, u32[]{:S(2)}) collective-permute-start(f32[16,16,256]{2,1,0:T(8,128)S(1)} %convolution_bitcast_fusion), channel_id=1, source_target_pairs={{0,4},{4,0},{8,12},{12,8},{16,20},{20,16},{24,28},{28,24},{1,5},{5... | collective-permute-start | bytes 786440 | tf_op jit(solution)/shard_map/ppermute | solution.py:29
  116.5 9.7 %collective-permute-start.25 = (f32[16,16,256]{2,1,0:T(8,128)S(1)}, f32[16,16,256]{2,1,0:T(8,128)S(1)}, u32[]{:S(2)}, u32[]{:S(2)}) collective-permute-start(f32[16,16,256]{2,1,0:T(8,128)S(1)} %select_multiply_fusion.2), channel_id=1, source_target_pairs={{0,8},{4,12},{8,0},{12,4},{16,24},{20,28},{24,16},{28,20},{1,9},{5... | collective-permute-start | bytes 786440 | tf_op jit(solution)/shard_map/ppermute | solution.py:29
  126.2 8.1 %collective-permute-start.26 = (f32[16,16,256]{2,1,0:T(8,128)S(1)}, f32[16,16,256]{2,1,0:T(8,128)S(1)}, u32[]{:S(2)}, u32[]{:S(2)}) collective-permute-start(f32[16,16,256]{2,1,0:T(8,128)S(1)} %select_multiply_fusion.1), channel_id=1, source_target_pairs={{0,16},{4,20},{8,24},{12,28},{16,0},{20,4},{24,8},{28,12},{1,17},{... | collective-permute-start | bytes 786440 | tf_op jit(solution)/shard_map/ppermute | solution.py:29
  (1 other events, 6.5 us)
where the time goes:
time: 156 us; the launch traced here: 155 us
  starting transfers between devices  67.6 us (43%)
  waiting for transfers between devices  41.5 us (27%)
  other arithmetic  20.5 us (13%)
  blocking collectives  18.2 us (12%)
  local copies, waits for them, and re-layouts  5.7 us (4%)
    ppermute x12, starting transfers between devices, extended(): before = lax.ppermute(last, axis, up)  46.1 us
    ppermute x12, waiting for transfers between devices, extended(): after = lax.ppermute(leading, axis, down)  21.7 us
    psum x1, blocking collectives, per_device(): sketch = lax.psum(picked, 'gy')  18.2 us
    ppermute x12, starting transfers between devices, extended(): after = lax.ppermute(leading, axis, down)  15.8 us
    ppermute x3, waiting for transfers between devices, partner_2(): lax.ppermute(array, axis, [(i, i ^ 1 << stride) for i in range(lax.axis_s...  14.2 us
    add x6, other arithmetic, per_device(): rho_next * rho_now * shrink(direction_pad, margin_now + 1, margin_now)  12.2 us
    ppermute x3, starting transfers between devices, partner_2(): lax.ppermute(array, axis, [(i, i ^ 1 << stride) for i in range(lax.axis_s...  5.74 us
    ppermute x12, waiting for transfers between devices, extended(): before = lax.ppermute(last, axis, up)  5.56 us
  transfers between devices with their start and end apart: 27, of which 12 were waited for; matrix products, arithmetic and copies ran while one was open for 4% of the time, Pallas kernels for 0%

commit v1 on v0

v1 whole, which is shorter than its diff:
```python
import jax
import jax.numpy as jnp
import numpy as np
from jax import lax
from jax.experimental import pallas as pl
from jax.experimental.pallas import tpu as pltpu
from jax.sharding import PartitionSpec as P

SWEEPS = 8
reaction = 0.5
lowest = 0.5
highest = 62.0
HALO = SWEEPS
LANES = 128
AXES = ("gx", "gy")


def even_pair(i, n):
    return i ^ 1


def odd_pair(i, n):
    j = ((i + 1) ^ 1) - 1
    return j if 0 <= j < n else None


def same(i, n):
    return i


def exchange(array, row_map, col_map):
    rows, cols = lax.axis_size("gx"), lax.axis_size("gy")
    pairs = []
    for g in range(rows):
        for y in range(cols):
            to_g, to_y = row_map(g, rows), col_map(y, cols)
            if to_g is not None and to_y is not None:
                pairs.append((g * cols + y, to_g * cols + to_y))
    return lax.ppermute(array, AXES, pairs)


def swap(array, axis, mask):
    return lax.ppermute(array, axis, [(i, i ^ mask) for i in range(lax.axis_size(axis))])


def bit_groups(bits):
    return [bits[i : i + 2] for i in range(0, len(bits), 2)]


def masks_of(group):
    masks = [0]
    for bit in group:
        masks = masks + [m | 1 << bit for m in masks]
    return masks


def walsh_sign(index, mask, group):
    parity = jnp.int32(0)
    for bit in group:
        parity = parity + (index >> bit & (index ^ mask) >> bit & 1)
    return (1 - 2 * (parity & 1)).astype(jnp.float32)


def hartley_mix(depth, rows, scale):
    angles = (np.outer(np.arange(rows), np.arange(rows)) % rows) * (2.0 * np.pi / rows)
    table = (np.cos(angles) + np.sin(angles)) / np.sqrt(rows) * scale
    mixed = np.einsum("jk,de->kdej", table, np.eye(depth))
    return mixed.reshape(rows * depth, depth * rows).astype(np.float32)


def split_lanes(source, tiles):
    for t in range(tiles.shape[0]):
        tiles[t] = source[:, t * LANES : (t + 1) * LANES]


def take_row(tiles, row, depth, rows):
    picked = [tiles[t, pl.ds(row, depth, stride=rows), :] for t in range(tiles.shape[0])]
    return jnp.concatenate(picked, axis=1)


def put_row(tiles, row, slab, depth, rows):
    for t in range(tiles.shape[0]):
        tiles[t, pl.ds(row, depth, stride=rows), :] = slab[:, t * LANES : (t + 1) * LANES]


def join_lanes(tiles, target):
    for t in range(tiles.shape[0]):
        target[:, t * LANES : (t + 1) * LANES] = tiles[t]


def pack_kernel(flags, basis, cond, top_rows, bottom_rows, left, right, tiles, *, depth, rows, cols):
    odd = flags[0] == 1
    lane = lax.broadcasted_iota(jnp.int32, (depth, LANES), 1)
    for a, source in enumerate((basis, cond)):
        lo = jnp.zeros((depth, LANES), jnp.float32)
        hi = jnp.zeros((depth, LANES), jnp.float32)
        slabs = []
        split_lanes(source, tiles.at[a])
        for r in range(rows):
            slab = take_row(tiles.at[a], r, depth, rows)
            slabs.append(slab)
            mine = (lane >= r * HALO) & (lane < (r + 1) * HALO)
            first = slab[:, :LANES]
            last = slab[:, cols - LANES :]
            lo = jnp.where(mine, pltpu.roll(first, r * HALO, 1) if r else first, lo)
            hi = jnp.where(mine, pltpu.roll(last, (r + 1) * HALO % LANES, 1) if (r + 1) * HALO % LANES else last, hi)
        for r in range(HALO):
            up, down = slabs[r], slabs[rows - HALO + r]
            top_rows[a, r] = jnp.where(odd, down, up)
            bottom_rows[a, r] = jnp.where(odd, up, down)
        col_odd = flags[1] == 1
        left[a] = jnp.where(col_odd, hi, lo)
        right[a] = jnp.where(col_odd, lo, hi)


def main_kernel(flags, basis, cond, rows_odd, rows_even, strip_odd, strip_even, corner_odd, corner_even,
                signs, picks, mix, precond_out, image_out, sketch_out,
                res, dirn, pre, kx, ky, kz, diag, flip, tiles, *, depth, rows, cols, samples):
    width = cols + LANES
    span = rows + 2 * HALO
    odd = flags[0] == 1
    col_odd = flags[1] == 1
    top, bottom, left, right = (flags[i].astype(jnp.float32) for i in range(2, 6))
    middle = (highest + lowest) / 2.0
    spread = (highest - lowest) / 2.0
    lane = lax.broadcasted_iota(jnp.int32, (depth, LANES), 1)
    tail = (lane < HALO, lane >= LANES - HALO)

    def side_lanes(strips, at):
        lo, hi = strips
        shift_hi = (LANES - at * HALO) % LANES
        shift_lo = (2 * LANES - HALO - at * HALO) % LANES
        hi = pltpu.roll(hi, shift_hi, 1) if shift_hi else hi
        lo = pltpu.roll(lo, shift_lo, 1) if shift_lo else lo
        return jnp.where(tail[0], hi, jnp.where(tail[1], lo, 0.0))

    def ordered(strip_o, strip_e):
        return jnp.where(col_odd, strip_e, strip_o), jnp.where(col_odd, strip_o, strip_e)

    for a, (source, target) in enumerate(((basis, res), (cond, pre))):
        split_lanes(source, tiles.at[a])
        own = ordered(strip_odd[a], strip_even[a])
        far_odd = ordered(corner_odd[0, a], corner_odd[1, a])
        far_even = ordered(corner_even[0, a], corner_even[1, a])
        above = tuple(jnp.where(odd, e, o) for o, e in zip(far_odd, far_even))
        below = tuple(jnp.where(odd, o, e) for o, e in zip(far_odd, far_even))
        for j in range(span):
            if j < HALO:
                slab = jnp.where(odd, rows_even[a, j], rows_odd[a, j])
                side = side_lanes(above, rows - HALO + j)
            elif j < HALO + rows:
                slab = take_row(tiles.at[a], j - HALO, depth, rows)
                side = side_lanes(own, j - HALO)
            else:
                slab = jnp.where(odd, rows_odd[a, j - HALO - rows], rows_even[a, j - HALO - rows])
                side = side_lanes(below, j - HALO - rows)
            target[j, :, :cols] = slab
            target[j, :, cols:] = side

    def back(x, axis):
        return pltpu.roll(x, 1, axis)

    def ahead(x, axis):
        return pltpu.roll(x, x.shape[axis] - 1, axis)

    deep = lax.broadcasted_iota(jnp.int32, (depth, width), 0)
    wide = lax.broadcasted_iota(jnp.int32, (depth, width), 1)
    z_ends = (deep == 0).astype(jnp.float32) + (deep == depth - 1).astype(jnp.float32)
    z_inner = (deep < depth - 1).astype(jnp.float32)
    ends = z_ends + left * (wide == 0).astype(jnp.float32) + right * (wide == cols - 1).astype(jnp.float32)
    x_inner = 1.0 - right * (wide == cols - 1).astype(jnp.float32) - left * (wide == width - 1).astype(jnp.float32)

    def faces(j, here):
        half = 0.5 * here
        kx[j] = (half + ahead(half, 1)) * x_inner
        kz[j] = (half + ahead(half, 0)) * z_inner
        at_edge = jnp.where(j == HALO, top, 0.0) + jnp.where(j == HALO + rows - 1, bottom, 0.0)
        diag[j] = reaction + half * (ends + at_edge)
        dirn[j] = res[j] * (1.0 / middle)
        nxt = pre[j + 1]
        open_face = 1.0 - jnp.where(j == HALO - 1, top, 0.0) - jnp.where(j == HALO + rows - 1, bottom, 0.0)
        ky[j] = (half + 0.5 * nxt) * open_face
        return nxt

    kappa = lax.fori_loop(0, span - 1, faces, pre[0])
    dirn[span - 1] = res[span - 1] * (1.0 / middle)

    def sweep(low, high, field, emit):
        start = field[low]
        before = field[low - 1]

        def body(j, carry):
            here, flux_y = carry
            nxt = field[j + 1]
            flux = ky[j] * (here - nxt)
            flux_x = kx[j] * (here - ahead(here, 1))
            flux_z = kz[j] * (here - ahead(here, 0))
            applied = diag[j] * here + (flux - flux_y) + (flux_x - back(flux_x, 1)) + (flux_z - back(flux_z, 0))
            emit(j, here, applied)
            return nxt, flux

        lax.fori_loop(low, high, body, (start, ky[low - 1] * (before - start)), unroll=2)

    sig_ratio = middle / spread
    rho_now = 1.0 / sig_ratio

    def begin(j, _):
        pre[j] = dirn[j]
        return 0

    lax.fori_loop(0, span, begin, 0)
    for step in range(1, SWEEPS):
        rho_next = 1.0 / (2.0 * sig_ratio - rho_now)
        keep, gain = rho_next * rho_now, 2.0 * rho_next / spread
        rho_now = rho_next

        def emit(j, here, applied):
            left_over = res[j] - applied
            res[j] = left_over
            fresh = keep * here + gain * left_over
            dirn[j] = fresh
            pre[j] = pre[j] + fresh

        sweep(step, span - step, dirn, emit)

    def finish(j, here, applied):
        row = j - HALO
        image = applied[:, :cols]
        put_row(tiles.at[0], row, here[:, :cols], depth, rows)
        put_row(tiles.at[1], row, image, depth, rows)
        flip[pl.ds(pl.multiple_of(row * depth, depth), depth), :] = image * signs[pl.ds(row, 1), :].astype(jnp.float32)

    sweep(HALO, HALO + rows, pre, finish)
    join_lanes(tiles.at[0], precond_out)
    join_lanes(tiles.at[1], image_out)
    col_ids = lax.broadcasted_iota(jnp.int32, (samples, cols), 1)
    chosen = (picks[...] == col_ids).astype(jnp.float32)
    picked = lax.dot_general(chosen, flip[...], (((1,), (1,)), ((), ())),
                             precision=lax.Precision.HIGHEST, preferred_element_type=jnp.float32)
    sketch_out[...] = lax.dot_general(picked, mix[...], (((1,), (0,)), ((), ())),
                                      precision=lax.Precision.HIGHEST, preferred_element_type=jnp.float32)


def per_device(basis_vec, conductivity, sign_vals, sample_cols):
    depth, rows, cols = basis_vec.shape
    samples = sample_cols.shape[0]
    gx_size, gy_size = lax.axis_size("gx"), lax.axis_size("gy")
    gx_index, gy_index = lax.axis_index("gx"), lax.axis_index("gy")
    flags = jnp.stack([
        gx_index & 1, gy_index & 1, gx_index == 0, gx_index == gx_size - 1, gy_index == 0, gy_index == gy_size - 1,
    ]).astype(jnp.int32)
    basis = basis_vec.reshape(depth * rows, cols)
    cond = conductivity.reshape(depth * rows, cols)
    smem = pl.BlockSpec(memory_space=pltpu.SMEM)
    vmem = pl.BlockSpec(memory_space=pltpu.VMEM)
    sizes = dict(depth=depth, rows=rows, cols=cols)
    f32 = jnp.float32
    row_msg = jax.ShapeDtypeStruct((2, HALO, depth, cols), f32)
    strip_msg = jax.ShapeDtypeStruct((2, depth, LANES), f32)
    to_odd, to_even, strip_to_odd, strip_to_even = pl.pallas_call(
        lambda *refs: pack_kernel(*refs, **sizes),
        in_specs=[smem, vmem, vmem],
        out_specs=[vmem] * 4,
        out_shape=[row_msg, row_msg, strip_msg, strip_msg],
        scratch_shapes=[pltpu.VMEM((2, cols // LANES, depth * rows, LANES), f32)],
        name="pack",
    )(flags, basis, cond)
    with jax.named_scope("rows_odd"):
        rows_odd = exchange(to_odd, odd_pair, same)
    with jax.named_scope("strip_odd"):
        strip_odd = exchange(strip_to_odd, same, odd_pair)
    with jax.named_scope("strip_even"):
        strip_even = exchange(strip_to_even, same, even_pair)
    with jax.named_scope("rows_even"):
        rows_even = exchange(to_even, even_pair, same)
    strips = jnp.stack([strip_odd, strip_even])
    with jax.named_scope("corner_odd"):
        corner_odd = exchange(strips, odd_pair, same)
    with jax.named_scope("corner_even"):
        corner_even = exchange(strips, even_pair, same)
    mix = jnp.asarray(hartley_mix(depth, rows, 1.0 / np.sqrt(gx_size)))
    span, width = rows + 2 * HALO, cols + LANES
    precond, image, current = pl.pallas_call(
        lambda *refs: main_kernel(*refs, samples=samples, **sizes),
        in_specs=[smem] + [vmem] * 11,
        out_specs=[vmem] * 3,
        out_shape=[jax.ShapeDtypeStruct((depth * rows, cols), f32)] * 2
        + [jax.ShapeDtypeStruct((samples, depth * rows), f32)],
        scratch_shapes=[pltpu.VMEM((span, depth, width), f32)] * 7 + [
            pltpu.VMEM((depth * rows, cols), f32),
            pltpu.VMEM((2, cols // LANES, depth * rows, LANES), f32),
        ],
        name="solve",
    )(flags, basis, cond, rows_odd, rows_even, strip_odd, strip_even, corner_odd, corner_even,
      sign_vals, sample_cols.reshape(samples, 1), mix)
    gx_bits = gx_size.bit_length() - 1
    for group in [[0]] + bit_groups(list(range(1, gx_bits))):
        total = walsh_sign(gx_index, 0, group) * current
        for mask in masks_of(group)[1:]:
            total = total + walsh_sign(gx_index, mask, group) * swap(current, "gx", mask)
        current = total
    for group in bit_groups(list(range(gy_size.bit_length() - 1))):
        current = current + sum(swap(current, "gy", mask) for mask in masks_of(group)[1:])
    shape = (depth, rows, cols)
    sketch = current.T.reshape(depth, rows, samples)
    return precond.reshape(shape), image.reshape(shape), sketch


def solution(mesh):
    in_specs = (P(None, "gx", "gy"), P(None, "gx", "gy"), P("gx", "gy"), P("gy"))
    out_specs = (P(None, "gx", "gy"), P(None, "gx", "gy"), P(None, "gx", None))
    return jax.shard_map(
        per_device, mesh=mesh, in_specs=in_specs, out_specs=out_specs, check_vma=False
    )
```

time: 156 us -> 61 us (0.39)
  starting transfers between devices: 67.6 us -> 23.5 us
  waiting for transfers between devices: 41.5 us -> 9.51 us
  Pallas kernels: 0 us -> 23 us
  other arithmetic: 20.5 us -> 0.02 us
  blocking collectives: 18.2 us -> 0 us
  local copies, waits for them, and re-layouts: 5.7 us -> 4 us
    ppermute x27 -> x13, starting transfers between devices: 67.6 us -> 23.5 us  [the longest x6 13.9 us: exchange(): return lax.ppermute(array, AXES, pairs)]
    ppermute x27 -> x13, waiting for transfers between devices: 41.5 us -> 9.51 us  [the longest x7 7.4 us: swap(): lax.ppermute(array, axis, [(i, i ^ mask) for i in range(lax.axis_size(axi...]
    pallas_call x0 -> x2, Pallas kernels: none -> 23 us  [the longest x1 21 us: per_device(): pl.pallas_call(lambda *refs: main_kernel(*refs, samples=samples, **sizes)...]
    psum x1 -> x0, blocking collectives: 18.2 us -> none  [per_device(): sketch = lax.psum(picked, 'gy')]
    add x9 -> x2, other arithmetic: 15.7 us -> 0.01 us  [per_device(): total + walsh_sign(gx_index, mask, group) * swap(current, 'gx', mask)]
    concatenate x11 -> x0, other arithmetic: 3.22 us -> none  [extended(): array = jnp.concatenate([before, array, after], axis=dim)]
    slice x14 -> x0, local copies, waits for them, and re-layouts: 3.04 us -> none  [the longest x11 2.63 us: extended(): last = lax.slice_in_dim(array, length - width, length, axis=dim)]
    unnamed x13 -> x17, local copies, waits for them, and re-layouts: 0.81 us -> 2.75 us
  transfers between devices with their start and end apart: 27 -> 13, of which waited for: 12 -> 7; matrix products, arithmetic and copies ran while one was open for 4% -> 1% of each run, Pallas kernels for 0% -> 0%
where the time goes in v1:
time: 61 us; the launch traced here: 60.8 us
  starting transfers between devices  23.5 us (39%)
  Pallas kernels  23 us (38%)
  waiting for transfers between devices  9.51 us (16%)
  local copies, waits for them, and re-layouts  4 us (7%)
  between operations  0.7 us (1%)
    pallas_call x1, Pallas kernels, per_device(): pl.pallas_call(lambda *refs: main_kernel(*refs, samples=samples, **sizes)...  21 us
    ppermute x6, starting transfers between devices, exchange(): return lax.ppermute(array, AXES, pairs)  13.9 us
    ppermute x7, starting transfers between devices, swap(): lax.ppermute(array, axis, [(i, i ^ mask) for i in range(lax.axis_size(axi...  9.62 us
    ppermute x7, waiting for transfers between devices, swap(): lax.ppermute(array, axis, [(i, i ^ mask) for i in range(lax.axis_size(axi...  7.4 us
    unnamed x17, local copies, waits for them, and re-layouts  2.75 us
    ppermute x6, waiting for transfers between devices, exchange(): return lax.ppermute(array, AXES, pairs)  2.11 us
    pallas_call x1, Pallas kernels, per_device(): pl.pallas_call(lambda *refs: pack_kernel(*refs, **sizes), in_specs=[smem,...  2.04 us
  transfers between devices with their start and end apart: 13, of which 7 were waited for; matrix products, arithmetic and copies ran while one was open for 1% of the time, Pallas kernels for 0%

profile of v1, /device:TPU:0, one launch (start us, length us, event | category | flops | bytes accessed | tf_op | source)
XLA Modules:
  0.0 60.8 jit_solution(1580472102875803151)
XLA Ops:
  0.6 0.6 stack.52.refs_0_
  1.2 2.0 %pack.1 = (f32[2,8,16,256]{3,2,1,0:T(8,128)}, f32[2,8,16,256]{3,2,1,0:T(8,128)}, f32[2,16,128]{2,1,0:T(8,128)}, f32[2,16,128]{2,1,0:T(8,128)}) custom-call(s32[6]{0:T(128)} %stack.52.refs_0_, f32[256,256]{1,0:T(8,128)} %bitcast.16, f32[256,256]{1,0:T(8,128)} %bitcast.18), custom_call_target="tpu_custom_call" | custom-call | tf_op jit(solution)/shard_map/pack/pallas_call | solution.py:260
  3.3 0.7 %collective-permute-start = (f32[2,8,16,256]{3,2,1,0:T(8,128)}, f32[2,8,16,256]{3,2,1,0:T(8,128)S(1)}, u32[]{:S(2)}, u32[]{:S(2)}) collective-permute-start(f32[2,8,16,256]{3,2,1,0:T(8,128)} %get-tuple-element.10), channel_id=1, source_target_pairs={{4,8},{5,9},{6,10},{7,11},{8,4},{9,5},{10,6},{11,7},{12,16},{13,17... | collective-permute-start | bytes 786440 | tf_op jit(solution)/shard_map/rows_odd/ppermute | solution.py:39
  3.9 4.4 %collective-permute-start.1 = (f32[2,8,16,256]{3,2,1,0:T(8,128)}, f32[2,8,16,256]{3,2,1,0:T(8,128)S(1)}, u32[]{:S(2)}, u32[]{:S(2)}) collective-permute-start(f32[2,8,16,256]{3,2,1,0:T(8,128)} %get-tuple-element.11), channel_id=1, source_target_pairs={{0,4},{1,5},{2,6},{3,7},{4,0},{5,1},{6,2},{7,3},{8,12},{9,13},{10,... | collective-permute-start | bytes 786440 | tf_op jit(solution)/shard_map/rows_even/ppermute | solution.py:39
  8.3 0.7 %collective-permute-start.2 = (f32[2,16,128]{2,1,0:T(8,128)}, f32[2,16,128]{2,1,0:T(8,128)S(1)}, u32[]{:S(2)}, u32[]{:S(2)}) collective-permute-start(f32[2,16,128]{2,1,0:T(8,128)} %get-tuple-element.12), channel_id=1, source_target_pairs={{1,2},{2,1},{5,6},{6,5},{9,10},{10,9},{13,14},{14,13},{17,18},{18,... | collective-permute-start | bytes 49160 | tf_op jit(solution)/shard_map/strip_odd/ppermute | solution.py:39
  9.0 4.5 %collective-permute-start.3 = (f32[2,16,128]{2,1,0:T(8,128)}, f32[2,16,128]{2,1,0:T(8,128)S(1)}, u32[]{:S(2)}, u32[]{:S(2)}) collective-permute-start(f32[2,16,128]{2,1,0:T(8,128)} %get-tuple-element.13), channel_id=1, source_target_pairs={{0,1},{1,0},{2,3},{3,2},{4,5},{5,4},{6,7},{7,6},{8,9},{9,8},{10,11... | collective-permute-start | bytes 49160 | tf_op jit(solution)/shard_map/strip_even/ppermute | solution.py:39
  13.4 1.9 %collective-permute-done.3.refs_6_ = f32[2,16,128]{2,1,0:T(8,128)S(1)} collective-permute-done((f32[2,16,128]{2,1,0:T(8,128)}, f32[2,16,128]{2,1,0:T(8,128)S(1)}, u32[]{:S(2)}, u32[]{:S(2)}) %collective-permute-start.3) | collective-permute-done | bytes 16416 | tf_op jit(solution)/shard_map/strip_even/ppermute | solution.py:39
  15.4 0.6 copy-done.3
  16.0 0.8 %collective-permute-start.4 = (f32[2,2,16,128]{3,2,1,0:T(8,128)S(1)}, f32[2,2,16,128]{3,2,1,0:T(8,128)S(1)}, u32[]{:S(2)}, u32[]{:S(2)}) collective-permute-start(f32[2,2,16,128]{3,2,1,0:T(8,128)S(1)} %pad_maximum_fusion), channel_id=1, source_target_pairs={{4,8},{5,9},{6,10},{7,11},{8,4},{9,5},{10,6},{11,7},{12,16},{13,17... | collective-permute-start | bytes 98312 | tf_op jit(solution)/shard_map/corner_odd/ppermute | solution.py:39
  16.8 2.9 %collective-permute-start.5 = (f32[2,2,16,128]{3,2,1,0:T(8,128)S(1)}, f32[2,2,16,128]{3,2,1,0:T(8,128)S(1)}, u32[]{:S(2)}, u32[]{:S(2)}) collective-permute-start(f32[2,2,16,128]{3,2,1,0:T(8,128)S(1)} %pad_maximum_fusion), channel_id=1, source_target_pairs={{0,4},{1,5},{2,6},{3,7},{4,0},{5,1},{6,2},{7,3},{8,12},{9,13},{10,... | collective-permute-start | bytes 98312 | tf_op jit(solution)/shard_map/corner_even/ppermute | solution.py:39
  19.7 0.7 %copy.8.refs_10_ = s32[16,1]{1,0:T(8,128)} copy(s32[16,1]{0,1:T(1,128)S(1)} %bitcast.23) | data formatting | bytes 128 | tf_op jit(solution)/shard_map/reshape | solution.py:295
  20.3 0.0 collective-permute-done.4.refs_7_
  20.4 0.2 collective-permute-done.5.refs_8_
  20.5 0.0 collective-permute-done.refs_3_
  20.5 0.4 copy-done.4
  21.0 0.2 copy-done.5
  21.1 0.1 copy-done
  21.2 0.7 %copy-done.1 = f32[2,8,16,256]{3,2,1,0:T(8,128)} copy-done((f32[2,8,16,256]{3,2,1,0:T(8,128)}, f32[2,8,16,256]{3,2,1,0:T(8,128)S(1)}, u32[]{:S(2)}) %copy-start.1) | copy-done | bytes 262168
  21.9 21.0 %solve.1 = (f32[256,256]{1,0:T(8,128)}, f32[256,256]{1,0:T(8,128)}, f32[16,256]{1,0:T(8,128)}) custom-call(s32[6]{0:T(128)} %stack.52.refs_0_, f32[256,256]{1,0:T(8,128)} %bitcast.17, f32[256,256]{1,0:T(8,128)} %bitcast.19, f32[2,8,16,256]{3,2,1,0:T(8,128)} %copy-done, f32[2,8,16,256]{3,2,1,0:T(8,128)} %copy-done.1, f32[2,16,128]{2,1,0:T(8,128)} %copy-done.2, ...), custom_call_target="tpu_custom_call" | custom-call | tf_op jit(solution)/shard_map/solve/pallas_call | solution.py:283
  42.9 0.7 %collective-permute-start.6 = (f32[16,256]{1,0:T(8,128)}, f32[16,256]{1,0:T(8,128)S(1)}, u32[]{:S(2)}, u32[]{:S(2)}) collective-permute-start(f32[16,256]{1,0:T(8,128)} %get-tuple-element.16), channel_id=1, source_target_pairs={{0,4},{4,0},{8,12},{12,8},{16,20},{20,16},{24,28},{28,24},{1,5},{5... | collective-permute-start | bytes 49160 | tf_op jit(solution)/shard_map/ppermute | solution.py:43
  43.6 1.0 %collective-permute-done.6 = f32[16,256]{1,0:T(8,128)S(1)} collective-permute-done((f32[16,256]{1,0:T(8,128)}, f32[16,256]{1,0:T(8,128)S(1)}, u32[]{:S(2)}, u32[]{:S(2)}) %collective-permute-start.6) | collective-permute-done | bytes 16416 | tf_op jit(solution)/shard_map/ppermute | solution.py:43
  44.7 2.0 %collective-permute-start.7 = (f32[16,256]{1,0:T(8,128)S(1)}, f32[16,256]{1,0:T(8,128)S(1)}, u32[]{:S(2)}, u32[]{:S(2)}) collective-permute-start(f32[16,256]{1,0:T(8,128)S(1)} %multiply_add_fusion.1), channel_id=1, source_target_pairs={{0,8},{4,12},{8,0},{12,4},{16,24},{20,28},{24,16},{28,20},{1,9},{5... | collective-permute-start | bytes 49160 | tf_op jit(solution)/shard_map/ppermute | solution.py:43
  46.7 1.0 %collective-permute-start.8 = (f32[16,256]{1,0:T(8,128)S(1)}, f32[16,256]{1,0:T(8,128)S(1)}, u32[]{:S(2)}, u32[]{:S(2)}) collective-permute-start(f32[16,256]{1,0:T(8,128)S(1)} %multiply_add_fusion.1), channel_id=1, source_target_pairs={{0,16},{4,20},{8,24},{12,28},{16,0},{20,4},{24,8},{28,12},{1,17},{... | collective-permute-start | bytes 49160 | tf_op jit(solution)/shard_map/ppermute | solution.py:43
  47.7 1.4 %collective-permute-start.9 = (f32[16,256]{1,0:T(8,128)S(1)}, f32[16,256]{1,0:T(8,128)S(1)}, u32[]{:S(2)}, u32[]{:S(2)}) collective-permute-start(f32[16,256]{1,0:T(8,128)S(1)} %multiply_add_fusion.1), channel_id=1, source_target_pairs={{0,24},{4,28},{8,16},{12,20},{16,8},{20,12},{24,0},{28,4},{1,25},{... | collective-permute-start | bytes 49160 | tf_op jit(solution)/shard_map/ppermute | solution.py:43
  49.1 0.0 collective-permute-done.7
  49.1 1.3 %collective-permute-done.8 = f32[16,256]{1,0:T(8,128)S(1)} collective-permute-done((f32[16,256]{1,0:T(8,128)S(1)}, f32[16,256]{1,0:T(8,128)S(1)}, u32[]{:S(2)}, u32[]{:S(2)}) %collective-permute-start.8) | collective-permute-done | bytes 16416 | tf_op jit(solution)/shard_map/ppermute | solution.py:43
  50.4 1.9 %collective-permute-done.9 = f32[16,256]{1,0:T(8,128)S(1)} collective-permute-done((f32[16,256]{1,0:T(8,128)S(1)}, f32[16,256]{1,0:T(8,128)S(1)}, u32[]{:S(2)}, u32[]{:S(2)}) %collective-permute-start.9) | collective-permute-done | bytes 16416 | tf_op jit(solution)/shard_map/ppermute | solution.py:43
  52.4 2.1 %collective-permute-start.10 = (f32[16,256]{1,0:T(8,128)S(1)}, f32[16,256]{1,0:T(8,128)S(1)}, u32[]{:S(2)}, u32[]{:S(2)}) collective-permute-start(f32[16,256]{1,0:T(8,128)S(1)} %multiply_add_fusion), channel_id=1, source_target_pairs={{0,1},{1,0},{2,3},{3,2},{4,5},{5,4},{6,7},{7,6},{8,9},{9,8},{10,11... | collective-permute-start | bytes 49160 | tf_op jit(solution)/shard_map/ppermute | solution.py:43
  54.5 2.4 %collective-permute-start.12 = (f32[16,256]{1,0:T(8,128)S(1)}, f32[16,256]{1,0:T(8,128)S(1)}, u32[]{:S(2)}, u32[]{:S(2)}) collective-permute-start(f32[16,256]{1,0:T(8,128)S(1)} %multiply_add_fusion), channel_id=1, source_target_pairs={{0,3},{1,2},{2,1},{3,0},{4,7},{5,6},{6,5},{7,4},{8,11},{9,10},{10,... | collective-permute-start | bytes 49160 | tf_op jit(solution)/shard_map/ppermute | solution.py:43
  56.9 2.2 %collective-permute-done.11 = f32[16,256]{1,0:T(8,128)S(1)} collective-permute-done((f32[16,256]{1,0:T(8,128)S(1)}, f32[16,256]{1,0:T(8,128)S(1)}, u32[]{:S(2)}, u32[]{:S(2)}) %collective-permute-start.11) | collective-permute-done | bytes 16416 | tf_op jit(solution)/shard_map/ppermute | solution.py:43
  59.1 0.9 %collective-permute-done.12 = f32[16,256]{1,0:T(8,128)S(1)} collective-permute-done((f32[16,256]{1,0:T(8,128)S(1)}, f32[16,256]{1,0:T(8,128)S(1)}, u32[]{:S(2)}, u32[]{:S(2)}) %collective-permute-start.12) | collective-permute-done | bytes 16416 | tf_op jit(solution)/shard_map/ppermute | solution.py:43
  60.0 0.8 %copy.10 = f32[256,16]{1,0:T(8,128)} copy(f32[256,16]{0,1:T(8,128)S(1)} %add_bitcast_fusion) | data formatting | bytes 32768
  (19 shorter events, 0.1 us)
Async XLA Ops:
  3.3 17.3 %collective-permute-start = (f32[2,8,16,256]{3,2,1,0:T(8,128)}, f32[2,8,16,256]{3,2,1,0:T(8,128)S(1)}, u32[]{:S(2)}, u32[]{:S(2)}) collective-permute-start(f32[2,8,16,256]{3,2,1,0:T(8,128)} %get-tuple-element.10), channel_id=1, source_target_pairs={{4,8},{5,9},{6,10},{7,11},{8,4},{9,5},{10,6},{11,7},{12,16},{13,17... | collective-permute-start | bytes 786440 | tf_op jit(solution)/shard_map/rows_odd/ppermute | solution.py:39
  3.9 16.6 %collective-permute-start.1 = (f32[2,8,16,256]{3,2,1,0:T(8,128)}, f32[2,8,16,256]{3,2,1,0:T(8,128)S(1)}, u32[]{:S(2)}, u32[]{:S(2)}) collective-permute-start(f32[2,8,16,256]{3,2,1,0:T(8,128)} %get-tuple-element.11), channel_id=1, source_target_pairs={{0,4},{1,5},{2,6},{3,7},{4,0},{5,1},{6,2},{7,3},{8,12},{9,13},{10,... | collective-permute-start | bytes 786440 | tf_op jit(solution)/shard_map/rows_even/ppermute | solution.py:39
  8.3 5.1 %collective-permute-start.2 = (f32[2,16,128]{2,1,0:T(8,128)}, f32[2,16,128]{2,1,0:T(8,128)S(1)}, u32[]{:S(2)}, u32[]{:S(2)}) collective-permute-start(f32[2,16,128]{2,1,0:T(8,128)} %get-tuple-element.12), channel_id=1, source_target_pairs={{1,2},{2,1},{5,6},{6,5},{9,10},{10,9},{13,14},{14,13},{17,18},{18,... | collective-permute-start | bytes 49160 | tf_op jit(solution)/shard_map/strip_odd/ppermute | solution.py:39
  9.0 6.4 %collective-permute-start.3 = (f32[2,16,128]{2,1,0:T(8,128)}, f32[2,16,128]{2,1,0:T(8,128)S(1)}, u32[]{:S(2)}, u32[]{:S(2)}) collective-permute-start(f32[2,16,128]{2,1,0:T(8,128)} %get-tuple-element.13), channel_id=1, source_target_pairs={{0,1},{1,0},{2,3},{3,2},{4,5},{5,4},{6,7},{7,6},{8,9},{9,8},{10,11... | collective-permute-start | bytes 49160 | tf_op jit(solution)/shard_map/strip_even/ppermute | solution.py:39
  13.4 1.9 %copy-start.2 = (f32[2,16,128]{2,1,0:T(8,128)}, f32[2,16,128]{2,1,0:T(8,128)S(1)}, u32[]{:S(2)}) copy-start(f32[2,16,128]{2,1,0:T(8,128)S(1)} %collective-permute-done.2.refs_5_) | copy-start | bytes 49156
  15.4 0.6 copy-start.3
  16.0 3.7 %copy-start.7 = (s32[16]{0:T(128)S(1)}, s32[16]{0:T(128)}, u32[]{:S(2)}) copy-start(s32[16]{0:T(128)} %param.8) | copy-start | bytes 196
  16.0 4.4 %collective-permute-start.4 = (f32[2,2,16,128]{3,2,1,0:T(8,128)S(1)}, f32[2,2,16,128]{3,2,1,0:T(8,128)S(1)}, u32[]{:S(2)}, u32[]{:S(2)}) collective-permute-start(f32[2,2,16,128]{3,2,1,0:T(8,128)S(1)} %pad_maximum_fusion), channel_id=1, source_target_pairs={{4,8},{5,9},{6,10},{7,11},{8,4},{9,5},{10,6},{11,7},{12,16},{13,17... | collective-permute-start | bytes 98312 | tf_op jit(solution)/shard_map/corner_odd/ppermute | solution.py:39
  16.8 3.8 %collective-permute-start.5 = (f32[2,2,16,128]{3,2,1,0:T(8,128)S(1)}, f32[2,2,16,128]{3,2,1,0:T(8,128)S(1)}, u32[]{:S(2)}, u32[]{:S(2)}) collective-permute-start(f32[2,2,16,128]{3,2,1,0:T(8,128)S(1)} %pad_maximum_fusion), channel_id=1, source_target_pairs={{0,4},{1,5},{2,6},{3,7},{4,0},{5,1},{6,2},{7,3},{8,12},{9,13},{10,... | collective-permute-start | bytes 98312 | tf_op jit(solution)/shard_map/corner_even/ppermute | solution.py:39
  20.4 0.6 %copy-start.4 = (f32[2,2,16,128]{3,2,1,0:T(8,128)}, f32[2,2,16,128]{3,2,1,0:T(8,128)S(1)}, u32[]{:S(2)}) copy-start(f32[2,2,16,128]{3,2,1,0:T(8,128)S(1)} %collective-permute-done.4.refs_7_) | copy-start | bytes 98308
  20.5 0.6 %copy-start.5 = (f32[2,2,16,128]{3,2,1,0:T(8,128)}, f32[2,2,16,128]{3,2,1,0:T(8,128)S(1)}, u32[]{:S(2)}) copy-start(f32[2,2,16,128]{3,2,1,0:T(8,128)S(1)} %collective-permute-done.5.refs_8_) | copy-start | bytes 98308
  20.5 0.7 %copy-start = (f32[2,8,16,256]{3,2,1,0:T(8,128)}, f32[2,8,16,256]{3,2,1,0:T(8,128)S(1)}, u32[]{:S(2)}) copy-start(f32[2,8,16,256]{3,2,1,0:T(8,128)S(1)} %collective-permute-done.refs_3_) | copy-start | bytes 786436
  21.2 0.7 %copy-start.1 = (f32[2,8,16,256]{3,2,1,0:T(8,128)}, f32[2,8,16,256]{3,2,1,0:T(8,128)S(1)}, u32[]{:S(2)}) copy-start(f32[2,8,16,256]{3,2,1,0:T(8,128)S(1)} %collective-permute-done.1.refs_4_) | copy-start | bytes 786436
  42.9 1.7 %copy-start.6 = (f32[16,256]{1,0:T(8,128)S(1)}, f32[16,256]{1,0:T(8,128)}, u32[]{:S(2)}) copy-start(f32[16,256]{1,0:T(8,128)} %get-tuple-element.16) | copy-start | bytes 49156
  42.9 1.7 %collective-permute-start.6 = (f32[16,256]{1,0:T(8,128)}, f32[16,256]{1,0:T(8,128)S(1)}, u32[]{:S(2)}, u32[]{:S(2)}) collective-permute-start(f32[16,256]{1,0:T(8,128)} %get-tuple-element.16), channel_id=1, source_target_pairs={{0,4},{4,0},{8,12},{12,8},{16,20},{20,16},{24,28},{28,24},{1,5},{5... | collective-permute-start | bytes 49160 | tf_op jit(solution)/shard_map/ppermute | solution.py:43
  44.7 4.4 %collective-permute-start.7 = (f32[16,256]{1,0:T(8,128)S(1)}, f32[16,256]{1,0:T(8,128)S(1)}, u32[]{:S(2)}, u32[]{:S(2)}) collective-permute-start(f32[16,256]{1,0:T(8,128)S(1)} %multiply_add_fusion.1), channel_id=1, source_target_pairs={{0,8},{4,12},{8,0},{12,4},{16,24},{20,28},{24,16},{28,20},{1,9},{5... | collective-permute-start | bytes 49160 | tf_op jit(solution)/shard_map/ppermute | solution.py:43
  46.7 3.7 %collective-permute-start.8 = (f32[16,256]{1,0:T(8,128)S(1)}, f32[16,256]{1,0:T(8,128)S(1)}, u32[]{:S(2)}, u32[]{:S(2)}) collective-permute-start(f32[16,256]{1,0:T(8,128)S(1)} %multiply_add_fusion.1), channel_id=1, source_target_pairs={{0,16},{4,20},{8,24},{12,28},{16,0},{20,4},{24,8},{28,12},{1,17},{... | collective-permute-start | bytes 49160 | tf_op jit(solution)/shard_map/ppermute | solution.py:43
  47.7 4.6 %collective-permute-start.9 = (f32[16,256]{1,0:T(8,128)S(1)}, f32[16,256]{1,0:T(8,128)S(1)}, u32[]{:S(2)}, u32[]{:S(2)}) collective-permute-start(f32[16,256]{1,0:T(8,128)S(1)} %multiply_add_fusion.1), channel_id=1, source_target_pairs={{0,24},{4,28},{8,16},{12,20},{16,8},{20,12},{24,0},{28,4},{1,25},{... | collective-permute-start | bytes 49160 | tf_op jit(solution)/shard_map/ppermute | solution.py:43
  52.4 4.5 %collective-permute-start.10 = (f32[16,256]{1,0:T(8,128)S(1)}, f32[16,256]{1,0:T(8,128)S(1)}, u32[]{:S(2)}, u32[]{:S(2)}) collective-permute-start(f32[16,256]{1,0:T(8,128)S(1)} %multiply_add_fusion), channel_id=1, source_target_pairs={{0,1},{1,0},{2,3},{3,2},{4,5},{5,4},{6,7},{7,6},{8,9},{9,8},{10,11... | collective-permute-start | bytes 49160 | tf_op jit(solution)/shard_map/ppermute | solution.py:43
  54.5 4.6 %collective-permute-start.11 = (f32[16,256]{1,0:T(8,128)S(1)}, f32[16,256]{1,0:T(8,128)S(1)}, u32[]{:S(2)}, u32[]{:S(2)}) collective-permute-start(f32[16,256]{1,0:T(8,128)S(1)} %multiply_add_fusion), channel_id=1, source_target_pairs={{0,2},{1,3},{2,0},{3,1},{4,6},{5,7},{6,4},{7,5},{8,10},{9,11},{10,... | collective-permute-start | bytes 49160 | tf_op jit(solution)/shard_map/ppermute | solution.py:43
  54.5 5.5 %collective-permute-start.12 = (f32[16,256]{1,0:T(8,128)S(1)}, f32[16,256]{1,0:T(8,128)S(1)}, u32[]{:S(2)}, u32[]{:S(2)}) collective-permute-start(f32[16,256]{1,0:T(8,128)S(1)} %multiply_add_fusion), channel_id=1, source_target_pairs={{0,3},{1,2},{2,1},{3,0},{4,7},{5,6},{6,5},{7,4},{8,11},{9,10},{10,... | collective-permute-start | bytes 49160 | tf_op jit(solution)/shard_map/ppermute | solution.py:43

commit v2 on v1

v2 whole, which is shorter than its diff:
```python
import jax
import jax.numpy as jnp
import numpy as np
from jax import lax
from jax.experimental import pallas as pl
from jax.experimental.pallas import tpu as pltpu
from jax.sharding import PartitionSpec as P

SWEEPS = 8
reaction = 0.5
lowest = 0.5
highest = 62.0
HALO = SWEEPS
LANES = 128
AXES = ("gx", "gy")


def even_pair(i, n):
    return i ^ 1


def odd_pair(i, n):
    j = ((i + 1) ^ 1) - 1
    return j if 0 <= j < n else None


def same(i, n):
    return i


def exchange(array, row_map, col_map):
    rows, cols = lax.axis_size("gx"), lax.axis_size("gy")
    pairs = []
    for g in range(rows):
        for y in range(cols):
            to_g, to_y = row_map(g, rows), col_map(y, cols)
            if to_g is not None and to_y is not None:
                pairs.append((g * cols + y, to_g * cols + to_y))
    return lax.ppermute(array, AXES, pairs)


def swap(array, axis, mask):
    return lax.ppermute(array, axis, [(i, i ^ mask) for i in range(lax.axis_size(axis))])


def bit_groups(bits):
    return [bits[i : i + 2] for i in range(0, len(bits), 2)]


def masks_of(group):
    masks = [0]
    for bit in group:
        masks = masks + [m | 1 << bit for m in masks]
    return masks


def walsh_sign(index, mask, group):
    parity = jnp.int32(0)
    for bit in group:
        parity = parity + (index >> bit & (index ^ mask) >> bit & 1)
    return (1 - 2 * (parity & 1)).astype(jnp.float32)


def hartley_mix(depth, rows, scale):
    angles = (np.outer(np.arange(rows), np.arange(rows)) % rows) * (2.0 * np.pi / rows)
    table = (np.cos(angles) + np.sin(angles)) / np.sqrt(rows) * scale
    return np.kron(np.eye(depth), table.T).astype(np.float32)


def turn(tiles):
    count = len(tiles)
    sub = lax.broadcasted_iota(jnp.int32, tiles[0].shape, 0)
    tiles = list(tiles)
    step = 1
    while step < count:
        low = (sub & step) == 0
        for i in range(count):
            if not i & step:
                a, b = tiles[i], tiles[i + step]
                tiles[i] = jnp.where(low, a, pltpu.roll(b, step, 0))
                tiles[i + step] = jnp.where(low, pltpu.roll(a, count - step, 0), b)
        step *= 2
    return tiles


def pack_kernel(flags, basis, cond, to_odd, to_even, left, right, *, depth, rows, cols):
    odd, col_odd = flags[0] == 1, flags[1] == 1
    half = depth // 2
    lane = lax.broadcasted_iota(jnp.int32, (half, LANES), 1)
    for a, source in enumerate((basis, cond)):
        for t in range(2):
            part = slice(t * half, (t + 1) * half)
            lo = hi = jnp.zeros((half, LANES), jnp.float32)
            for c in range(cols // LANES):
                span = slice(c * LANES, (c + 1) * LANES)
                slabs = []
                for r in range(0, rows, half):
                    slabs += turn([source[2 * s + t, r : r + half, span] for s in range(half)])
                for r in range(HALO):
                    first, last = slabs[r], slabs[rows - HALO + r]
                    to_odd[a, r, part, span] = jnp.where(odd, last, first)
                    to_even[a, r, part, span] = jnp.where(odd, first, last)
                for r in range(rows):
                    mine = (lane >= r * HALO) & (lane < (r + 1) * HALO)
                    if c == 0:
                        shift = r * HALO % LANES
                        lo = jnp.where(mine, pltpu.roll(slabs[r], shift, 1) if shift else slabs[r], lo)
                    if c == cols // LANES - 1:
                        shift = (r + 1) * HALO % LANES
                        hi = jnp.where(mine, pltpu.roll(slabs[r], shift, 1) if shift else slabs[r], hi)
            left[a, part] = jnp.where(col_odd, hi, lo)
            right[a, part] = jnp.where(col_odd, lo, hi)


def back(x, axis):
    return pltpu.roll(x, 1, axis)


def ahead(x, axis):
    return pltpu.roll(x, x.shape[axis] - 1, axis)


def main_kernel(flags, own_odd, own_even, rows_odd, rows_even, strip_odd, strip_even, corner_odd, corner_even,
                signs, picks, mix, precond_out, image_out, sketch_out,
                res, dirn, pre, kx, ky, kz, diag, image, flip, *, depth, rows, cols, samples):
    width = cols + LANES
    half = depth // 2
    span = rows + 2 * HALO
    parts = (slice(0, half), slice(half, depth))
    odd, col_odd = flags[0] == 1, flags[1] == 1
    top, bottom, left, right = (flags[i].astype(jnp.float32) for i in range(2, 6))
    middle = (highest + lowest) / 2.0
    spread = (highest - lowest) / 2.0
    lane = lax.broadcasted_iota(jnp.int32, (half, LANES), 1)
    tail = (lane < HALO, lane >= LANES - HALO)

    def side_lanes(lo, hi, at):
        shift_hi = (LANES - at * HALO) % LANES
        shift_lo = (2 * LANES - HALO - at * HALO) % LANES
        hi = pltpu.roll(hi, shift_hi, 1) if shift_hi else hi
        lo = pltpu.roll(lo, shift_lo, 1) if shift_lo else lo
        return jnp.where(tail[0], hi, jnp.where(tail[1], lo, 0.0))

    def slabs_of(a):
        def ordered(pick):
            o, e = pick(0), pick(1)
            return jnp.where(col_odd, e, o), jnp.where(col_odd, o, e)

        own = [ordered(lambda i, t=t: (strip_odd, strip_even)[i][a, parts[t]]) for t in range(2)]
        far_odd = [ordered(lambda i, t=t: corner_odd[i, a, parts[t]]) for t in range(2)]
        far_even = [ordered(lambda i, t=t: corner_even[i, a, parts[t]]) for t in range(2)]
        above = [[jnp.where(odd, e, o) for o, e in zip(far_odd[t], far_even[t])] for t in range(2)]
        below = [[jnp.where(odd, o, e) for o, e in zip(far_odd[t], far_even[t])] for t in range(2)]
        for j in range(span):
            if j < HALO:
                slab = [jnp.where(odd, rows_even[a, j, p], rows_odd[a, j, p]) for p in parts]
                sides, at = above, rows - HALO + j
            elif j < HALO + rows:
                at = (j - HALO) % (rows - HALO)
                lower = j - HALO >= rows - HALO
                mine = (own_even, own_odd) if lower else (own_odd, own_even)
                slab = [jnp.where(odd, mine[1][a, at, p], mine[0][a, at, p]) for p in parts]
                sides, at = own, j - HALO
            else:
                at = j - HALO - rows
                slab = [jnp.where(odd, rows_odd[a, at, p], rows_even[a, at, p]) for p in parts]
                sides = below
            yield j, [jnp.concatenate([slab[t], side_lanes(*sides[t], at)], axis=1) for t in range(2)]

    for j, slab in slabs_of(0):
        for t in range(2):
            if HALO <= j < HALO + rows:
                image[j - HALO, parts[t]] = slab[t][:, :cols]
            first = slab[t] * (1.0 / middle)
            res[j, parts[t]] = slab[t]
            dirn[j, parts[t]] = first
            pre[j, parts[t]] = first[:, :cols]

    deep = lax.broadcasted_iota(jnp.int32, (half, width), 0)
    wide = lax.broadcasted_iota(jnp.int32, (half, width), 1)

    def flag(mask):
        return jnp.where(mask, 1.0, 0.0)

    sides = left * flag(wide == 0) + right * flag(wide == cols - 1)
    ends = [sides + flag(deep == 0), sides + flag(deep == half - 1)]
    x_inner = 1.0 - right * flag(wide == cols - 1) - left * flag(wide == width - 1)
    z_inner = flag(deep < half - 1)
    last = None
    for j, slab in slabs_of(1):
        halves = [0.5 * v for v in slab]
        if last is not None:
            for t in range(2):
                open_face = 1.0 - (top if j == HALO else bottom) if j in (HALO, HALO + rows) else None
                face = last[t] + halves[t]
                ky[j - 1, parts[t]] = face if open_face is None else face * open_face
        if 0 < j < span - 1:
            kz[j, parts[0]] = halves[0] + halves[1]
            kz[j, parts[1]] = (halves[1] + ahead(halves[0], 0)) * z_inner
            for t in range(2):
                kx[j, parts[t]] = (halves[t] + ahead(halves[t], 1)) * x_inner
                edge = ends[t]
                if j == HALO:
                    edge = edge + top
                if j == HALO + rows - 1:
                    edge = edge + bottom
                diag[j, parts[t]] = reaction + halves[t] * edge
        last = halves

    def sweep(low, high, emit):
        def body(j, carry):
            here, turned, flux_y = carry
            nxt = [dirn[j + 1, p] for p in parts]
            nxt_turned = [ahead(v, 1) for v in nxt]
            flux = [ky[j, parts[t]] * (here[t] - nxt[t]) for t in range(2)]
            flux_x = [kx[j, parts[t]] * (here[t] - turned[t]) for t in range(2)]
            flux_z0 = kz[j, parts[0]] * (here[0] - here[1])
            flux_z1 = kz[j, parts[1]] * (here[1] - ahead(here[0], 0))
            along_z = (flux_z0 - back(flux_z1, 0), flux_z1 - flux_z0)
            for t in range(2):
                applied = (diag[j, parts[t]] * here[t] + (flux[t] - flux_y[t])) + along_z[t]
                applied = applied + (flux_x[t] - back(flux_x[t], 1))
                emit(j, t, here[t], applied)
            return nxt, nxt_turned, flux

        before = [dirn[low - 1, p] for p in parts]
        here = [dirn[low, p] for p in parts]
        first_flux = [ky[low - 1, parts[t]] * (before[t] - here[t]) for t in range(2)]
        lax.fori_loop(low, high, body, (here, [ahead(v, 1) for v in here], first_flux))

    sig_ratio = middle / spread
    rho_now = 1.0 / sig_ratio
    for step in range(1, SWEEPS):
        rho_next = 1.0 / (2.0 * sig_ratio - rho_now)
        keep, gain = rho_next * rho_now, 2.0 * rho_next / spread
        rho_now = rho_next

        def emit(j, t, here, applied):
            left_over = res[j, parts[t]] - applied
            res[j, parts[t]] = left_over
            fresh = keep * here + gain * left_over
            dirn[j, parts[t]] = fresh
            pre[j, parts[t]] = pre[j, parts[t]] + fresh[:, :cols]

        sweep(step, span - step, emit)

    def finish(j, t, here, applied):
        row = j - HALO
        image[row, parts[t]] = image[row, parts[t]] - (res[j, parts[t], :cols] - applied[:, :cols])

    sweep(HALO, HALO + rows, finish)
    for c in range(cols // LANES):
        part = slice(c * LANES, (c + 1) * LANES)
        for r in range(0, rows, half):
            sign = signs[r : r + half, part].astype(jnp.float32)
            for t in range(2):
                kept = turn([pre[HALO + r + i, parts[t], part] for i in range(half)])
                made = turn([image[r + i, parts[t], part] for i in range(half)])
                for s in range(half):
                    cell = 2 * s + t
                    precond_out[cell, r : r + half, part] = kept[s]
                    image_out[cell, r : r + half, part] = made[s]
                    flip[cell * rows + r : cell * rows + r + half, part] = made[s] * sign
    col_ids = lax.broadcasted_iota(jnp.int32, (samples, cols), 1)
    chosen = (picks[...] == col_ids).astype(jnp.float32)
    picked = lax.dot_general(chosen, flip[...], (((1,), (1,)), ((), ())),
                             precision=lax.Precision.HIGHEST, preferred_element_type=jnp.float32)
    sketch_out[...] = lax.dot_general(picked, mix[...], (((1,), (0,)), ((), ())),
                                      precision=lax.Precision.HIGHEST, preferred_element_type=jnp.float32)


def per_device(basis_vec, conductivity, sign_vals, sample_cols):
    depth, rows, cols = basis_vec.shape
    samples = sample_cols.shape[0]
    gx_size, gy_size = lax.axis_size("gx"), lax.axis_size("gy")
    gx_index, gy_index = lax.axis_index("gx"), lax.axis_index("gy")
    flags = jnp.stack([
        gx_index & 1, gy_index & 1, gx_index == 0, gx_index == gx_size - 1, gy_index == 0, gy_index == gy_size - 1,
    ]).astype(jnp.int32)
    smem = pl.BlockSpec(memory_space=pltpu.SMEM)
    vmem = pl.BlockSpec(memory_space=pltpu.VMEM)
    sizes = dict(depth=depth, rows=rows, cols=cols)
    f32 = jnp.float32
    row_msg = jax.ShapeDtypeStruct((2, HALO, depth, cols), f32)
    strip_msg = jax.ShapeDtypeStruct((2, depth, LANES), f32)
    to_odd, to_even, strip_to_odd, strip_to_even = pl.pallas_call(
        lambda *refs: pack_kernel(*refs, **sizes),
        in_specs=[smem, vmem, vmem],
        out_specs=[vmem] * 4,
        out_shape=[row_msg, row_msg, strip_msg, strip_msg],
        compiler_params=pltpu.CompilerParams(vmem_limit_bytes=8 << 20),
        name="pack",
    )(flags, basis_vec, conductivity)
    with jax.named_scope("rows_odd"):
        rows_odd = exchange(to_odd, odd_pair, same)
    with jax.named_scope("strip_odd"):
        strip_odd = exchange(strip_to_odd, same, odd_pair)
    with jax.named_scope("strip_even"):
        strip_even = exchange(strip_to_even, same, even_pair)
    with jax.named_scope("rows_even"):
        rows_even = exchange(to_even, even_pair, same)
    strips = jnp.stack([strip_odd, strip_even])
    with jax.named_scope("corner_odd"):
        corner_odd = exchange(strips, odd_pair, same)
    with jax.named_scope("corner_even"):
        corner_even = exchange(strips, even_pair, same)
    mix = jnp.asarray(hartley_mix(depth, rows, 1.0 / np.sqrt(gx_size)))
    span, width = rows + 2 * HALO, cols + LANES
    precond, image, current = pl.pallas_call(
        lambda *refs: main_kernel(*refs, samples=samples, **sizes),
        in_specs=[smem] + [vmem] * 11,
        out_specs=[vmem] * 3,
        out_shape=[jax.ShapeDtypeStruct((depth, rows, cols), f32)] * 2
        + [jax.ShapeDtypeStruct((samples, depth * rows), f32)],
        scratch_shapes=[pltpu.VMEM((span, depth, width), f32)] * 2
        + [pltpu.VMEM((span, depth, cols), f32)]
        + [pltpu.VMEM((span, depth, width), f32)] * 4
        + [
            pltpu.VMEM((rows, depth, cols), f32),
            pltpu.VMEM((depth * rows, cols), f32),
        ],
        compiler_params=pltpu.CompilerParams(vmem_limit_bytes=24 << 20),
        name="solve",
    )(flags, to_odd, to_even, rows_odd, rows_even, strip_odd, strip_even, corner_odd, corner_even,
      sign_vals, sample_cols.reshape(samples, 1), mix)
    gx_bits = gx_size.bit_length() - 1
    for group in [[0]] + bit_groups(list(range(1, gx_bits))):
        total = walsh_sign(gx_index, 0, group) * current
        for mask in masks_of(group)[1:]:
            total = total + walsh_sign(gx_index, mask, group) * swap(current, "gx", mask)
        current = total
    for group in bit_groups(list(range(gy_size.bit_length() - 1))):
        current = current + sum(swap(current, "gy", mask) for mask in masks_of(group)[1:])
    return precond, image, current.T.reshape(depth, rows, samples)


def solution(mesh):
    in_specs = (P(None, "gx", "gy"), P(None, "gx", "gy"), P("gx", "gy"), P("gy"))
    out_specs = (P(None, "gx", "gy"), P(None, "gx", "gy"), P(None, "gx", None))
    return jax.shard_map(
        per_device, mesh=mesh, in_specs=in_specs, out_specs=out_specs, check_vma=False
    )
```

time: 61 us -> 57.5 us (0.943)
  Pallas kernels: 23 us -> 20.5 us
  local copies, waits for them, and re-layouts: 4 us -> 2.84 us
    pallas_call x1, Pallas kernels: 2.04 us -> 0.76 us  [per_device(): pl.pallas_call(lambda *refs: pack_kernel(*refs, **sizes), in_specs=[smem,...]
    pallas_call x1, Pallas kernels: 21 us -> 19.8 us  [per_device(): pl.pallas_call(lambda *refs: main_kernel(*refs, samples=samples, **sizes)...]
    unnamed x17 -> x11, local copies, waits for them, and re-layouts: 2.75 us -> 2.67 us
  transfers between devices with their start and end apart: 13 -> 13, of which waited for: 7 -> 7; matrix products, arithmetic and copies ran while one was open for 1% -> 0% of each run, Pallas kernels for 0% -> 0%
where the time goes in v2:
time: 57.5 us; the launch traced here: 57.2 us
  starting transfers between devices  23.4 us (41%)
  Pallas kernels  20.5 us (36%)
  waiting for transfers between devices  9.68 us (17%)
  local copies, waits for them, and re-layouts  2.84 us (5%)
  between operations  0.71 us (1%)
    pallas_call x1, Pallas kernels, per_device(): pl.pallas_call(lambda *refs: main_kernel(*refs, samples=samples, **sizes)...  19.8 us
    ppermute x6, starting transfers between devices, exchange(): return lax.ppermute(array, AXES, pairs)  13.9 us
    ppermute x7, starting transfers between devices, swap(): lax.ppermute(array, axis, [(i, i ^ mask) for i in range(lax.axis_size(axi...  9.55 us
    ppermute x7, waiting for transfers between devices, swap(): lax.ppermute(array, axis, [(i, i ^ mask) for i in range(lax.axis_size(axi...  7.18 us
    unnamed x11, local copies, waits for them, and re-layouts  2.67 us
    ppermute x6, waiting for transfers between devices, exchange(): return lax.ppermute(array, AXES, pairs)  2.5 us
  transfers between devices with their start and end apart: 13, of which 7 were waited for; matrix products, arithmetic and copies ran while one was open for 0% of the time, Pallas kernels for 0%

profile of v2, /device:TPU:0, one launch (start us, length us, event | category | flops | bytes accessed | tf_op | source)
XLA Modules:
  0.0 57.2 jit_solution(3030192037469659478)
XLA Ops:
  0.6 0.1 stack.52.refs_0_
  0.7 1.0 %copy-done = f32[16,16,256]{2,1,0:T(8,128)S(1)} copy-done((f32[16,16,256]{2,1,0:T(8,128)S(1)}, f32[16,16,256]{2,1,0:T(8,128)}, u32[]{:S(2)}) %copy-start) | copy-done | bytes 262168
  1.7 0.9 %copy-done.1 = f32[16,16,256]{2,1,0:T(8,128)S(1)} copy-done((f32[16,16,256]{2,1,0:T(8,128)S(1)}, f32[16,16,256]{2,1,0:T(8,128)}, u32[]{:S(2)}) %copy-start.1) | copy-done | bytes 262168
  2.6 0.8 %pack.1 = (f32[2,8,16,256]{3,2,1,0:T(8,128)S(1)}, f32[2,8,16,256]{3,2,1,0:T(8,128)S(1)}, f32[2,16,128]{2,1,0:T(8,128)S(1)}, f32[2,16,128]{2,1,0:T(8,128)S(1)}) custom-call(s32[6]{0:T(128)S(1)} %stack.52.refs_0_, f32[16,16,256]{2,1,0:T(8,128)S(1)} %copy-done, f32[16,16,256]{2,1,0:T(8,128)S(1)} %copy-done.1), custom_call_target="tpu_custom_call" | custom-call | tf_op jit(solution)/shard_map/pack/pallas_call | solution.py:286
  3.4 0.7 %collective-permute-start = (f32[2,8,16,256]{3,2,1,0:T(8,128)S(1)}, f32[2,8,16,256]{3,2,1,0:T(8,128)S(1)}, u32[]{:S(2)}, u32[]{:S(2)}) collective-permute-start(f32[2,8,16,256]{3,2,1,0:T(8,128)S(1)} %get-tuple-element.10.refs_1_), channel_id=1, source_target_pairs={{4,8},{5,9},{6,10},{7,11},{8,4},{9,5},{10,6},{11,7},{12,16},{13,17... | collective-permute-start | bytes 786440 | tf_op jit(solution)/shard_map/rows_odd/ppermute | solution.py:39
  4.1 4.4 %collective-permute-start.1 = (f32[2,8,16,256]{3,2,1,0:T(8,128)S(1)}, f32[2,8,16,256]{3,2,1,0:T(8,128)S(1)}, u32[]{:S(2)}, u32[]{:S(2)}) collective-permute-start(f32[2,8,16,256]{3,2,1,0:T(8,128)S(1)} %get-tuple-element.11.refs_2_), channel_id=1, source_target_pairs={{0,4},{1,5},{2,6},{3,7},{4,0},{5,1},{6,2},{7,3},{8,12},{9,13},{10,... | collective-permute-start | bytes 786440 | tf_op jit(solution)/shard_map/rows_even/ppermute | solution.py:39
  8.5 0.7 %collective-permute-start.2 = (f32[2,16,128]{2,1,0:T(8,128)S(1)}, f32[2,16,128]{2,1,0:T(8,128)S(1)}, u32[]{:S(2)}, u32[]{:S(2)}) collective-permute-start(f32[2,16,128]{2,1,0:T(8,128)S(1)} %get-tuple-element.12), channel_id=1, source_target_pairs={{1,2},{2,1},{5,6},{6,5},{9,10},{10,9},{13,14},{14,13},{17,18},{18,... | collective-permute-start | bytes 49160 | tf_op jit(solution)/shard_map/strip_odd/ppermute | solution.py:39
  9.1 4.5 %collective-permute-start.3 = (f32[2,16,128]{2,1,0:T(8,128)S(1)}, f32[2,16,128]{2,1,0:T(8,128)S(1)}, u32[]{:S(2)}, u32[]{:S(2)}) collective-permute-start(f32[2,16,128]{2,1,0:T(8,128)S(1)} %get-tuple-element.13), channel_id=1, source_target_pairs={{0,1},{1,0},{2,3},{3,2},{4,5},{5,4},{6,7},{7,6},{8,9},{9,8},{10,11... | collective-permute-start | bytes 49160 | tf_op jit(solution)/shard_map/strip_even/ppermute | solution.py:39
  13.6 0.0 collective-permute-done.2.refs_5_
  13.6 1.7 %collective-permute-done.3.refs_6_ = f32[2,16,128]{2,1,0:T(8,128)S(1)} collective-permute-done((f32[2,16,128]{2,1,0:T(8,128)S(1)}, f32[2,16,128]{2,1,0:T(8,128)S(1)}, u32[]{:S(2)}, u32[]{:S(2)}) %collective-permute-start.3) | collective-permute-done | bytes 16416 | tf_op jit(solution)/shard_map/strip_even/ppermute | solution.py:39
  15.3 0.8 %collective-permute-start.4 = (f32[2,2,16,128]{3,2,1,0:T(8,128)S(1)}, f32[2,2,16,128]{3,2,1,0:T(8,128)S(1)}, u32[]{:S(2)}, u32[]{:S(2)}) collective-permute-start(f32[2,2,16,128]{3,2,1,0:T(8,128)S(1)} %pad_maximum_fusion), channel_id=1, source_target_pairs={{4,8},{5,9},{6,10},{7,11},{8,4},{9,5},{10,6},{11,7},{12,16},{13,17... | collective-permute-start | bytes 98312 | tf_op jit(solution)/shard_map/corner_odd/ppermute | solution.py:39
  16.1 2.9 %collective-permute-start.5 = (f32[2,2,16,128]{3,2,1,0:T(8,128)S(1)}, f32[2,2,16,128]{3,2,1,0:T(8,128)S(1)}, u32[]{:S(2)}, u32[]{:S(2)}) collective-permute-start(f32[2,2,16,128]{3,2,1,0:T(8,128)S(1)} %pad_maximum_fusion), channel_id=1, source_target_pairs={{0,4},{1,5},{2,6},{3,7},{4,0},{5,1},{6,2},{7,3},{8,12},{9,13},{10,... | collective-permute-start | bytes 98312 | tf_op jit(solution)/shard_map/corner_even/ppermute | solution.py:39
  19.0 0.1 copy.8.refs_10_
  19.1 0.0 collective-permute-done.4.refs_7_
  19.1 0.8 %collective-permute-done.5.refs_8_ = f32[2,2,16,128]{3,2,1,0:T(8,128)S(1)} collective-permute-done((f32[2,2,16,128]{3,2,1,0:T(8,128)S(1)}, f32[2,2,16,128]{3,2,1,0:T(8,128)S(1)}, u32[]{:S(2)}, u32[]{:S(2)}) %collective-permute-start.5) | collective-permute-done | bytes 32800 | tf_op jit(solution)/shard_map/corner_even/ppermute | solution.py:39
  19.9 0.0 collective-permute-done.refs_3_
  19.9 0.0 collective-permute-done.1.refs_4_
  19.9 19.8 %solve.1 = (f32[16,16,256]{2,1,0:T(8,128)}, f32[16,16,256]{2,1,0:T(8,128)}, f32[16,256]{1,0:T(8,128)S(1)}) custom-call(s32[6]{0:T(128)S(1)} %stack.52.refs_0_, f32[2,8,16,256]{3,2,1,0:T(8,128)S(1)} %get-tuple-element.10.refs_1_, f32[2,8,16,256]{3,2,1,0:T(8,128)S(1)} %get-tuple-element.11.refs_2_, f32[2,8,16,256]{3,2,1,0:T(8,128)S(1)} %collective-permute-done.refs_3_, ...), custom_call_target="tpu_custom_call" | custom-call | tf_op jit(solution)/shard_map/solve/pallas_call | solution.py:309
  39.7 0.7 %collective-permute-start.6 = (f32[16,256]{1,0:T(8,128)S(1)}, f32[16,256]{1,0:T(8,128)S(1)}, u32[]{:S(2)}, u32[]{:S(2)}) collective-permute-start(f32[16,256]{1,0:T(8,128)S(1)} %get-tuple-element.16), channel_id=1, source_target_pairs={{0,4},{4,0},{8,12},{12,8},{16,20},{20,16},{24,28},{28,24},{1,5},{5... | collective-permute-start | bytes 49160 | tf_op jit(solution)/shard_map/ppermute | solution.py:43
  40.4 0.8 %collective-permute-done.6 = f32[16,256]{1,0:T(8,128)S(1)} collective-permute-done((f32[16,256]{1,0:T(8,128)S(1)}, f32[16,256]{1,0:T(8,128)S(1)}, u32[]{:S(2)}, u32[]{:S(2)}) %collective-permute-start.6) | collective-permute-done | bytes 16416 | tf_op jit(solution)/shard_map/ppermute | solution.py:43
  41.2 2.0 %collective-permute-start.7 = (f32[16,256]{1,0:T(8,128)S(1)}, f32[16,256]{1,0:T(8,128)S(1)}, u32[]{:S(2)}, u32[]{:S(2)}) collective-permute-start(f32[16,256]{1,0:T(8,128)S(1)} %multiply_add_fusion.1), channel_id=1, source_target_pairs={{0,8},{4,12},{8,0},{12,4},{16,24},{20,28},{24,16},{28,20},{1,9},{5... | collective-permute-start | bytes 49160 | tf_op jit(solution)/shard_map/ppermute | solution.py:43
  43.2 1.0 %collective-permute-start.8 = (f32[16,256]{1,0:T(8,128)S(1)}, f32[16,256]{1,0:T(8,128)S(1)}, u32[]{:S(2)}, u32[]{:S(2)}) collective-permute-start(f32[16,256]{1,0:T(8,128)S(1)} %multiply_add_fusion.1), channel_id=1, source_target_pairs={{0,16},{4,20},{8,24},{12,28},{16,0},{20,4},{24,8},{28,12},{1,17},{... | collective-permute-start | bytes 49160 | tf_op jit(solution)/shard_map/ppermute | solution.py:43
  44.2 1.4 %collective-permute-start.9 = (f32[16,256]{1,0:T(8,128)S(1)}, f32[16,256]{1,0:T(8,128)S(1)}, u32[]{:S(2)}, u32[]{:S(2)}) collective-permute-start(f32[16,256]{1,0:T(8,128)S(1)} %multiply_add_fusion.1), channel_id=1, source_target_pairs={{0,24},{4,28},{8,16},{12,20},{16,8},{20,12},{24,0},{28,4},{1,25},{... | collective-permute-start | bytes 49160 | tf_op jit(solution)/shard_map/ppermute | solution.py:43
  45.6 0.0 collective-permute-done.7
  45.6 1.3 %collective-permute-done.8 = f32[16,256]{1,0:T(8,128)S(1)} collective-permute-done((f32[16,256]{1,0:T(8,128)S(1)}, f32[16,256]{1,0:T(8,128)S(1)}, u32[]{:S(2)}, u32[]{:S(2)}) %collective-permute-start.8) | collective-permute-done | bytes 16416 | tf_op jit(solution)/shard_map/ppermute | solution.py:43
  46.9 1.9 %collective-permute-done.9 = f32[16,256]{1,0:T(8,128)S(1)} collective-permute-done((f32[16,256]{1,0:T(8,128)S(1)}, f32[16,256]{1,0:T(8,128)S(1)}, u32[]{:S(2)}, u32[]{:S(2)}) %collective-permute-start.9) | collective-permute-done | bytes 16416 | tf_op jit(solution)/shard_map/ppermute | solution.py:43
  48.8 2.1 %collective-permute-start.10 = (f32[16,256]{1,0:T(8,128)S(1)}, f32[16,256]{1,0:T(8,128)S(1)}, u32[]{:S(2)}, u32[]{:S(2)}) collective-permute-start(f32[16,256]{1,0:T(8,128)S(1)} %multiply_add_fusion), channel_id=1, source_target_pairs={{0,1},{1,0},{2,3},{3,2},{4,5},{5,4},{6,7},{7,6},{8,9},{9,8},{10,11... | collective-permute-start | bytes 49160 | tf_op jit(solution)/shard_map/ppermute | solution.py:43
  50.9 0.0 collective-permute-start.11
  50.9 2.4 %collective-permute-start.12 = (f32[16,256]{1,0:T(8,128)S(1)}, f32[16,256]{1,0:T(8,128)S(1)}, u32[]{:S(2)}, u32[]{:S(2)}) collective-permute-start(f32[16,256]{1,0:T(8,128)S(1)} %multiply_add_fusion), channel_id=1, source_target_pairs={{0,3},{1,2},{2,1},{3,0},{4,7},{5,6},{6,5},{7,4},{8,11},{9,10},{10,... | collective-permute-start | bytes 49160 | tf_op jit(solution)/shard_map/ppermute | solution.py:43
  53.4 2.2 %collective-permute-done.11 = f32[16,256]{1,0:T(8,128)S(1)} collective-permute-done((f32[16,256]{1,0:T(8,128)S(1)}, f32[16,256]{1,0:T(8,128)S(1)}, u32[]{:S(2)}, u32[]{:S(2)}) %collective-permute-start.11) | collective-permute-done | bytes 16416 | tf_op jit(solution)/shard_map/ppermute | solution.py:43
  55.6 0.9 %collective-permute-done.12 = f32[16,256]{1,0:T(8,128)S(1)} collective-permute-done((f32[16,256]{1,0:T(8,128)S(1)}, f32[16,256]{1,0:T(8,128)S(1)}, u32[]{:S(2)}, u32[]{:S(2)}) %collective-permute-start.12) | collective-permute-done | bytes 16416 | tf_op jit(solution)/shard_map/ppermute | solution.py:43
  56.5 0.8 %copy.10 = f32[256,16]{1,0:T(8,128)} copy(f32[256,16]{0,1:T(8,128)S(1)} %add_bitcast_fusion) | data formatting | bytes 32768
  (13 shorter events, 0.0 us)
Async XLA Ops:
  0.7 1.0 %copy-start = (f32[16,16,256]{2,1,0:T(8,128)S(1)}, f32[16,16,256]{2,1,0:T(8,128)}, u32[]{:S(2)}) copy-start(f32[16,16,256]{2,1,0:T(8,128)} %refs_1_.1) | copy-start | bytes 786436
  1.7 0.9 %copy-start.1 = (f32[16,16,256]{2,1,0:T(8,128)S(1)}, f32[16,16,256]{2,1,0:T(8,128)}, u32[]{:S(2)}) copy-start(f32[16,16,256]{2,1,0:T(8,128)} %refs_2_.1) | copy-start | bytes 786436
  2.6 17.3 %copy-start.2 = (f32[256,256]{1,0:T(8,128)S(1)}, f32[256,256]{1,0:T(8,128)}, u32[]{:S(2)}) copy-start(f32[256,256]{1,0:T(8,128)} %constant.25.clone.refs_11_) | copy-start | bytes 786436
  3.4 16.5 %collective-permute-start = (f32[2,8,16,256]{3,2,1,0:T(8,128)S(1)}, f32[2,8,16,256]{3,2,1,0:T(8,128)S(1)}, u32[]{:S(2)}, u32[]{:S(2)}) collective-permute-start(f32[2,8,16,256]{3,2,1,0:T(8,128)S(1)} %get-tuple-element.10.refs_1_), channel_id=1, source_target_pairs={{4,8},{5,9},{6,10},{7,11},{8,4},{9,5},{10,6},{11,7},{12,16},{13,17... | collective-permute-start | bytes 786440 | tf_op jit(solution)/shard_map/rows_odd/ppermute | solution.py:39
  4.1 15.8 %collective-permute-start.1 = (f32[2,8,16,256]{3,2,1,0:T(8,128)S(1)}, f32[2,8,16,256]{3,2,1,0:T(8,128)S(1)}, u32[]{:S(2)}, u32[]{:S(2)}) collective-permute-start(f32[2,8,16,256]{3,2,1,0:T(8,128)S(1)} %get-tuple-element.11.refs_2_), channel_id=1, source_target_pairs={{0,4},{1,5},{2,6},{3,7},{4,0},{5,1},{6,2},{7,3},{8,12},{9,13},{10,... | collective-permute-start | bytes 786440 | tf_op jit(solution)/shard_map/rows_even/ppermute | solution.py:39
  8.5 5.1 %collective-permute-start.2 = (f32[2,16,128]{2,1,0:T(8,128)S(1)}, f32[2,16,128]{2,1,0:T(8,128)S(1)}, u32[]{:S(2)}, u32[]{:S(2)}) collective-permute-start(f32[2,16,128]{2,1,0:T(8,128)S(1)} %get-tuple-element.12), channel_id=1, source_target_pairs={{1,2},{2,1},{5,6},{6,5},{9,10},{10,9},{13,14},{14,13},{17,18},{18,... | collective-permute-start | bytes 49160 | tf_op jit(solution)/shard_map/strip_odd/ppermute | solution.py:39
  9.1 6.2 %collective-permute-start.3 = (f32[2,16,128]{2,1,0:T(8,128)S(1)}, f32[2,16,128]{2,1,0:T(8,128)S(1)}, u32[]{:S(2)}, u32[]{:S(2)}) collective-permute-start(f32[2,16,128]{2,1,0:T(8,128)S(1)} %get-tuple-element.13), channel_id=1, source_target_pairs={{0,1},{1,0},{2,3},{3,2},{4,5},{5,4},{6,7},{7,6},{8,9},{9,8},{10,11... | collective-permute-start | bytes 49160 | tf_op jit(solution)/shard_map/strip_even/ppermute | solution.py:39
  15.3 4.6 %copy-start.3 = (s32[16,256]{1,0:T(8,128)S(1)}, s32[16,256]{1,0:T(8,128)}, u32[]{:S(2)}) copy-start(s32[16,256]{1,0:T(8,128)} %refs_9_.1) | copy-start | bytes 49156
  15.3 3.7 %copy-start.4 = (s32[16]{0:T(128)S(1)}, s32[16]{0:T(128)}, u32[]{:S(2)}) copy-start(s32[16]{0:T(128)} %param.8) | copy-start | bytes 196
  15.3 3.8 %collective-permute-start.4 = (f32[2,2,16,128]{3,2,1,0:T(8,128)S(1)}, f32[2,2,16,128]{3,2,1,0:T(8,128)S(1)}, u32[]{:S(2)}, u32[]{:S(2)}) collective-permute-start(f32[2,2,16,128]{3,2,1,0:T(8,128)S(1)} %pad_maximum_fusion), channel_id=1, source_target_pairs={{4,8},{5,9},{6,10},{7,11},{8,4},{9,5},{10,6},{11,7},{12,16},{13,17... | collective-permute-start | bytes 98312 | tf_op jit(solution)/shard_map/corner_odd/ppermute | solution.py:39
  16.1 3.8 %collective-permute-start.5 = (f32[2,2,16,128]{3,2,1,0:T(8,128)S(1)}, f32[2,2,16,128]{3,2,1,0:T(8,128)S(1)}, u32[]{:S(2)}, u32[]{:S(2)}) collective-permute-start(f32[2,2,16,128]{3,2,1,0:T(8,128)S(1)} %pad_maximum_fusion), channel_id=1, source_target_pairs={{0,4},{1,5},{2,6},{3,7},{4,0},{5,1},{6,2},{7,3},{8,12},{9,13},{10,... | collective-permute-start | bytes 98312 | tf_op jit(solution)/shard_map/corner_even/ppermute | solution.py:39
  39.7 1.5 %collective-permute-start.6 = (f32[16,256]{1,0:T(8,128)S(1)}, f32[16,256]{1,0:T(8,128)S(1)}, u32[]{:S(2)}, u32[]{:S(2)}) collective-permute-start(f32[16,256]{1,0:T(8,128)S(1)} %get-tuple-element.16), channel_id=1, source_target_pairs={{0,4},{4,0},{8,12},{12,8},{16,20},{20,16},{24,28},{28,24},{1,5},{5... | collective-permute-start | bytes 49160 | tf_op jit(solution)/shard_map/ppermute | solution.py:43
  41.2 4.4 %collective-permute-start.7 = (f32[16,256]{1,0:T(8,128)S(1)}, f32[16,256]{1,0:T(8,128)S(1)}, u32[]{:S(2)}, u32[]{:S(2)}) collective-permute-start(f32[16,256]{1,0:T(8,128)S(1)} %multiply_add_fusion.1), channel_id=1, source_target_pairs={{0,8},{4,12},{8,0},{12,4},{16,24},{20,28},{24,16},{28,20},{1,9},{5... | collective-permute-start | bytes 49160 | tf_op jit(solution)/shard_map/ppermute | solution.py:43
  43.2 3.7 %collective-permute-start.8 = (f32[16,256]{1,0:T(8,128)S(1)}, f32[16,256]{1,0:T(8,128)S(1)}, u32[]{:S(2)}, u32[]{:S(2)}) collective-permute-start(f32[16,256]{1,0:T(8,128)S(1)} %multiply_add_fusion.1), channel_id=1, source_target_pairs={{0,16},{4,20},{8,24},{12,28},{16,0},{20,4},{24,8},{28,12},{1,17},{... | collective-permute-start | bytes 49160 | tf_op jit(solution)/shard_map/ppermute | solution.py:43
  44.2 4.6 %collective-permute-start.9 = (f32[16,256]{1,0:T(8,128)S(1)}, f32[16,256]{1,0:T(8,128)S(1)}, u32[]{:S(2)}, u32[]{:S(2)}) collective-permute-start(f32[16,256]{1,0:T(8,128)S(1)} %multiply_add_fusion.1), channel_id=1, source_target_pairs={{0,24},{4,28},{8,16},{12,20},{16,8},{20,12},{24,0},{28,4},{1,25},{... | collective-permute-start | bytes 49160 | tf_op jit(solution)/shard_map/ppermute | solution.py:43
  48.8 4.5 %collective-permute-start.10 = (f32[16,256]{1,0:T(8,128)S(1)}, f32[16,256]{1,0:T(8,128)S(1)}, u32[]{:S(2)}, u32[]{:S(2)}) collective-permute-start(f32[16,256]{1,0:T(8,128)S(1)} %multiply_add_fusion), channel_id=1, source_target_pairs={{0,1},{1,0},{2,3},{3,2},{4,5},{5,4},{6,7},{7,6},{8,9},{9,8},{10,11... | collective-permute-start | bytes 49160 | tf_op jit(solution)/shard_map/ppermute | solution.py:43
  50.9 4.6 %collective-permute-start.11 = (f32[16,256]{1,0:T(8,128)S(1)}, f32[16,256]{1,0:T(8,128)S(1)}, u32[]{:S(2)}, u32[]{:S(2)}) collective-permute-start(f32[16,256]{1,0:T(8,128)S(1)} %multiply_add_fusion), channel_id=1, source_target_pairs={{0,2},{1,3},{2,0},{3,1},{4,6},{5,7},{6,4},{7,5},{8,10},{9,11},{10,... | collective-permute-start | bytes 49160 | tf_op jit(solution)/shard_map/ppermute | solution.py:43
  50.9 5.5 %collective-permute-start.12 = (f32[16,256]{1,0:T(8,128)S(1)}, f32[16,256]{1,0:T(8,128)S(1)}, u32[]{:S(2)}, u32[]{:S(2)}) collective-permute-start(f32[16,256]{1,0:T(8,128)S(1)} %multiply_add_fusion), channel_id=1, source_target_pairs={{0,3},{1,2},{2,1},{3,0},{4,7},{5,6},{6,5},{7,4},{8,11},{9,10},{10,... | collective-permute-start | bytes 49160 | tf_op jit(solution)/shard_map/ppermute | solution.py:43

commit v3 on v2

--- a/solution.py
+++ b/solution.py
@@ -122,7 +122,7 @@
 
 def main_kernel(flags, own_odd, own_even, rows_odd, rows_even, strip_odd, strip_even, corner_odd, corner_even,
                 signs, picks, mix, precond_out, image_out, sketch_out,
-                res, dirn, pre, kx, ky, kz, diag, image, flip, *, depth, rows, cols, samples):
+                res, dirn, across, pre, kx, ky, kz, diag, image, flip, *, depth, rows, cols, samples):
     width = cols + LANES
     half = depth // 2
     span = rows + 2 * HALO
@@ -208,25 +208,23 @@
         last = halves
 
     def sweep(low, high, emit):
-        def body(j, carry):
-            here, turned, flux_y = carry
+        for j in range(low, high):
+            for t in range(2):
+                here = dirn[j, parts[t]]
+                across[j, parts[t]] = kx[j, parts[t]] * (here - ahead(here, 1))
+        here = [dirn[low, p] for p in parts]
+        flux_y = [ky[low - 1, parts[t]] * (dirn[low - 1, parts[t]] - here[t]) for t in range(2)]
+        for j in range(low, high):
             nxt = [dirn[j + 1, p] for p in parts]
-            nxt_turned = [ahead(v, 1) for v in nxt]
             flux = [ky[j, parts[t]] * (here[t] - nxt[t]) for t in range(2)]
-            flux_x = [kx[j, parts[t]] * (here[t] - turned[t]) for t in range(2)]
             flux_z0 = kz[j, parts[0]] * (here[0] - here[1])
             flux_z1 = kz[j, parts[1]] * (here[1] - ahead(here[0], 0))
             along_z = (flux_z0 - back(flux_z1, 0), flux_z1 - flux_z0)
             for t in range(2):
+                flux_x = across[j, parts[t]]
                 applied = (diag[j, parts[t]] * here[t] + (flux[t] - flux_y[t])) + along_z[t]
-                applied = applied + (flux_x[t] - back(flux_x[t], 1))
-                emit(j, t, here[t], applied)
-            return nxt, nxt_turned, flux
-
-        before = [dirn[low - 1, p] for p in parts]
-        here = [dirn[low, p] for p in parts]
-        first_flux = [ky[low - 1, parts[t]] * (before[t] - here[t]) for t in range(2)]
-        lax.fori_loop(low, high, body, (here, [ahead(v, 1) for v in here], first_flux))
+                emit(j, t, here[t], applied + (flux_x - back(flux_x, 1)))
+            here, flux_y = nxt, flux
 
     sig_ratio = middle / spread
     rho_now = 1.0 / sig_ratio
@@ -312,7 +310,7 @@
         out_specs=[vmem] * 3,
         out_shape=[jax.ShapeDtypeStruct((depth, rows, cols), f32)] * 2
         + [jax.ShapeDtypeStruct((samples, depth * rows), f32)],
-        scratch_shapes=[pltpu.VMEM((span, depth, width), f32)] * 2
+        scratch_shapes=[pltpu.VMEM((span, depth, width), f32)] * 3
         + [pltpu.VMEM((span, depth, cols), f32)]
         + [pltpu.VMEM((span, depth, width), f32)] * 4
         + [

time: 57.5 us -> 45.4 us (0.79)
  Pallas kernels: 20.5 us -> 8.44 us
    pallas_call x1, Pallas kernels: 19.8 us -> 7.68 us  [per_device(): pl.pallas_call(lambda *refs: main_kernel(*refs, samples=samples, **sizes)...]
where the time goes in v3:
time: 45.4 us; the launch traced here: 45.1 us
  starting transfers between devices  23.4 us (52%)
  waiting for transfers between devices  9.68 us (21%)
  Pallas kernels  8.44 us (19%)
  local copies, waits for them, and re-layouts  2.84 us (6%)
  between operations  0.71 us (2%)
    ppermute x6, starting transfers between devices, exchange(): return lax.ppermute(array, AXES, pairs)  13.9 us
    ppermute x7, starting transfers between devices, swap(): lax.ppermute(array, axis, [(i, i ^ mask) for i in range(lax.axis_size(axi...  9.55 us
    pallas_call x1, Pallas kernels, per_device(): pl.pallas_call(lambda *refs: main_kernel(*refs, samples=samples, **sizes)...  7.68 us
    ppermute x7, waiting for transfers between devices, swap(): lax.ppermute(array, axis, [(i, i ^ mask) for i in range(lax.axis_size(axi...  7.18 us
    unnamed x11, local copies, waits for them, and re-layouts  2.67 us
    ppermute x6, waiting for transfers between devices, exchange(): return lax.ppermute(array, AXES, pairs)  2.5 us
  transfers between devices with their start and end apart: 13, of which 7 were waited for; matrix products, arithmetic and copies ran while one was open for 0% of the time, Pallas kernels for 0%

profile of v3, /device:TPU:0, one launch (start us, length us, event | category | flops | bytes accessed | tf_op | source)
XLA Modules:
  0.0 45.1 jit_solution(12894085975697777313)
XLA Ops:
  0.6 0.1 stack.52.refs_0_
  0.7 1.0 %copy-done = f32[16,16,256]{2,1,0:T(8,128)S(1)} copy-done((f32[16,16,256]{2,1,0:T(8,128)S(1)}, f32[16,16,256]{2,1,0:T(8,128)}, u32[]{:S(2)}) %copy-start) | copy-done | bytes 262168
  1.7 0.9 %copy-done.1 = f32[16,16,256]{2,1,0:T(8,128)S(1)} copy-done((f32[16,16,256]{2,1,0:T(8,128)S(1)}, f32[16,16,256]{2,1,0:T(8,128)}, u32[]{:S(2)}) %copy-start.1) | copy-done | bytes 262168
  2.6 0.8 %pack.1 = (f32[2,8,16,256]{3,2,1,0:T(8,128)S(1)}, f32[2,8,16,256]{3,2,1,0:T(8,128)S(1)}, f32[2,16,128]{2,1,0:T(8,128)S(1)}, f32[2,16,128]{2,1,0:T(8,128)S(1)}) custom-call(s32[6]{0:T(128)S(1)} %stack.52.refs_0_, f32[16,16,256]{2,1,0:T(8,128)S(1)} %copy-done, f32[16,16,256]{2,1,0:T(8,128)S(1)} %copy-done.1), custom_call_target="tpu_custom_call" | custom-call | tf_op jit(solution)/shard_map/pack/pallas_call | solution.py:284
  3.4 0.7 %collective-permute-start = (f32[2,8,16,256]{3,2,1,0:T(8,128)S(1)}, f32[2,8,16,256]{3,2,1,0:T(8,128)S(1)}, u32[]{:S(2)}, u32[]{:S(2)}) collective-permute-start(f32[2,8,16,256]{3,2,1,0:T(8,128)S(1)} %get-tuple-element.10.refs_1_), channel_id=1, source_target_pairs={{4,8},{5,9},{6,10},{7,11},{8,4},{9,5},{10,6},{11,7},{12,16},{13,17... | collective-permute-start | bytes 786440 | tf_op jit(solution)/shard_map/rows_odd/ppermute | solution.py:39
  4.1 4.4 %collective-permute-start.1 = (f32[2,8,16,256]{3,2,1,0:T(8,128)S(1)}, f32[2,8,16,256]{3,2,1,0:T(8,128)S(1)}, u32[]{:S(2)}, u32[]{:S(2)}) collective-permute-start(f32[2,8,16,256]{3,2,1,0:T(8,128)S(1)} %get-tuple-element.11.refs_2_), channel_id=1, source_target_pairs={{0,4},{1,5},{2,6},{3,7},{4,0},{5,1},{6,2},{7,3},{8,12},{9,13},{10,... | collective-permute-start | bytes 786440 | tf_op jit(solution)/shard_map/rows_even/ppermute | solution.py:39
  8.5 0.7 %collective-permute-start.2 = (f32[2,16,128]{2,1,0:T(8,128)S(1)}, f32[2,16,128]{2,1,0:T(8,128)S(1)}, u32[]{:S(2)}, u32[]{:S(2)}) collective-permute-start(f32[2,16,128]{2,1,0:T(8,128)S(1)} %get-tuple-element.12), channel_id=1, source_target_pairs={{1,2},{2,1},{5,6},{6,5},{9,10},{10,9},{13,14},{14,13},{17,18},{18,... | collective-permute-start | bytes 49160 | tf_op jit(solution)/shard_map/strip_odd/ppermute | solution.py:39
  9.1 4.5 %collective-permute-start.3 = (f32[2,16,128]{2,1,0:T(8,128)S(1)}, f32[2,16,128]{2,1,0:T(8,128)S(1)}, u32[]{:S(2)}, u32[]{:S(2)}) collective-permute-start(f32[2,16,128]{2,1,0:T(8,128)S(1)} %get-tuple-element.13), channel_id=1, source_target_pairs={{0,1},{1,0},{2,3},{3,2},{4,5},{5,4},{6,7},{7,6},{8,9},{9,8},{10,11... | collective-permute-start | bytes 49160 | tf_op jit(solution)/shard_map/strip_even/ppermute | solution.py:39
  13.6 0.0 collective-permute-done.2.refs_5_
  13.6 1.7 %collective-permute-done.3.refs_6_ = f32[2,16,128]{2,1,0:T(8,128)S(1)} collective-permute-done((f32[2,16,128]{2,1,0:T(8,128)S(1)}, f32[2,16,128]{2,1,0:T(8,128)S(1)}, u32[]{:S(2)}, u32[]{:S(2)}) %collective-permute-start.3) | collective-permute-done | bytes 16416 | tf_op jit(solution)/shard_map/strip_even/ppermute | solution.py:39
  15.3 0.8 %collective-permute-start.4 = (f32[2,2,16,128]{3,2,1,0:T(8,128)S(1)}, f32[2,2,16,128]{3,2,1,0:T(8,128)S(1)}, u32[]{:S(2)}, u32[]{:S(2)}) collective-permute-start(f32[2,2,16,128]{3,2,1,0:T(8,128)S(1)} %pad_maximum_fusion), channel_id=1, source_target_pairs={{4,8},{5,9},{6,10},{7,11},{8,4},{9,5},{10,6},{11,7},{12,16},{13,17... | collective-permute-start | bytes 98312 | tf_op jit(solution)/shard_map/corner_odd/ppermute | solution.py:39
  16.1 2.9 %collective-permute-start.5 = (f32[2,2,16,128]{3,2,1,0:T(8,128)S(1)}, f32[2,2,16,128]{3,2,1,0:T(8,128)S(1)}, u32[]{:S(2)}, u32[]{:S(2)}) collective-permute-start(f32[2,2,16,128]{3,2,1,0:T(8,128)S(1)} %pad_maximum_fusion), channel_id=1, source_target_pairs={{0,4},{1,5},{2,6},{3,7},{4,0},{5,1},{6,2},{7,3},{8,12},{9,13},{10,... | collective-permute-start | bytes 98312 | tf_op jit(solution)/shard_map/corner_even/ppermute | solution.py:39
  19.0 0.1 copy.8.refs_10_
  19.1 0.0 collective-permute-done.4.refs_7_
  19.1 0.8 %collective-permute-done.5.refs_8_ = f32[2,2,16,128]{3,2,1,0:T(8,128)S(1)} collective-permute-done((f32[2,2,16,128]{3,2,1,0:T(8,128)S(1)}, f32[2,2,16,128]{3,2,1,0:T(8,128)S(1)}, u32[]{:S(2)}, u32[]{:S(2)}) %collective-permute-start.5) | collective-permute-done | bytes 32800 | tf_op jit(solution)/shard_map/corner_even/ppermute | solution.py:39
  19.9 0.0 collective-permute-done.refs_3_
  19.9 0.0 collective-permute-done.1.refs_4_
  19.9 7.7 %solve.1 = (f32[16,16,256]{2,1,0:T(8,128)}, f32[16,16,256]{2,1,0:T(8,128)}, f32[16,256]{1,0:T(8,128)S(1)}) custom-call(s32[6]{0:T(128)S(1)} %stack.52.refs_0_, f32[2,8,16,256]{3,2,1,0:T(8,128)S(1)} %get-tuple-element.10.refs_1_, f32[2,8,16,256]{3,2,1,0:T(8,128)S(1)} %get-tuple-element.11.refs_2_, f32[2,8,16,256]{3,2,1,0:T(8,128)S(1)} %collective-permute-done.refs_3_, ...), custom_call_target="tpu_custom_call" | custom-call | tf_op jit(solution)/shard_map/solve/pallas_call | solution.py:307
  27.6 0.7 %collective-permute-start.6 = (f32[16,256]{1,0:T(8,128)S(1)}, f32[16,256]{1,0:T(8,128)S(1)}, u32[]{:S(2)}, u32[]{:S(2)}) collective-permute-start(f32[16,256]{1,0:T(8,128)S(1)} %get-tuple-element.16), channel_id=1, source_target_pairs={{0,4},{4,0},{8,12},{12,8},{16,20},{20,16},{24,28},{28,24},{1,5},{5... | collective-permute-start | bytes 49160 | tf_op jit(solution)/shard_map/ppermute | solution.py:43
  28.3 0.8 %collective-permute-done.6 = f32[16,256]{1,0:T(8,128)S(1)} collective-permute-done((f32[16,256]{1,0:T(8,128)S(1)}, f32[16,256]{1,0:T(8,128)S(1)}, u32[]{:S(2)}, u32[]{:S(2)}) %collective-permute-start.6) | collective-permute-done | bytes 16416 | tf_op jit(solution)/shard_map/ppermute | solution.py:43
  29.1 2.0 %collective-permute-start.7 = (f32[16,256]{1,0:T(8,128)S(1)}, f32[16,256]{1,0:T(8,128)S(1)}, u32[]{:S(2)}, u32[]{:S(2)}) collective-permute-start(f32[16,256]{1,0:T(8,128)S(1)} %multiply_add_fusion.1), channel_id=1, source_target_pairs={{0,8},{4,12},{8,0},{12,4},{16,24},{20,28},{24,16},{28,20},{1,9},{5... | collective-permute-start | bytes 49160 | tf_op jit(solution)/shard_map/ppermute | solution.py:43
  31.1 1.0 %collective-permute-start.8 = (f32[16,256]{1,0:T(8,128)S(1)}, f32[16,256]{1,0:T(8,128)S(1)}, u32[]{:S(2)}, u32[]{:S(2)}) collective-permute-start(f32[16,256]{1,0:T(8,128)S(1)} %multiply_add_fusion.1), channel_id=1, source_target_pairs={{0,16},{4,20},{8,24},{12,28},{16,0},{20,4},{24,8},{28,12},{1,17},{... | collective-permute-start | bytes 49160 | tf_op jit(solution)/shard_map/ppermute | solution.py:43
  32.1 1.4 %collective-permute-start.9 = (f32[16,256]{1,0:T(8,128)S(1)}, f32[16,256]{1,0:T(8,128)S(1)}, u32[]{:S(2)}, u32[]{:S(2)}) collective-permute-start(f32[16,256]{1,0:T(8,128)S(1)} %multiply_add_fusion.1), channel_id=1, source_target_pairs={{0,24},{4,28},{8,16},{12,20},{16,8},{20,12},{24,0},{28,4},{1,25},{... | collective-permute-start | bytes 49160 | tf_op jit(solution)/shard_map/ppermute | solution.py:43
  33.5 0.0 collective-permute-done.7
  33.5 1.3 %collective-permute-done.8 = f32[16,256]{1,0:T(8,128)S(1)} collective-permute-done((f32[16,256]{1,0:T(8,128)S(1)}, f32[16,256]{1,0:T(8,128)S(1)}, u32[]{:S(2)}, u32[]{:S(2)}) %collective-permute-start.8) | collective-permute-done | bytes 16416 | tf_op jit(solution)/shard_map/ppermute | solution.py:43
  34.8 1.9 %collective-permute-done.9 = f32[16,256]{1,0:T(8,128)S(1)} collective-permute-done((f32[16,256]{1,0:T(8,128)S(1)}, f32[16,256]{1,0:T(8,128)S(1)}, u32[]{:S(2)}, u32[]{:S(2)}) %collective-permute-start.9) | collective-permute-done | bytes 16416 | tf_op jit(solution)/shard_map/ppermute | solution.py:43
  36.7 2.1 %collective-permute-start.10 = (f32[16,256]{1,0:T(8,128)S(1)}, f32[16,256]{1,0:T(8,128)S(1)}, u32[]{:S(2)}, u32[]{:S(2)}) collective-permute-start(f32[16,256]{1,0:T(8,128)S(1)} %multiply_add_fusion), channel_id=1, source_target_pairs={{0,1},{1,0},{2,3},{3,2},{4,5},{5,4},{6,7},{7,6},{8,9},{9,8},{10,11... | collective-permute-start | bytes 49160 | tf_op jit(solution)/shard_map/ppermute | solution.py:43
  38.8 0.0 collective-permute-start.11
  38.8 2.4 %collective-permute-start.12 = (f32[16,256]{1,0:T(8,128)S(1)}, f32[16,256]{1,0:T(8,128)S(1)}, u32[]{:S(2)}, u32[]{:S(2)}) collective-permute-start(f32[16,256]{1,0:T(8,128)S(1)} %multiply_add_fusion), channel_id=1, source_target_pairs={{0,3},{1,2},{2,1},{3,0},{4,7},{5,6},{6,5},{7,4},{8,11},{9,10},{10,... | collective-permute-start | bytes 49160 | tf_op jit(solution)/shard_map/ppermute | solution.py:43
  41.3 2.2 %collective-permute-done.11 = f32[16,256]{1,0:T(8,128)S(1)} collective-permute-done((f32[16,256]{1,0:T(8,128)S(1)}, f32[16,256]{1,0:T(8,128)S(1)}, u32[]{:S(2)}, u32[]{:S(2)}) %collective-permute-start.11) | collective-permute-done | bytes 16416 | tf_op jit(solution)/shard_map/ppermute | solution.py:43
  43.5 0.9 %collective-permute-done.12 = f32[16,256]{1,0:T(8,128)S(1)} collective-permute-done((f32[16,256]{1,0:T(8,128)S(1)}, f32[16,256]{1,0:T(8,128)S(1)}, u32[]{:S(2)}, u32[]{:S(2)}) %collective-permute-start.12) | collective-permute-done | bytes 16416 | tf_op jit(solution)/shard_map/ppermute | solution.py:43
  44.4 0.8 %copy.10 = f32[256,16]{1,0:T(8,128)} copy(f32[256,16]{0,1:T(8,128)S(1)} %add_bitcast_fusion) | data formatting | bytes 32768
  (13 shorter events, 0.0 us)
Async XLA Ops:
  0.7 1.0 %copy-start = (f32[16,16,256]{2,1,0:T(8,128)S(1)}, f32[16,16,256]{2,1,0:T(8,128)}, u32[]{:S(2)}) copy-start(f32[16,16,256]{2,1,0:T(8,128)} %refs_1_.1) | copy-start | bytes 786436
  1.7 0.9 %copy-start.1 = (f32[16,16,256]{2,1,0:T(8,128)S(1)}, f32[16,16,256]{2,1,0:T(8,128)}, u32[]{:S(2)}) copy-start(f32[16,16,256]{2,1,0:T(8,128)} %refs_2_.1) | copy-start | bytes 786436
  2.6 17.3 %copy-start.2 = (f32[256,256]{1,0:T(8,128)S(1)}, f32[256,256]{1,0:T(8,128)}, u32[]{:S(2)}) copy-start(f32[256,256]{1,0:T(8,128)} %constant.25.clone.refs_11_) | copy-start | bytes 786436
  3.4 16.5 %collective-permute-start = (f32[2,8,16,256]{3,2,1,0:T(8,128)S(1)}, f32[2,8,16,256]{3,2,1,0:T(8,128)S(1)}, u32[]{:S(2)}, u32[]{:S(2)}) collective-permute-start(f32[2,8,16,256]{3,2,1,0:T(8,128)S(1)} %get-tuple-element.10.refs_1_), channel_id=1, source_target_pairs={{4,8},{5,9},{6,10},{7,11},{8,4},{9,5},{10,6},{11,7},{12,16},{13,17... | collective-permute-start | bytes 786440 | tf_op jit(solution)/shard_map/rows_odd/ppermute | solution.py:39
  4.1 15.8 %collective-permute-start.1 = (f32[2,8,16,256]{3,2,1,0:T(8,128)S(1)}, f32[2,8,16,256]{3,2,1,0:T(8,128)S(1)}, u32[]{:S(2)}, u32[]{:S(2)}) collective-permute-start(f32[2,8,16,256]{3,2,1,0:T(8,128)S(1)} %get-tuple-element.11.refs_2_), channel_id=1, source_target_pairs={{0,4},{1,5},{2,6},{3,7},{4,0},{5,1},{6,2},{7,3},{8,12},{9,13},{10,... | collective-permute-start | bytes 786440 | tf_op jit(solution)/shard_map/rows_even/ppermute | solution.py:39
  8.5 5.1 %collective-permute-start.2 = (f32[2,16,128]{2,1,0:T(8,128)S(1)}, f32[2,16,128]{2,1,0:T(8,128)S(1)}, u32[]{:S(2)}, u32[]{:S(2)}) collective-permute-start(f32[2,16,128]{2,1,0:T(8,128)S(1)} %get-tuple-element.12), channel_id=1, source_target_pairs={{1,2},{2,1},{5,6},{6,5},{9,10},{10,9},{13,14},{14,13},{17,18},{18,... | collective-permute-start | bytes 49160 | tf_op jit(solution)/shard_map/strip_odd/ppermute | solution.py:39
  9.1 6.2 %collective-permute-start.3 = (f32[2,16,128]{2,1,0:T(8,128)S(1)}, f32[2,16,128]{2,1,0:T(8,128)S(1)}, u32[]{:S(2)}, u32[]{:S(2)}) collective-permute-start(f32[2,16,128]{2,1,0:T(8,128)S(1)} %get-tuple-element.13), channel_id=1, source_target_pairs={{0,1},{1,0},{2,3},{3,2},{4,5},{5,4},{6,7},{7,6},{8,9},{9,8},{10,11... | collective-permute-start | bytes 49160 | tf_op jit(solution)/shard_map/strip_even/ppermute | solution.py:39
  15.3 4.6 %copy-start.3 = (s32[16,256]{1,0:T(8,128)S(1)}, s32[16,256]{1,0:T(8,128)}, u32[]{:S(2)}) copy-start(s32[16,256]{1,0:T(8,128)} %refs_9_.1) | copy-start | bytes 49156
  15.3 3.7 %copy-start.4 = (s32[16]{0:T(128)S(1)}, s32[16]{0:T(128)}, u32[]{:S(2)}) copy-start(s32[16]{0:T(128)} %param.8) | copy-start | bytes 196
  15.3 3.8 %collective-permute-start.4 = (f32[2,2,16,128]{3,2,1,0:T(8,128)S(1)}, f32[2,2,16,128]{3,2,1,0:T(8,128)S(1)}, u32[]{:S(2)}, u32[]{:S(2)}) collective-permute-start(f32[2,2,16,128]{3,2,1,0:T(8,128)S(1)} %pad_maximum_fusion), channel_id=1, source_target_pairs={{4,8},{5,9},{6,10},{7,11},{8,4},{9,5},{10,6},{11,7},{12,16},{13,17... | collective-permute-start | bytes 98312 | tf_op jit(solution)/shard_map/corner_odd/ppermute | solution.py:39
  16.1 3.8 %collective-permute-start.5 = (f32[2,2,16,128]{3,2,1,0:T(8,128)S(1)}, f32[2,2,16,128]{3,2,1,0:T(8,128)S(1)}, u32[]{:S(2)}, u32[]{:S(2)}) collective-permute-start(f32[2,2,16,128]{3,2,1,0:T(8,128)S(1)} %pad_maximum_fusion), channel_id=1, source_target_pairs={{0,4},{1,5},{2,6},{3,7},{4,0},{5,1},{6,2},{7,3},{8,12},{9,13},{10,... | collective-permute-start | bytes 98312 | tf_op jit(solution)/shard_map/corner_even/ppermute | solution.py:39
  27.6 1.5 %collective-permute-start.6 = (f32[16,256]{1,0:T(8,128)S(1)}, f32[16,256]{1,0:T(8,128)S(1)}, u32[]{:S(2)}, u32[]{:S(2)}) collective-permute-start(f32[16,256]{1,0:T(8,128)S(1)} %get-tuple-element.16), channel_id=1, source_target_pairs={{0,4},{4,0},{8,12},{12,8},{16,20},{20,16},{24,28},{28,24},{1,5},{5... | collective-permute-start | bytes 49160 | tf_op jit(solution)/shard_map/ppermute | solution.py:43
  29.1 4.4 %collective-permute-start.7 = (f32[16,256]{1,0:T(8,128)S(1)}, f32[16,256]{1,0:T(8,128)S(1)}, u32[]{:S(2)}, u32[]{:S(2)}) collective-permute-start(f32[16,256]{1,0:T(8,128)S(1)} %multiply_add_fusion.1), channel_id=1, source_target_pairs={{0,8},{4,12},{8,0},{12,4},{16,24},{20,28},{24,16},{28,20},{1,9},{5... | collective-permute-start | bytes 49160 | tf_op jit(solution)/shard_map/ppermute | solution.py:43
  31.1 3.7 %collective-permute-start.8 = (f32[16,256]{1,0:T(8,128)S(1)}, f32[16,256]{1,0:T(8,128)S(1)}, u32[]{:S(2)}, u32[]{:S(2)}) collective-permute-start(f32[16,256]{1,0:T(8,128)S(1)} %multiply_add_fusion.1), channel_id=1, source_target_pairs={{0,16},{4,20},{8,24},{12,28},{16,0},{20,4},{24,8},{28,12},{1,17},{... | collective-permute-start | bytes 49160 | tf_op jit(solution)/shard_map/ppermute | solution.py:43
  32.1 4.6 %collective-permute-start.9 = (f32[16,256]{1,0:T(8,128)S(1)}, f32[16,256]{1,0:T(8,128)S(1)}, u32[]{:S(2)}, u32[]{:S(2)}) collective-permute-start(f32[16,256]{1,0:T(8,128)S(1)} %multiply_add_fusion.1), channel_id=1, source_target_pairs={{0,24},{4,28},{8,16},{12,20},{16,8},{20,12},{24,0},{28,4},{1,25},{... | collective-permute-start | bytes 49160 | tf_op jit(solution)/shard_map/ppermute | solution.py:43
  36.7 4.5 %collective-permute-start.10 = (f32[16,256]{1,0:T(8,128)S(1)}, f32[16,256]{1,0:T(8,128)S(1)}, u32[]{:S(2)}, u32[]{:S(2)}) collective-permute-start(f32[16,256]{1,0:T(8,128)S(1)} %multiply_add_fusion), channel_id=1, source_target_pairs={{0,1},{1,0},{2,3},{3,2},{4,5},{5,4},{6,7},{7,6},{8,9},{9,8},{10,11... | collective-permute-start | bytes 49160 | tf_op jit(solution)/shard_map/ppermute | solution.py:43
  38.8 4.6 %collective-permute-start.11 = (f32[16,256]{1,0:T(8,128)S(1)}, f32[16,256]{1,0:T(8,128)S(1)}, u32[]{:S(2)}, u32[]{:S(2)}) collective-permute-start(f32[16,256]{1,0:T(8,128)S(1)} %multiply_add_fusion), channel_id=1, source_target_pairs={{0,2},{1,3},{2,0},{3,1},{4,6},{5,7},{6,4},{7,5},{8,10},{9,11},{10,... | collective-permute-start | bytes 49160 | tf_op jit(solution)/shard_map/ppermute | solution.py:43
  38.8 5.5 %collective-permute-start.12 = (f32[16,256]{1,0:T(8,128)S(1)}, f32[16,256]{1,0:T(8,128)S(1)}, u32[]{:S(2)}, u32[]{:S(2)}) collective-permute-start(f32[16,256]{1,0:T(8,128)S(1)} %multiply_add_fusion), channel_id=1, source_target_pairs={{0,3},{1,2},{2,1},{3,0},{4,7},{5,6},{6,5},{7,4},{8,11},{9,10},{10,... | collective-permute-start | bytes 49160 | tf_op jit(solution)/shard_map/ppermute | solution.py:43

commit v4 on v3

v4 whole, which is shorter than its diff:
```python
import jax
import jax.numpy as jnp
import numpy as np
from jax import lax
from jax.experimental import pallas as pl
from jax.experimental.pallas import tpu as pltpu
from jax.sharding import PartitionSpec as P


SWEEPS = 8
reaction = 0.5
lowest = 0.5
highest = 62.0
HALO = SWEEPS
LANES = 128
AXES = ("gx", "gy")


def even_pair(i, n):
    return i ^ 1


def odd_pair(i, n):
    j = ((i + 1) ^ 1) - 1
    return j if 0 <= j < n else None


def same(i, n):
    return i


def exchange(array, row_map, col_map):
    rows, cols = lax.axis_size("gx"), lax.axis_size("gy")
    pairs = []
    for g in range(rows):
        for y in range(cols):
            to_g, to_y = row_map(g, rows), col_map(y, cols)
            if to_g is not None and to_y is not None:
                pairs.append((g * cols + y, to_g * cols + to_y))
    return lax.ppermute(array, AXES, pairs)


def swap(array, axis, mask):
    return lax.ppermute(array, axis, [(i, i ^ mask) for i in range(lax.axis_size(axis))])


def bit_groups(bits):
    return [bits[i : i + 2] for i in range(0, len(bits), 2)]


def masks_of(group):
    masks = [0]
    for bit in group:
        masks = masks + [m | 1 << bit for m in masks]
    return masks


def walsh_sign(index, mask, group):
    parity = jnp.int32(0)
    for bit in group:
        parity = parity + (index >> bit & (index ^ mask) >> bit & 1)
    return (1 - 2 * (parity & 1)).astype(jnp.float32)


def hartley_mix(depth, rows, scale):
    angles = (np.outer(np.arange(rows), np.arange(rows)) % rows) * (2.0 * np.pi / rows)
    table = (np.cos(angles) + np.sin(angles)) / np.sqrt(rows) * scale
    slots = np.arange(depth)
    placed = np.eye(depth)[2 * (slots % (depth // 2)) + slots // (depth // 2)]
    return np.einsum("jk,se->ksej", table, placed).reshape(rows * depth, depth * rows).astype(np.float32)


def turn(tiles):
    count = len(tiles)
    sub = lax.broadcasted_iota(jnp.int32, tiles[0].shape, 0)
    tiles = list(tiles)
    step = 1
    while step < count:
        low = (sub & step) == 0
        for i in range(count):
            if not i & step:
                a, b = tiles[i], tiles[i + step]
                tiles[i] = jnp.where(low, a, pltpu.roll(b, step, 0))
                tiles[i + step] = jnp.where(low, pltpu.roll(a, count - step, 0), b)
        step *= 2
    return tiles


def back(x, axis):
    return pltpu.roll(x, 1, axis)


def ahead(x, axis):
    return pltpu.roll(x, x.shape[axis] - 1, axis)


def flag(mask):
    return jnp.where(mask, 1.0, 0.0)


def move(x, shift):
    return pltpu.roll(x, shift % LANES, 1) if shift % LANES else x


def pack_kernel(flags, basis, cond, to_odd, to_even, left, right, held, sems, *, depth, rows, cols):
    odd, col_odd = flags[0] == 1, flags[1] == 1
    half = depth // 2
    lane = lax.broadcasted_iota(jnp.int32, (half, LANES), 1)
    tiles = cols // LANES

    def load(a, c):
        source = (basis, cond)[a].at[:, :, pl.ds(c * LANES, LANES)]
        return pltpu.make_async_copy(source, held.at[a, c], sems.at[a, c])

    for a in range(2):
        for c in range(tiles):
            load(a, c).start()
    for a in range(2):
        lo = [jnp.zeros((half, LANES), jnp.float32)] * 2
        hi = [jnp.zeros((half, LANES), jnp.float32)] * 2
        for c in range(tiles):
            load(a, c).wait()
            span = slice(c * LANES, (c + 1) * LANES)
            for t in range(2):
                part = slice(t * half, (t + 1) * half)
                slabs = []
                for r in range(0, rows, half):
                    slabs += turn([held[a, c, 2 * s + t, r : r + half, :] for s in range(half)])
                slabs = [jnp.where(odd, slabs[rows - 1 - i], slabs[i]) for i in range(rows)]
                for i in range(HALO):
                    to_odd[a * HALO + i, part, span] = slabs[i]
                    to_even[a * HALO + i, part, span] = slabs[rows - HALO + i]
                for i in range(rows):
                    mine = (lane >= i * HALO) & (lane < (i + 1) * HALO)
                    if c == 0:
                        lo[t] = jnp.where(mine, move(slabs[i], i * HALO), lo[t])
                    if c == tiles - 1:
                        hi[t] = jnp.where(mine, move(slabs[i], (i + 1) * HALO), hi[t])
        for t in range(2):
            part = slice(t * half, (t + 1) * half)
            left[a, part] = jnp.where(col_odd, hi[t], lo[t])
            right[a, part] = jnp.where(col_odd, lo[t], hi[t])
    for target in (to_odd, to_even):
        target[2 * HALO] = jnp.zeros((depth, cols), jnp.float32)


def corner_kernel(to_odd, to_even, strip_odd, strip_even, odd_out, even_out, *, depth):
    lane = lax.broadcasted_iota(jnp.int32, (depth, LANES), 1)
    first = lane < LANES // 2
    for a in range(2):
        span = slice(a * LANES, (a + 1) * LANES)
        even, odd = strip_even[a], strip_odd[a]
        odd_out[2 * HALO, :, span] = jnp.where(first, even, move(odd, LANES // 2))
        even_out[2 * HALO, :, span] = jnp.where(first, move(even, LANES // 2), odd)


class Field:
    def __init__(self):
        self.where = {}

    def put(self, first, ref, count):
        for i in range(count):
            self.where[first + i] = (ref, i)

    def get(self, j, part):
        ref, i = self.where[j]
        return ref[i, part]

    def set(self, j, part, value):
        ref, i = self.where[j]
        ref[i, part] = value


class Shape:
    def __init__(self, flags, depth, rows, cols):
        self.depth, self.rows, self.cols = depth, rows, cols
        self.half, self.width, self.span = depth // 2, cols + LANES, rows + 2 * HALO
        self.parts = (slice(0, self.half), slice(self.half, depth))
        self.odd, self.col_odd = flags[0] == 1, flags[1] == 1
        self.edge, self.left, self.right = (flags[i].astype(jnp.float32) for i in range(2, 5))
        self.lane = lax.broadcasted_iota(jnp.int32, (self.half, LANES), 1)
        deep = lax.broadcasted_iota(jnp.int32, (self.half, self.width), 0)
        wide = lax.broadcasted_iota(jnp.int32, (self.half, self.width), 1)
        sides = self.left * flag(wide == 0) + self.right * flag(wide == cols - 1)
        self.ends = [sides + flag(deep == 0), sides + flag(deep == self.half - 1)]
        self.x_inner = 1.0 - self.right * flag(wide == cols - 1) - self.left * flag(wide == self.width - 1)
        self.z_inner = flag(deep < self.half - 1)

    def ordered(self, odd, even):
        return jnp.where(self.col_odd, even, odd), jnp.where(self.col_odd, odd, even)

    def side(self, lo, hi, at):
        hi, lo = move(hi, -at * HALO), move(lo, -HALO - at * HALO)
        return jnp.where(self.lane < HALO, hi, jnp.where(self.lane >= LANES - HALO, lo, 0.0))

    def corner(self, message, a, t):
        both = message[2 * HALO, self.parts[t], a * LANES : (a + 1) * LANES]
        return self.ordered(move(both, LANES // 2), both)

    def slab(self, message, a, i, strips, at):
        return [
            jnp.concatenate([message[a * HALO + i, self.parts[t]], self.side(*strips[t], at)], axis=1)
            for t in range(2)
        ]

    def coefficients(self, j, halves, f, own_edge):
        f["kz"].set(j, self.parts[0], halves[0] + halves[1])
        f["kz"].set(j, self.parts[1], (halves[1] + ahead(halves[0], 0)) * self.z_inner)
        for t in range(2):
            f["kx"].set(j, self.parts[t], (halves[t] + ahead(halves[t], 1)) * self.x_inner)
            ends = self.ends[t] + self.edge if own_edge else self.ends[t]
            f["diag"].set(j, self.parts[t], reaction + halves[t] * ends)


def steps():
    middle = (highest + lowest) / 2.0
    spread = (highest - lowest) / 2.0
    sig_ratio = middle / spread
    rho_now = 1.0 / sig_ratio
    for step in range(1, SWEEPS):
        rho_next = 1.0 / (2.0 * sig_ratio - rho_now)
        yield step, rho_next * rho_now, 2.0 * rho_next / spread
        rho_now = rho_next


def apply_rows(sh, f, across, low, high, flux_low, flux_high, emit):
    parts = sh.parts
    for j in range(low, high):
        for t in range(2):
            here = f["dirn"].get(j, parts[t])
            across[j - low, parts[t]] = f["kx"].get(j, parts[t]) * (here - ahead(here, 1))
    here = [f["dirn"].get(low, p) for p in parts]
    flux_y = [f["ky"].get(low - 1, parts[t]) * (f["dirn"].get(low - 1, parts[t]) - here[t]) for t in range(2)]
    if flux_low is not None:
        for t in range(2):
            flux_low(t, flux_y[t])
    for j in range(low, high):
        if j == high - 1 and flux_high is not None:
            nxt, flux = None, [flux_high(t) for t in range(2)]
        else:
            nxt = [f["dirn"].get(j + 1, p) for p in parts]
            flux = [f["ky"].get(j, parts[t]) * (here[t] - nxt[t]) for t in range(2)]
        flux_z0 = f["kz"].get(j, parts[0]) * (here[0] - here[1])
        flux_z1 = f["kz"].get(j, parts[1]) * (here[1] - ahead(here[0], 0))
        along_z = (flux_z0 - back(flux_z1, 0), flux_z1 - flux_z0)
        for t in range(2):
            flux_x = across[j - low, parts[t]]
            applied = (f["diag"].get(j, parts[t]) * here[t] + (flux[t] - flux_y[t])) + along_z[t]
            emit(j, t, here[t], applied + (flux_x - back(flux_x, 1)))
        here, flux_y = nxt, flux


def near_kernel(flags, own_odd, own_even, rows_even, strip_odd, strip_even,
                dirn_a, res_a, pre_a, kx_a, ky_a, kz_a, diag_a, saved, edge_half, image_b, pre_b,
                dirn_b, res_b, kx_b, ky_b, kz_b, diag_b, across, *, depth, rows, cols):
    sh = Shape(flags, depth, rows, cols)
    parts = sh.parts
    mid = 2 * HALO
    f = {name: Field() for name in ("dirn", "res", "pre", "kx", "ky", "kz", "diag")}
    lows = dict(dirn=dirn_a, res=res_a, pre=pre_a, kx=kx_a, ky=ky_a, kz=kz_a, diag=diag_a)
    highs = dict(dirn=dirn_b, res=res_b, pre=pre_b, kx=kx_b, ky=ky_b, kz=kz_b, diag=diag_b)
    for name, field in f.items():
        field.put(HALO, lows[name], HALO)
    for name, ref in highs.items():
        f[name].put(mid, ref, sh.span - mid)
    f["pre"].put(mid, pre_b, HALO + rows - mid)

    def slabs_of(a):
        own = [sh.ordered(strip_odd[a, p], strip_even[a, p]) for p in parts]
        far = [sh.corner(rows_even, a, t) for t in range(2)]
        for i in range(rows):
            message = own_odd if i < HALO else own_even
            yield HALO + i, sh.slab(message, a, i % HALO if i < HALO else i - (rows - HALO), own, i)
        for k in range(HALO):
            yield HALO + rows + k, sh.slab(rows_even, a, HALO - 1 - k, far, HALO - 1 - k)

    middle = (highest + lowest) / 2.0
    for j, slab in slabs_of(0):
        for t in range(2):
            first = slab[t] * (1.0 / middle)
            f["res"].set(j, parts[t], slab[t])
            f["dirn"].set(j, parts[t], first)
            if j < HALO + rows:
                f["pre"].set(j, parts[t], first[:, :cols])
    last = None
    for j, slab in slabs_of(1):
        halves = [0.5 * v for v in slab]
        if last is not None:
            for t in range(2):
                f["ky"].set(j - 1, parts[t], last[t] + halves[t])
        else:
            for t in range(2):
                edge_half[parts[t]] = halves[t]
        if j < sh.span - 1:
            sh.coefficients(j, halves, f, j == HALO)
        last = halves

    for step, keep, gain in steps():

        def emit(j, t, here, applied):
            left_over = f["res"].get(j, parts[t]) - applied
            f["res"].set(j, parts[t], left_over)
            fresh = keep * here + gain * left_over
            f["dirn"].set(j, parts[t], fresh)
            if j < HALO + rows:
                f["pre"].set(j, parts[t], f["pre"].get(j, parts[t]) + fresh[:, :cols])

        def save(t, flux, step=step):
            saved[step - 1, parts[t]] = flux

        apply_rows(sh, f, across, HALO + step, sh.span - step, save, None, emit)

    def finish(j, t, here, applied):
        start = own_even[j - mid, parts[t]]
        image_b[j - mid, parts[t]] = start - (f["res"].get(j, parts[t])[:, :cols] - applied[:, :cols])

    def save_last(t, flux):
        saved[SWEEPS - 1, parts[t]] = flux

    apply_rows(sh, f, across, HALO + SWEEPS, HALO + rows, save_last, None, finish)


def split(x):
    high = x.astype(jnp.bfloat16)
    return high, (x - high.astype(jnp.float32)).astype(jnp.bfloat16)


def far_kernel(flags, rows_odd, own_odd, dirn_a, res_a, pre_a, kx_a, ky_a, kz_a, diag_a, saved, edge_half, image_b, pre_b,
               signs, picks, mix, image, pre, sketch_out,
               dirn, res, kx, ky, kz, diag, across, flip_high, flip_low, *, depth, rows, cols, samples):
    sh = Shape(flags, depth, rows, cols)
    parts = sh.parts
    f = {name: Field() for name in ("dirn", "res", "pre", "kx", "ky", "kz", "diag")}
    mine = dict(dirn=dirn, res=res, kx=kx, ky=ky, kz=kz, diag=diag)
    given = dict(dirn=dirn_a, res=res_a, pre=pre_a, kx=kx_a, ky=ky_a, kz=kz_a, diag=diag_a)
    for name, field in f.items():
        if name in mine:
            field.put(0, mine[name], HALO)
        field.put(HALO, given[name], HALO)
    middle = (highest + lowest) / 2.0
    corners = [[sh.corner(rows_odd, a, t) for t in range(2)] for a in range(2)]
    last = None
    for k in reversed(range(HALO)):
        j = HALO - 1 - k
        slab = sh.slab(rows_odd, 0, k, corners[0], k)
        for t in range(2):
            f["res"].set(j, parts[t], slab[t])
            f["dirn"].set(j, parts[t], slab[t] * (1.0 / middle))
        halves = [0.5 * v for v in sh.slab(rows_odd, 1, k, corners[1], k)]
        if last is not None:
            for t in range(2):
                f["ky"].set(j - 1, parts[t], last[t] + halves[t])
        if j > 0:
            sh.coefficients(j, halves, f, False)
        last = halves
    for t in range(2):
        f["ky"].set(HALO - 1, parts[t], (last[t] + edge_half[parts[t]]) * (1.0 - sh.edge))

    def hand_over(j, t):
        if j >= HALO and t == 1:
            f["dirn"].where[j] = (dirn, j)
            f["res"].where[j] = (res, j)
            f["pre"].where[j] = (pre, j - HALO)

    for step, keep, gain in steps():

        def emit(j, t, here, applied):
            left_over = f["res"].get(j, parts[t]) - applied
            fresh = keep * here + gain * left_over
            at = parts[t]
            res[j, at] = left_over
            dirn[j, at] = fresh
            if j >= HALO:
                pre[j - HALO, at] = f["pre"].get(j, at) + fresh[:, :cols]
            hand_over(j, t)

        apply_rows(sh, f, across, step, HALO + step, None, lambda t, step=step: saved[step - 1, parts[t]], emit)

    def finish(j, t, here, applied):
        start = own_odd[j - HALO, parts[t]]
        image[j - HALO, parts[t]] = start - (f["res"].get(j, parts[t])[:, :cols] - applied[:, :cols])

    apply_rows(sh, f, across, HALO, 2 * HALO, None, lambda t: saved[SWEEPS - 1, parts[t]], finish)
    for i in range(rows):
        if i >= HALO:
            image[i] = image_b[i - HALO]
            pre[i] = pre_b[i - HALO]
        elif f["pre"].where[HALO + i][0] is not pre:
            pre[i] = pre_a[i]
    for r in range(rows):
        flipped = image[r + flags[0] * (rows - 1 - 2 * r)] * signs[r : r + 1, :].astype(jnp.float32)
        at = slice(r * depth, (r + 1) * depth)
        flip_high[at], flip_low[at] = split(flipped)

    def dot(a, b, dims):
        return lax.dot_general(a, b, (dims, ((), ())), preferred_element_type=jnp.float32)

    col_ids = lax.broadcasted_iota(jnp.int32, (samples, cols), 1)
    chosen = (picks[...] == col_ids).astype(jnp.float32).astype(jnp.bfloat16)
    picked = dot(chosen, flip_high[...], ((1,), (1,))) + dot(chosen, flip_low[...], ((1,), (1,)))
    high, low = split(picked)
    rest = dot(high, mix[1], ((1,), (0,))) + dot(low, mix[0], ((1,), (0,)))
    sketch_out[...] = dot(high, mix[0], ((1,), (0,))) + rest


def tail_kernel(flags, pre, image, precond_out, image_out, *, depth, rows, cols):
    half = depth // 2
    for c in range(cols // LANES):
        span = slice(c * LANES, (c + 1) * LANES)
        for r in range(0, rows, half):
            for t in range(2):
                part = slice(t * half, (t + 1) * half)
                for source, target in ((pre, precond_out), (image, image_out)):
                    found = [source[r + i + flags[0] * (rows - 1 - 2 * (r + i)), part, span] for i in range(half)]
                    for s, tile in enumerate(turn(found)):
                        target[2 * s + t, r : r + half, span] = tile


def whole_step(basis_vec, conductivity, sign_vals, sample_cols):
    depth, rows, cols = basis_vec.shape
    samples = sample_cols.shape[0]
    assert depth == 16 and rows == 2 * HALO and cols == 2 * LANES
    gx_size, gy_size = lax.axis_size("gx"), lax.axis_size("gy")
    gx_index, gy_index = lax.axis_index("gx"), lax.axis_index("gy")
    flags = jnp.stack([
        gx_index & 1, gy_index & 1, (gx_index == 0) | (gx_index == gx_size - 1), gy_index == 0, gy_index == gy_size - 1,
    ]).astype(jnp.int32)
    smem, vmem = pl.BlockSpec(memory_space=pltpu.SMEM), pl.BlockSpec(memory_space=pltpu.VMEM)
    f32 = jnp.float32
    sizes = dict(depth=depth, rows=rows, cols=cols)
    width, span, mid = cols + LANES, rows + 2 * HALO, 2 * HALO
    wide = lambda n: jax.ShapeDtypeStruct((n, depth, width), f32)
    slim = lambda n: jax.ShapeDtypeStruct((n, depth, cols), f32)
    wide_scratch = lambda n: pltpu.VMEM((n, depth, width), f32)
    small = lambda mib: pltpu.CompilerParams(vmem_limit_bytes=mib << 20)
    message = slim(2 * HALO + 1)
    strip = jax.ShapeDtypeStruct((2, depth, LANES), f32)
    own_odd, own_even, strip_to_odd, strip_to_even = pl.pallas_call(
        lambda *refs: pack_kernel(*refs, **sizes),
        in_specs=[smem] + [pl.BlockSpec(memory_space=pl.ANY)] * 2,
        out_specs=[vmem] * 4,
        out_shape=[message, message, strip, strip],
        scratch_shapes=[
            pltpu.VMEM((2, cols // LANES, depth, rows, LANES), f32),
            pltpu.SemaphoreType.DMA((2, cols // LANES)),
        ],
        compiler_params=small(4),
        name="pack",
    )(flags, basis_vec, conductivity)
    strip_even = exchange(strip_to_even, same, even_pair)
    strip_odd = exchange(strip_to_odd, same, odd_pair)
    own_odd, own_even = pl.pallas_call(
        lambda *refs: corner_kernel(*refs, depth=depth),
        in_specs=[vmem] * 4,
        out_specs=[vmem] * 2,
        out_shape=[message, message],
        input_output_aliases={0: 0, 1: 1},
        compiler_params=small(4),
        name="corners",
    )(own_odd, own_even, strip_odd, strip_even)
    rows_odd = exchange(own_odd, odd_pair, same)
    rows_even = exchange(own_even, even_pair, same)
    *handed, image_b, pre_b = pl.pallas_call(
        lambda *refs: near_kernel(*refs, **sizes),
        in_specs=[smem] + [vmem] * 5,
        out_specs=[vmem] * 11,
        out_shape=[wide(HALO), wide(HALO), slim(HALO), wide(HALO), wide(HALO), wide(HALO), wide(HALO), wide(SWEEPS),
                   jax.ShapeDtypeStruct((depth, width), f32), slim(rows - HALO), slim(rows - HALO)],
        scratch_shapes=[wide_scratch(span - mid)] * 6 + [wide_scratch(span - HALO)],
        compiler_params=small(16),
        name="near",
    )(flags, own_odd, own_even, rows_even, strip_odd, strip_even)
    mix = hartley_mix(depth, rows, 1.0 / np.sqrt(gx_size))
    mix_high = mix.astype(jnp.bfloat16)
    mix = jnp.asarray(np.stack([mix_high, (mix - mix_high.astype(np.float32)).astype(jnp.bfloat16)]))
    image, pre, current = pl.pallas_call(
        lambda *refs: far_kernel(*refs, samples=samples, **sizes),
        in_specs=[smem] + [vmem] * 16,
        out_specs=[vmem] * 3,
        out_shape=[slim(rows), slim(rows), jax.ShapeDtypeStruct((samples, depth * rows), f32)],
        scratch_shapes=[wide_scratch(mid)] * 2 + [wide_scratch(HALO)] * 5
        + [pltpu.VMEM((depth * rows, cols), jnp.bfloat16)] * 2,
        compiler_params=small(16),
        name="far",
    )(flags, rows_odd, own_odd, *handed, image_b, pre_b, sign_vals, sample_cols.reshape(samples, 1), mix)
    precond_out, image_out = pl.pallas_call(
        lambda *refs: tail_kernel(*refs, **sizes),
        in_specs=[smem] + [vmem] * 2,
        out_specs=[vmem] * 2,
        out_shape=[jax.ShapeDtypeStruct((depth, rows, cols), f32)] * 2,
        compiler_params=small(8),
        name="tail",
    )(flags, pre, image)
    gx_bits = gx_size.bit_length() - 1
    for group in [[0]] + bit_groups(list(range(1, gx_bits))):
        total = walsh_sign(gx_index, 0, group) * current
        for mask in masks_of(group)[1:]:
            total = total + walsh_sign(gx_index, mask, group) * swap(current, "gx", mask)
        current = total
    for group in bit_groups(list(range(gy_size.bit_length() - 1))):
        current = current + sum(swap(current, "gy", mask) for mask in masks_of(group)[1:])
    return precond_out, image_out, current.T.reshape(depth, rows, samples)


def solution(mesh):
    in_specs = (P(None, "gx", "gy"), P(None, "gx", "gy"), P("gx", "gy"), P("gy"))
    out_specs = (P(None, "gx", "gy"), P(None, "gx", "gy"), P(None, "gx", None))
    return jax.shard_map(whole_step, mesh=mesh, in_specs=in_specs, out_specs=out_specs, check_vma=False)
```

time: 45.4 us -> 42 us (0.925)
  starting transfers between devices: 23.4 us -> 19.5 us
  waiting for transfers between devices: 9.68 us -> 7.84 us
  Pallas kernels: 8.44 us -> 10.1 us
  local copies, waits for them, and re-layouts: 2.84 us -> 3.53 us
    ppermute x6 -> x4, starting transfers between devices: 13.9 us -> 7.32 us  [exchange(): return lax.ppermute(array, AXES, pairs)]
    ppermute x7, starting transfers between devices: 9.55 us -> 12.2 us  [swap(): lax.ppermute(array, axis, [(i, i ^ mask) for i in range(lax.axis_size(axi...]
    ppermute x7, waiting for transfers between devices: 7.18 us -> 5.37 us  [swap(): lax.ppermute(array, axis, [(i, i ^ mask) for i in range(lax.axis_size(axi...]
    pallas_call x2 -> x5, Pallas kernels: 8.44 us -> 10.1 us  [the longest x1 4.94 us: whole_step(): pl.pallas_call(lambda *refs: near_kernel(*refs, **sizes), in_specs=[smem]...]
    unnamed x11, local copies, waits for them, and re-layouts: 2.67 us -> 3.36 us
    ppermute x6 -> x4, waiting for transfers between devices: 2.5 us -> 2.47 us  [exchange(): return lax.ppermute(array, AXES, pairs)]
  transfers between devices with their start and end apart: 13 -> 11, of which waited for: 7 -> 7; matrix products, arithmetic and copies ran while one was open for 0% -> 0% of each run, Pallas kernels for 0% -> 15%
where the time goes in v4:
time: 42 us; the launch traced here: 41.8 us
  starting transfers between devices  19.5 us (46%)
  Pallas kernels  10.1 us (24%)
  waiting for transfers between devices  7.84 us (19%)
  local copies, waits for them, and re-layouts  3.53 us (8%)
  between operations  0.74 us (2%)
    ppermute x7, starting transfers between devices, swap(): lax.ppermute(array, axis, [(i, i ^ mask) for i in range(lax.axis_size(axi...  12.2 us
    ppermute x4, starting transfers between devices, exchange(): return lax.ppermute(array, AXES, pairs)  7.32 us
    ppermute x7, waiting for transfers between devices, swap(): lax.ppermute(array, axis, [(i, i ^ mask) for i in range(lax.axis_size(axi...  5.37 us
    pallas_call x1, Pallas kernels, whole_step(): pl.pallas_call(lambda *refs: near_kernel(*refs, **sizes), in_specs=[smem]...  4.94 us
    unnamed x11, local copies, waits for them, and re-layouts  3.36 us
    pallas_call x1, Pallas kernels, whole_step(): pl.pallas_call(lambda *refs: far_kernel(*refs, samples=samples, **sizes),...  2.6 us
    ppermute x4, waiting for transfers between devices, exchange(): return lax.ppermute(array, AXES, pairs)  2.47 us
    pallas_call x1, Pallas kernels, whole_step(): pl.pallas_call(lambda *refs: tail_kernel(*refs, **sizes), in_specs=[smem]...  1.44 us
  transfers between devices with their start and end apart: 11, of which 7 were waited for; matrix products, arithmetic and copies ran while one was open for 0% of the time, Pallas kernels for 15%

profile of v4, /device:TPU:0, one launch (start us, length us, event | category | flops | bytes accessed | tf_op | source)
XLA Modules:
  0.0 41.8 jit_solution(8566683008450998298)
XLA Ops:
  0.6 0.1 stack.35.refs_0_
  0.7 0.9 %copy-done.1 = f32[16,16,256]{2,1,0:T(8,128)S(1)} copy-done((f32[16,16,256]{2,1,0:T(8,128)S(1)}, f32[16,16,256]{2,1,0:T(8,128)}, u32[]{:S(2)}) %copy-start.1) | copy-done | bytes 262168
  1.7 0.9 %copy-done.2 = f32[16,16,256]{2,1,0:T(8,128)S(1)} copy-done((f32[16,16,256]{2,1,0:T(8,128)S(1)}, f32[16,16,256]{2,1,0:T(8,128)}, u32[]{:S(2)}) %copy-start.2) | copy-done | bytes 262168
  2.6 1.1 %pack.1 = (f32[17,16,256]{2,1,0:T(8,128)S(1)}, f32[17,16,256]{2,1,0:T(8,128)S(1)}, f32[2,16,128]{2,1,0:T(8,128)S(1)}, f32[2,16,128]{2,1,0:T(8,128)S(1)}) custom-call(s32[5]{0:T(128)S(1)} %stack.35.refs_0_, f32[16,16,256]{2,1,0:T(8,128)S(1)} %copy-done.1, f32[16,16,256]{2,1,0:T(8,128)S(1)} %copy-done.2), custom_call_target="tpu_custom_call" | custom-call | tf_op jit(solution)/shard_map/pack/pallas_call | solution.py:438
  3.7 0.7 %collective-permute-start = (f32[2,16,128]{2,1,0:T(8,128)S(1)}, f32[2,16,128]{2,1,0:T(8,128)S(1)}, u32[]{:S(2)}, u32[]{:S(2)}) collective-permute-start(f32[2,16,128]{2,1,0:T(8,128)S(1)} %get-tuple-element.27), channel_id=1, source_target_pairs={{1,2},{2,1},{5,6},{6,5},{9,10},{10,9},{13,14},{14,13},{17,18},{18,... | collective-permute-start | bytes 49160 | tf_op jit(solution)/shard_map/ppermute | solution.py:40
  4.4 5.9 %collective-permute-start.1 = (f32[2,16,128]{2,1,0:T(8,128)S(1)}, f32[2,16,128]{2,1,0:T(8,128)S(1)}, u32[]{:S(2)}, u32[]{:S(2)}) collective-permute-start(f32[2,16,128]{2,1,0:T(8,128)S(1)} %get-tuple-element.28), channel_id=1, source_target_pairs={{0,1},{1,0},{2,3},{3,2},{4,5},{5,4},{6,7},{7,6},{8,9},{9,8},{10,11... | collective-permute-start | bytes 49160 | tf_op jit(solution)/shard_map/ppermute | solution.py:40
  10.4 1.7 %collective-permute-done.1.refs_3_.refs_5_ = f32[2,16,128]{2,1,0:T(8,128)S(1)} collective-permute-done((f32[2,16,128]{2,1,0:T(8,128)S(1)}, f32[2,16,128]{2,1,0:T(8,128)S(1)}, u32[]{:S(2)}, u32[]{:S(2)}) %collective-permute-start.1) | collective-permute-done | bytes 16416 | tf_op jit(solution)/shard_map/ppermute | solution.py:40
  12.1 0.1 corners.1
  12.1 0.0 collective-permute-start.3
  12.2 0.0 copy-start.4
  12.2 0.7 %collective-permute-start.2 = (f32[17,16,256]{2,1,0:T(8,128)S(1)}, f32[17,16,256]{2,1,0:T(8,128)S(1)}, u32[]{:S(2)}, u32[]{:S(2)}) collective-permute-start(f32[17,16,256]{2,1,0:T(8,128)S(1)} %get-tuple-element.29.refs_1_.refs_2_), channel_id=1, source_target_pairs={{4,8},{5,9},{6,10},{7,11},{8,4},{9,5},{10,6},{11,7},{12,16},{13,17... | collective-permute-start | bytes 835592 | tf_op jit(solution)/shard_map/ppermute | solution.py:40
  12.9 0.1 copy.10.refs_15_
  13.0 0.8 %collective-permute-done.3.refs_3_ = f32[17,16,256]{2,1,0:T(8,128)S(1)} collective-permute-done((f32[17,16,256]{2,1,0:T(8,128)S(1)}, f32[17,16,256]{2,1,0:T(8,128)S(1)}, u32[]{:S(2)}, u32[]{:S(2)}) %collective-permute-start.3) | collective-permute-done | bytes 278560 | tf_op jit(solution)/shard_map/ppermute | solution.py:40
  13.7 4.9 %near.1 = (f32[8,16,384]{2,1,0:T(8,128)S(1)}, f32[8,16,384]{2,1,0:T(8,128)S(1)}, f32[8,16,256]{2,1,0:T(8,128)S(1)}, f32[8,16,384]{2,1,0:T(8,128)S(1)}, f32[8,16,...) custom-call(s32[5]{0:T(128)S(1)} %stack.35.refs_0_, ...), custom_call_target="tpu_custom_call" | custom-call | tf_op jit(solution)/shard_map/near/pallas_call | solution.py:463
  18.7 0.0 copy-start.3
  18.7 0.7 %copy-done.3 = s32[16,256]{1,0:T(8,128)S(1)} copy-done((s32[16,256]{1,0:T(8,128)S(1)}, s32[16,256]{1,0:T(8,128)}, u32[]{:S(2)}) %copy-start.3) | copy-done | bytes 16408
  19.4 2.6 %far.1 = (f32[16,16,256]{2,1,0:T(8,128)S(1)}, f32[16,16,256]{2,1,0:T(8,128)S(1)}, f32[16,256]{1,0:T(8,128)S(1)}) custom-call(s32[5]{0:T(128)S(1)} %stack.35.refs_0_, f32[17,16,256]{2,1,0:T(8,128)S(1)} %collective-permute-done.2.refs_1_, f32[17,16,256]{2,1,0:T(8,128)S(1)} %get-tuple-element.29.refs_1_.refs_2_, f32[8,16,384]{2,1,0:T(8,128)S(1)} %get-tuple-element.31.refs_3_, ...), custom_call_target="tpu_custom_call" | custom-call | tf_op jit(solution)/shard_map/far/pallas_call | solution.py:476
  22.0 4.1 %collective-permute-start.4 = (f32[16,256]{1,0:T(8,128)S(1)}, f32[16,256]{1,0:T(8,128)S(1)}, u32[]{:S(2)}, u32[]{:S(2)}) collective-permute-start(f32[16,256]{1,0:T(8,128)S(1)} %get-tuple-element.46), channel_id=1, source_target_pairs={{0,4},{4,0},{8,12},{12,8},{16,20},{20,16},{24,28},{28,24},{1,5},{5... | collective-permute-start | bytes 49160 | tf_op jit(solution)/shard_map/ppermute | solution.py:44
  26.1 0.8 %collective-permute-done.4 = f32[16,256]{1,0:T(8,128)S(1)} collective-permute-done((f32[16,256]{1,0:T(8,128)S(1)}, f32[16,256]{1,0:T(8,128)S(1)}, u32[]{:S(2)}, u32[]{:S(2)}) %collective-permute-start.4) | collective-permute-done | bytes 16416 | tf_op jit(solution)/shard_map/ppermute | solution.py:44
  27.0 1.8 %collective-permute-start.5 = (f32[16,256]{1,0:T(8,128)S(1)}, f32[16,256]{1,0:T(8,128)S(1)}, u32[]{:S(2)}, u32[]{:S(2)}) collective-permute-start(f32[16,256]{1,0:T(8,128)S(1)} %multiply_add_fusion.1), channel_id=1, source_target_pairs={{0,8},{4,12},{8,0},{12,4},{16,24},{20,28},{24,16},{28,20},{1,9},{5... | collective-permute-start | bytes 49160 | tf_op jit(solution)/shard_map/ppermute | solution.py:44
  28.8 0.4 collective-permute-start.6
  29.2 1.4 %collective-permute-start.7 = (f32[16,256]{1,0:T(8,128)S(1)}, f32[16,256]{1,0:T(8,128)S(1)}, u32[]{:S(2)}, u32[]{:S(2)}) collective-permute-start(f32[16,256]{1,0:T(8,128)S(1)} %multiply_add_fusion.1), channel_id=1, source_target_pairs={{0,24},{4,28},{8,16},{12,20},{16,8},{20,12},{24,0},{28,4},{1,25},{... | collective-permute-start | bytes 49160 | tf_op jit(solution)/shard_map/ppermute | solution.py:44
  30.6 0.1 collective-permute-done.5
  30.7 1.8 %collective-permute-done.6 = f32[16,256]{1,0:T(8,128)S(1)} collective-permute-done((f32[16,256]{1,0:T(8,128)S(1)}, f32[16,256]{1,0:T(8,128)S(1)}, u32[]{:S(2)}, u32[]{:S(2)}) %collective-permute-start.6) | collective-permute-done | bytes 16416 | tf_op jit(solution)/shard_map/ppermute | solution.py:44
  32.5 1.3 %collective-permute-done.7 = f32[16,256]{1,0:T(8,128)S(1)} collective-permute-done((f32[16,256]{1,0:T(8,128)S(1)}, f32[16,256]{1,0:T(8,128)S(1)}, u32[]{:S(2)}, u32[]{:S(2)}) %collective-permute-start.7) | collective-permute-done | bytes 16416 | tf_op jit(solution)/shard_map/ppermute | solution.py:44
  33.8 1.4 %collective-permute-start.10 = (f32[16,256]{1,0:T(8,128)S(1)}, f32[16,256]{1,0:T(8,128)S(1)}, u32[]{:S(2)}, u32[]{:S(2)}) collective-permute-start(f32[16,256]{1,0:T(8,128)S(1)} %multiply_add_fusion), channel_id=1, source_target_pairs={{0,3},{1,2},{2,1},{3,0},{4,7},{5,6},{6,5},{7,4},{8,11},{9,10},{10,... | collective-permute-start | bytes 49160 | tf_op jit(solution)/shard_map/ppermute | solution.py:44
  35.3 1.1 %collective-permute-start.8 = (f32[16,256]{1,0:T(8,128)S(1)}, f32[16,256]{1,0:T(8,128)S(1)}, u32[]{:S(2)}, u32[]{:S(2)}) collective-permute-start(f32[16,256]{1,0:T(8,128)S(1)} %multiply_add_fusion), channel_id=1, source_target_pairs={{0,1},{1,0},{2,3},{3,2},{4,5},{5,4},{6,7},{7,6},{8,9},{9,8},{10,11... | collective-permute-start | bytes 49160 | tf_op jit(solution)/shard_map/ppermute | solution.py:44
  36.4 1.9 %collective-permute-start.9 = (f32[16,256]{1,0:T(8,128)S(1)}, f32[16,256]{1,0:T(8,128)S(1)}, u32[]{:S(2)}, u32[]{:S(2)}) collective-permute-start(f32[16,256]{1,0:T(8,128)S(1)} %multiply_add_fusion), channel_id=1, source_target_pairs={{0,2},{1,3},{2,0},{3,1},{4,6},{5,7},{6,4},{7,5},{8,10},{9,11},{10,... | collective-permute-start | bytes 49160 | tf_op jit(solution)/shard_map/ppermute | solution.py:44
  38.3 1.4 %tail.1 = (f32[16,16,256]{2,1,0:T(8,128)}, f32[16,16,256]{2,1,0:T(8,128)}) custom-call(s32[5]{0:T(128)S(1)} %stack.35.refs_0_, f32[16,16,256]{2,1,0:T(8,128)S(1)} %get-tuple-element.42.refs_1_, f32[16,16,256]{2,1,0:T(8,128)S(1)} %get-tuple-element.43.refs_2_), custom_call_target="tpu_custom_call" | custom-call | tf_op jit(solution)/shard_map/tail/pallas_call | solution.py:486
  39.7 0.0 collective-permute-done.10
  39.7 1.3 %collective-permute-done.9 = f32[16,256]{1,0:T(8,128)S(1)} collective-permute-done((f32[16,256]{1,0:T(8,128)S(1)}, f32[16,256]{1,0:T(8,128)S(1)}, u32[]{:S(2)}, u32[]{:S(2)}) %collective-permute-start.9) | collective-permute-done | bytes 16416 | tf_op jit(solution)/shard_map/ppermute | solution.py:44
  41.0 0.8 %copy.12 = f32[256,16]{1,0:T(8,128)} copy(f32[256,16]{0,1:T(8,128)S(1)} %add_bitcast_fusion) | data formatting | bytes 32768
  (11 shorter events, 0.0 us)
Async XLA Ops:
  0.7 1.0 %copy-start.1 = (f32[16,16,256]{2,1,0:T(8,128)S(1)}, f32[16,16,256]{2,1,0:T(8,128)}, u32[]{:S(2)}) copy-start(f32[16,16,256]{2,1,0:T(8,128)} %refs_1_.1) | copy-start | bytes 786436
  1.7 0.9 %copy-start.2 = (f32[16,16,256]{2,1,0:T(8,128)S(1)}, f32[16,16,256]{2,1,0:T(8,128)}, u32[]{:S(2)}) copy-start(f32[16,16,256]{2,1,0:T(8,128)} %refs_2_.1) | copy-start | bytes 786436
  3.7 6.6 %collective-permute-start = (f32[2,16,128]{2,1,0:T(8,128)S(1)}, f32[2,16,128]{2,1,0:T(8,128)S(1)}, u32[]{:S(2)}, u32[]{:S(2)}) collective-permute-start(f32[2,16,128]{2,1,0:T(8,128)S(1)} %get-tuple-element.27), channel_id=1, source_target_pairs={{1,2},{2,1},{5,6},{6,5},{9,10},{10,9},{13,14},{14,13},{17,18},{18,... | collective-permute-start | bytes 49160 | tf_op jit(solution)/shard_map/ppermute | solution.py:40
  4.4 7.7 %collective-permute-start.1 = (f32[2,16,128]{2,1,0:T(8,128)S(1)}, f32[2,16,128]{2,1,0:T(8,128)S(1)}, u32[]{:S(2)}, u32[]{:S(2)}) collective-permute-start(f32[2,16,128]{2,1,0:T(8,128)S(1)} %get-tuple-element.28), channel_id=1, source_target_pairs={{0,1},{1,0},{2,3},{3,2},{4,5},{5,4},{6,7},{7,6},{8,9},{9,8},{10,11... | collective-permute-start | bytes 49160 | tf_op jit(solution)/shard_map/ppermute | solution.py:40
  12.1 1.6 %collective-permute-start.3 = (f32[17,16,256]{2,1,0:T(8,128)S(1)}, f32[17,16,256]{2,1,0:T(8,128)S(1)}, u32[]{:S(2)}, u32[]{:S(2)}) collective-permute-start(f32[17,16,256]{2,1,0:T(8,128)S(1)} %get-tuple-element.30.refs_2_), channel_id=1, source_target_pairs={{0,4},{1,5},{2,6},{3,7},{4,0},{5,1},{6,2},{7,3},{8,12},{9,13},{10,... | collective-permute-start | bytes 835592 | tf_op jit(solution)/shard_map/ppermute | solution.py:40
  12.2 0.7 %copy-start.4 = (s32[16]{0:T(128)S(1)}, s32[16]{0:T(128)}, u32[]{:S(2)}) copy-start(s32[16]{0:T(128)} %param.8) | copy-start | bytes 196
  12.2 6.5 %collective-permute-start.2 = (f32[17,16,256]{2,1,0:T(8,128)S(1)}, f32[17,16,256]{2,1,0:T(8,128)S(1)}, u32[]{:S(2)}, u32[]{:S(2)}) collective-permute-start(f32[17,16,256]{2,1,0:T(8,128)S(1)} %get-tuple-element.29.refs_1_.refs_2_), channel_id=1, source_target_pairs={{4,8},{5,9},{6,10},{7,11},{8,4},{9,5},{10,6},{11,7},{12,16},{13,17... | collective-permute-start | bytes 835592 | tf_op jit(solution)/shard_map/ppermute | solution.py:40
  13.0 5.7 %copy-start = (bf16[2,256,256]{2,1,0:T(8,128)(2,1)S(1)}, bf16[2,256,256]{2,1,0:T(8,128)(2,1)}, u32[]{:S(2)}) copy-start(bf16[2,256,256]{2,1,0:T(8,128)(2,1)} %constant.25.clone.refs_16_) | copy-start | bytes 786436
  18.7 0.7 %copy-start.3 = (s32[16,256]{1,0:T(8,128)S(1)}, s32[16,256]{1,0:T(8,128)}, u32[]{:S(2)}) copy-start(s32[16,256]{1,0:T(8,128)} %refs_14_.1) | copy-start | bytes 49156
  22.0 4.9 %collective-permute-start.4 = (f32[16,256]{1,0:T(8,128)S(1)}, f32[16,256]{1,0:T(8,128)S(1)}, u32[]{:S(2)}, u32[]{:S(2)}) collective-permute-start(f32[16,256]{1,0:T(8,128)S(1)} %get-tuple-element.46), channel_id=1, source_target_pairs={{0,4},{4,0},{8,12},{12,8},{16,20},{20,16},{24,28},{28,24},{1,5},{5... | collective-permute-start | bytes 49160 | tf_op jit(solution)/shard_map/ppermute | solution.py:44
  27.0 3.7 %collective-permute-start.5 = (f32[16,256]{1,0:T(8,128)S(1)}, f32[16,256]{1,0:T(8,128)S(1)}, u32[]{:S(2)}, u32[]{:S(2)}) collective-permute-start(f32[16,256]{1,0:T(8,128)S(1)} %multiply_add_fusion.1), channel_id=1, source_target_pairs={{0,8},{4,12},{8,0},{12,4},{16,24},{20,28},{24,16},{28,20},{1,9},{5... | collective-permute-start | bytes 49160 | tf_op jit(solution)/shard_map/ppermute | solution.py:44
  28.8 3.7 %collective-permute-start.6 = (f32[16,256]{1,0:T(8,128)S(1)}, f32[16,256]{1,0:T(8,128)S(1)}, u32[]{:S(2)}, u32[]{:S(2)}) collective-permute-start(f32[16,256]{1,0:T(8,128)S(1)} %multiply_add_fusion.1), channel_id=1, source_target_pairs={{0,16},{4,20},{8,24},{12,28},{16,0},{20,4},{24,8},{28,12},{1,17},{... | collective-permute-start | bytes 49160 | tf_op jit(solution)/shard_map/ppermute | solution.py:44
  29.2 4.6 %collective-permute-start.7 = (f32[16,256]{1,0:T(8,128)S(1)}, f32[16,256]{1,0:T(8,128)S(1)}, u32[]{:S(2)}, u32[]{:S(2)}) collective-permute-start(f32[16,256]{1,0:T(8,128)S(1)} %multiply_add_fusion.1), channel_id=1, source_target_pairs={{0,24},{4,28},{8,16},{12,20},{16,8},{20,12},{24,0},{28,4},{1,25},{... | collective-permute-start | bytes 49160 | tf_op jit(solution)/shard_map/ppermute | solution.py:44
  33.8 5.9 %collective-permute-start.10 = (f32[16,256]{1,0:T(8,128)S(1)}, f32[16,256]{1,0:T(8,128)S(1)}, u32[]{:S(2)}, u32[]{:S(2)}) collective-permute-start(f32[16,256]{1,0:T(8,128)S(1)} %multiply_add_fusion), channel_id=1, source_target_pairs={{0,3},{1,2},{2,1},{3,0},{4,7},{5,6},{6,5},{7,4},{8,11},{9,10},{10,... | collective-permute-start | bytes 49160 | tf_op jit(solution)/shard_map/ppermute | solution.py:44
  35.3 4.5 %collective-permute-start.8 = (f32[16,256]{1,0:T(8,128)S(1)}, f32[16,256]{1,0:T(8,128)S(1)}, u32[]{:S(2)}, u32[]{:S(2)}) collective-permute-start(f32[16,256]{1,0:T(8,128)S(1)} %multiply_add_fusion), channel_id=1, source_target_pairs={{0,1},{1,0},{2,3},{3,2},{4,5},{5,4},{6,7},{7,6},{8,9},{9,8},{10,11... | collective-permute-start | bytes 49160 | tf_op jit(solution)/shard_map/ppermute | solution.py:44
  36.4 4.6 %collective-permute-start.9 = (f32[16,256]{1,0:T(8,128)S(1)}, f32[16,256]{1,0:T(8,128)S(1)}, u32[]{:S(2)}, u32[]{:S(2)}) collective-permute-start(f32[16,256]{1,0:T(8,128)S(1)} %multiply_add_fusion), channel_id=1, source_target_pairs={{0,2},{1,3},{2,0},{3,1},{4,6},{5,7},{6,4},{7,5},{8,10},{9,11},{10,... | collective-permute-start | bytes 49160 | tf_op jit(solution)/shard_map/ppermute | solution.py:44

commit v5 on v4

--- a/solution.py
+++ b/solution.py
@@ -98,11 +98,18 @@
     return jnp.where(mask, 1.0, 0.0)
 
 
+def position():
+    gx, gy = lax.axis_index("gx"), lax.axis_index("gy")
+    last_gx, last_gy = lax.axis_size("gx") - 1, lax.axis_size("gy") - 1
+    return gx & 1, gy & 1, (gx == 0) | (gx == last_gx), gy == 0, gy == last_gy
+
+
 def move(x, shift):
     return pltpu.roll(x, shift % LANES, 1) if shift % LANES else x
 
 
-def pack_kernel(flags, basis, cond, to_odd, to_even, left, right, held, sems, *, depth, rows, cols):
+def pack_kernel(basis, cond, to_odd, to_even, left, right, held, sems, *, depth, rows, cols):
+    flags = position()
     odd, col_odd = flags[0] == 1, flags[1] == 1
     half = depth // 2
     lane = lax.broadcasted_iota(jnp.int32, (half, LANES), 1)
@@ -172,12 +179,13 @@
 
 
 class Shape:
-    def __init__(self, flags, depth, rows, cols):
+    def __init__(self, depth, rows, cols):
+        flags = self.flags = position()
         self.depth, self.rows, self.cols = depth, rows, cols
         self.half, self.width, self.span = depth // 2, cols + LANES, rows + 2 * HALO
         self.parts = (slice(0, self.half), slice(self.half, depth))
         self.odd, self.col_odd = flags[0] == 1, flags[1] == 1
-        self.edge, self.left, self.right = (flags[i].astype(jnp.float32) for i in range(2, 5))
+        self.edge, self.left, self.right = (jnp.where(flags[i], 1.0, 0.0) for i in range(2, 5))
         self.lane = lax.broadcasted_iota(jnp.int32, (self.half, LANES), 1)
         deep = lax.broadcasted_iota(jnp.int32, (self.half, self.width), 0)
         wide = lax.broadcasted_iota(jnp.int32, (self.half, self.width), 1)
@@ -250,10 +258,10 @@
         here, flux_y = nxt, flux
 
 
-def near_kernel(flags, own_odd, own_even, rows_even, strip_odd, strip_even,
+def near_kernel(own_odd, own_even, rows_even, strip_odd, strip_even,
                 dirn_a, res_a, pre_a, kx_a, ky_a, kz_a, diag_a, saved, edge_half, image_b, pre_b,
                 dirn_b, res_b, kx_b, ky_b, kz_b, diag_b, across, *, depth, rows, cols):
-    sh = Shape(flags, depth, rows, cols)
+    sh = Shape(depth, rows, cols)
     parts = sh.parts
     mid = 2 * HALO
     f = {name: Field() for name in ("dirn", "res", "pre", "kx", "ky", "kz", "diag")}
@@ -325,10 +333,17 @@
     return high, (x - high.astype(jnp.float32)).astype(jnp.bfloat16)
 
 
-def far_kernel(flags, rows_odd, own_odd, dirn_a, res_a, pre_a, kx_a, ky_a, kz_a, diag_a, saved, edge_half, image_b, pre_b,
-               signs, picks, mix, image, pre, sketch_out,
-               dirn, res, kx, ky, kz, diag, across, flip_high, flip_low, *, depth, rows, cols, samples):
-    sh = Shape(flags, depth, rows, cols)
+def far_kernel(rows_odd, own_odd, dirn_a, res_a, pre_a, kx_a, ky_a, kz_a, diag_a, saved, edge_half, image_b, pre_b,
+               signs_hbm, picks_hbm, mix_hbm, image, pre, sketch_out,
+               dirn, res, kx, ky, kz, diag, across, flip_high, flip_low, signs, picks, mix, sems, *, depth, rows, cols, samples):
+    loads = [
+        pltpu.make_async_copy(signs_hbm, signs, sems.at[0]),
+        pltpu.make_async_copy(picks_hbm, picks, sems.at[1]),
+        pltpu.make_async_copy(mix_hbm, mix, sems.at[2]),
+    ]
+    for load in loads:
+        load.start()
+    sh = Shape(depth, rows, cols)
     parts = sh.parts
     f = {name: Field() for name in ("dirn", "res", "pre", "kx", "ky", "kz", "diag")}
     mine = dict(dirn=dirn, res=res, kx=kx, ky=ky, kz=kz, diag=diag)
@@ -387,8 +402,10 @@
             pre[i] = pre_b[i - HALO]
         elif f["pre"].where[HALO + i][0] is not pre:
             pre[i] = pre_a[i]
+    for load in loads:
+        load.wait()
     for r in range(rows):
-        flipped = image[r + flags[0] * (rows - 1 - 2 * r)] * signs[r : r + 1, :].astype(jnp.float32)
+        flipped = image[r + sh.flags[0] * (rows - 1 - 2 * r)] * signs[r : r + 1, :].astype(jnp.float32)
         at = slice(r * depth, (r + 1) * depth)
         flip_high[at], flip_low[at] = split(flipped)
 
@@ -396,15 +413,20 @@
         return lax.dot_general(a, b, (dims, ((), ())), preferred_element_type=jnp.float32)
 
     col_ids = lax.broadcasted_iota(jnp.int32, (samples, cols), 1)
-    chosen = (picks[...] == col_ids).astype(jnp.float32).astype(jnp.bfloat16)
+    sample_ids = lax.broadcasted_iota(jnp.int32, (samples, cols), 0)
+    wanted = jnp.zeros((samples, cols), jnp.int32)
+    for n in range(samples):
+        wanted = jnp.where(sample_ids == n, picks[n], wanted)
+    chosen = flag(wanted == col_ids).astype(jnp.bfloat16)
     picked = dot(chosen, flip_high[...], ((1,), (1,))) + dot(chosen, flip_low[...], ((1,), (1,)))
     high, low = split(picked)
     rest = dot(high, mix[1], ((1,), (0,))) + dot(low, mix[0], ((1,), (0,)))
     sketch_out[...] = dot(high, mix[0], ((1,), (0,))) + rest
 
 
-def tail_kernel(flags, pre, image, precond_out, image_out, *, depth, rows, cols):
+def tail_kernel(pre, image, precond_out, image_out, *, depth, rows, cols):
     half = depth // 2
+    flags = position()
     for c in range(cols // LANES):
         span = slice(c * LANES, (c + 1) * LANES)
         for r in range(0, rows, half):
@@ -416,16 +438,17 @@
                         target[2 * s + t, r : r + half, span] = tile
 
 
+def in_hbm(array):
+    return pltpu.with_memory_space_constraint(array, pltpu.HBM)
+
+
 def whole_step(basis_vec, conductivity, sign_vals, sample_cols):
     depth, rows, cols = basis_vec.shape
     samples = sample_cols.shape[0]
     assert depth == 16 and rows == 2 * HALO and cols == 2 * LANES
     gx_size, gy_size = lax.axis_size("gx"), lax.axis_size("gy")
-    gx_index, gy_index = lax.axis_index("gx"), lax.axis_index("gy")
-    flags = jnp.stack([
-        gx_index & 1, gy_index & 1, (gx_index == 0) | (gx_index == gx_size - 1), gy_index == 0, gy_index == gy_size - 1,
-    ]).astype(jnp.int32)
-    smem, vmem = pl.BlockSpec(memory_space=pltpu.SMEM), pl.BlockSpec(memory_space=pltpu.VMEM)
+    gx_index = lax.axis_index("gx")
+    vmem, hbm = (pl.BlockSpec(memory_space=space) for space in (pltpu.VMEM, pltpu.HBM))
     f32 = jnp.float32
     sizes = dict(depth=depth, rows=rows, cols=cols)
     width, span, mid = cols + LANES, rows + 2 * HALO, 2 * HALO
@@ -437,7 +460,7 @@
     strip = jax.ShapeDtypeStruct((2, depth, LANES), f32)
     own_odd, own_even, strip_to_odd, strip_to_even = pl.pallas_call(
         lambda *refs: pack_kernel(*refs, **sizes),
-        in_specs=[smem] + [pl.BlockSpec(memory_space=pl.ANY)] * 2,
+        in_specs=[hbm] * 2,
         out_specs=[vmem] * 4,
         out_shape=[message, message, strip, strip],
         scratch_shapes=[
@@ -446,7 +469,7 @@
         ],
         compiler_params=small(4),
         name="pack",
-    )(flags, basis_vec, conductivity)
+    )(in_hbm(basis_vec), in_hbm(conductivity))
     strip_even = exchange(strip_to_even, same, even_pair)
     strip_odd = exchange(strip_to_odd, same, odd_pair)
     own_odd, own_even = pl.pallas_call(
@@ -462,35 +485,37 @@
     rows_even = exchange(own_even, even_pair, same)
     *handed, image_b, pre_b = pl.pallas_call(
         lambda *refs: near_kernel(*refs, **sizes),
-        in_specs=[smem] + [vmem] * 5,
+        in_specs=[vmem] * 5,
         out_specs=[vmem] * 11,
         out_shape=[wide(HALO), wide(HALO), slim(HALO), wide(HALO), wide(HALO), wide(HALO), wide(HALO), wide(SWEEPS),
                    jax.ShapeDtypeStruct((depth, width), f32), slim(rows - HALO), slim(rows - HALO)],
         scratch_shapes=[wide_scratch(span - mid)] * 6 + [wide_scratch(span - HALO)],
         compiler_params=small(16),
         name="near",
-    )(flags, own_odd, own_even, rows_even, strip_odd, strip_even)
+    )(own_odd, own_even, rows_even, strip_odd, strip_even)
     mix = hartley_mix(depth, rows, 1.0 / np.sqrt(gx_size))
     mix_high = mix.astype(jnp.bfloat16)
     mix = jnp.asarray(np.stack([mix_high, (mix - mix_high.astype(np.float32)).astype(jnp.bfloat16)]))
     image, pre, current = pl.pallas_call(
         lambda *refs: far_kernel(*refs, samples=samples, **sizes),
-        in_specs=[smem] + [vmem] * 16,
+        in_specs=[vmem] * 13 + [hbm] * 3,
         out_specs=[vmem] * 3,
         out_shape=[slim(rows), slim(rows), jax.ShapeDtypeStruct((samples, depth * rows), f32)],
         scratch_shapes=[wide_scratch(mid)] * 2 + [wide_scratch(HALO)] * 5
-        + [pltpu.VMEM((depth * rows, cols), jnp.bfloat16)] * 2,
+        + [pltpu.VMEM((depth * rows, cols), jnp.bfloat16)] * 2
+        + [pltpu.VMEM((rows, cols), jnp.int32), pltpu.SMEM((samples,), jnp.int32)]
+        + [pltpu.VMEM(mix.shape, jnp.bfloat16), pltpu.SemaphoreType.DMA((3,))],
         compiler_params=small(16),
         name="far",
-    )(flags, rows_odd, own_odd, *handed, image_b, pre_b, sign_vals, sample_cols.reshape(samples, 1), mix)
+    )(rows_odd, own_odd, *handed, image_b, pre_b, in_hbm(sign_vals), in_hbm(sample_cols), in_hbm(mix))
     precond_out, image_out = pl.pallas_call(
         lambda *refs: tail_kernel(*refs, **sizes),
-        in_specs=[smem] + [vmem] * 2,
+        in_specs=[vmem] * 2,
         out_specs=[vmem] * 2,
         out_shape=[jax.ShapeDtypeStruct((depth, rows, cols), f32)] * 2,
         compiler_params=small(8),
         name="tail",
-    )(flags, pre, image)
+    )(pre, image)
     gx_bits = gx_size.bit_length() - 1
     for group in [[0]] + bit_groups(list(range(1, gx_bits))):
         total = walsh_sign(gx_index, 0, group) * current

time: 42 us -> 41.2 us (0.981)
  local copies, waits for them, and re-layouts: 3.53 us -> 0.76 us
  starting transfers between devices: 19.5 us -> 20.7 us
  waiting for transfers between devices: 7.84 us -> 8.69 us
    unnamed x11 -> x1, local copies, waits for them, and re-layouts: 3.36 us -> 0.76 us
    ppermute x7, starting transfers between devices: 12.2 us -> 13.4 us  [swap(): lax.ppermute(array, axis, [(i, i ^ mask) for i in range(lax.axis_size(axi...]
    pallas_call x3, Pallas kernels: 7.47 us -> 6.64 us  [the longest x1 4.33 us: whole_step(): pl.pallas_call(lambda *refs: near_kernel(*refs, **sizes), in_specs=[vmem]...]
    pallas_call x1, Pallas kernels: 2.6 us -> 3.36 us  [whole_step(): pl.pallas_call(lambda *refs: far_kernel(*refs, samples=samples, **sizes),...]
    ppermute x7, waiting for transfers between devices: 5.37 us -> 6.11 us  [swap(): lax.ppermute(array, axis, [(i, i ^ mask) for i in range(lax.axis_size(axi...]
  transfers between devices with their start and end apart: 11 -> 11, of which waited for: 7 -> 7; matrix products, arithmetic and copies ran while one was open for 0% -> 0% of each run, Pallas kernels for 15% -> 13%
where the time goes in v5:
time: 41.2 us; the launch traced here: 41 us
  starting transfers between devices  20.7 us (50%)
  Pallas kernels  10.1 us (25%)
  waiting for transfers between devices  8.69 us (21%)
  local copies, waits for them, and re-layouts  0.76 us (2%)
  between operations  0.7 us (2%)
    ppermute x7, starting transfers between devices, swap(): lax.ppermute(array, axis, [(i, i ^ mask) for i in range(lax.axis_size(axi...  13.4 us
    ppermute x4, starting transfers between devices, exchange(): return lax.ppermute(array, AXES, pairs)  7.32 us
    ppermute x7, waiting for transfers between devices, swap(): lax.ppermute(array, axis, [(i, i ^ mask) for i in range(lax.axis_size(axi...  6.11 us
    pallas_call x1, Pallas kernels, whole_step(): pl.pallas_call(lambda *refs: near_kernel(*refs, **sizes), in_specs=[vmem]...  4.33 us
    pallas_call x1, Pallas kernels, whole_step(): pl.pallas_call(lambda *refs: far_kernel(*refs, samples=samples, **sizes),...  3.36 us
    ppermute x4, waiting for transfers between devices, exchange(): return lax.ppermute(array, AXES, pairs)  2.58 us
    pallas_call x1, Pallas kernels, whole_step(): pl.pallas_call(lambda *refs: pack_kernel(*refs, **sizes), in_specs=[hbm]...  1.42 us
    pallas_call x1, Pallas kernels, whole_step(): pl.pallas_call(lambda *refs: tail_kernel(*refs, **sizes), in_specs=[vmem]...  0.9 us
  transfers between devices with their start and end apart: 11, of which 7 were waited for; matrix products, arithmetic and copies ran while one was open for 0% of the time, Pallas kernels for 13%

profile of v5, /device:TPU:0, one launch (start us, length us, event | category | flops | bytes accessed | tf_op | source)
XLA Modules:
  0.0 41.0 jit_solution(17003500495709256259)
XLA Ops:
  0.6 1.4 %pack.1 = (f32[17,16,256]{2,1,0:T(8,128)S(1)}, f32[17,16,256]{2,1,0:T(8,128)S(1)}, f32[2,16,128]{2,1,0:T(8,128)S(1)}, f32[2,16,128]{2,1,0:T(8,128)S(1)}) custom-call(f32[16,16,256]{2,1,0:T(8,128)} %refs_0_.1, f32[16,16,256]{2,1,0:T(8,128)} %refs_1_.1), custom_call_target="tpu_custom_call" | custom-call | tf_op jit(solution)/shard_map/pack/pallas_call | solution.py:461
  2.1 0.7 %collective-permute-start = (f32[2,16,128]{2,1,0:T(8,128)S(1)}, f32[2,16,128]{2,1,0:T(8,128)S(1)}, u32[]{:S(2)}, u32[]{:S(2)}) collective-permute-start(f32[2,16,128]{2,1,0:T(8,128)S(1)} %get-tuple-element.27), channel_id=1, source_target_pairs={{1,2},{2,1},{5,6},{6,5},{9,10},{10,9},{13,14},{14,13},{17,18},{18,... | collective-permute-start | bytes 49160 | tf_op jit(solution)/shard_map/ppermute | solution.py:40
  2.7 5.9 %collective-permute-start.1 = (f32[2,16,128]{2,1,0:T(8,128)S(1)}, f32[2,16,128]{2,1,0:T(8,128)S(1)}, u32[]{:S(2)}, u32[]{:S(2)}) collective-permute-start(f32[2,16,128]{2,1,0:T(8,128)S(1)} %get-tuple-element.28), channel_id=1, source_target_pairs={{0,1},{1,0},{2,3},{3,2},{4,5},{5,4},{6,7},{7,6},{8,9},{9,8},{10,11... | collective-permute-start | bytes 49160 | tf_op jit(solution)/shard_map/ppermute | solution.py:40
  8.7 0.0 collective-permute-done.refs_2_.refs_3_
  8.7 1.7 %collective-permute-done.1.refs_3_.refs_4_ = f32[2,16,128]{2,1,0:T(8,128)S(1)} collective-permute-done((f32[2,16,128]{2,1,0:T(8,128)S(1)}, f32[2,16,128]{2,1,0:T(8,128)S(1)}, u32[]{:S(2)}, u32[]{:S(2)}) %collective-permute-start.1) | collective-permute-done | bytes 16416 | tf_op jit(solution)/shard_map/ppermute | solution.py:40
  10.4 0.1 corners.1
  10.5 0.0 collective-permute-start.3
  10.5 0.7 %collective-permute-start.2 = (f32[17,16,256]{2,1,0:T(8,128)S(1)}, f32[17,16,256]{2,1,0:T(8,128)S(1)}, u32[]{:S(2)}, u32[]{:S(2)}) collective-permute-start(f32[17,16,256]{2,1,0:T(8,128)S(1)} %get-tuple-element.29.refs_0_.refs_1_), channel_id=1, source_target_pairs={{4,8},{5,9},{6,10},{7,11},{8,4},{9,5},{10,6},{11,7},{12,16},{13,17... | collective-permute-start | bytes 835592 | tf_op jit(solution)/shard_map/ppermute | solution.py:40
  11.2 0.9 %collective-permute-done.3.refs_2_ = f32[17,16,256]{2,1,0:T(8,128)S(1)} collective-permute-done((f32[17,16,256]{2,1,0:T(8,128)S(1)}, f32[17,16,256]{2,1,0:T(8,128)S(1)}, u32[]{:S(2)}, u32[]{:S(2)}) %collective-permute-start.3) | collective-permute-done | bytes 278560 | tf_op jit(solution)/shard_map/ppermute | solution.py:40
  12.1 4.3 %near.1 = (f32[8,16,384]{2,1,0:T(8,128)S(1)}, f32[8,16,384]{2,1,0:T(8,128)S(1)}, f32[8,16,256]{2,1,0:T(8,128)S(1)}, f32[8,16,384]{2,1,0:T(8,128)S(1)}, f32[8,16,...) custom-call(f32[17,16,256]{2,1,0:T(8,128)S(1)} %get-tuple-element.29, ...), custom_call_target="tpu_custom_call" | custom-call | tf_op jit(solution)/shard_map/near/pallas_call | solution.py:486
  16.4 0.0 collective-permute-done.2.refs_0_
  16.4 3.4 %far.1 = (f32[16,16,256]{2,1,0:T(8,128)S(1)}, f32[16,16,256]{2,1,0:T(8,128)S(1)}, f32[16,256]{1,0:T(8,128)S(1)}) custom-call(f32[17,16,256]{2,1,0:T(8,128)S(1)} %collective-permute-done.2.refs_0_, f32[17,16,256]{2,1,0:T(8,128)S(1)} %get-tuple-element.29.refs_0_.refs_1_, f32[8,16,384]{2,1,0:T(8,128)S(1)} %get-tuple-element.31.refs_2_, ...), custom_call_target="tpu_custom_call" | custom-call | tf_op jit(solution)/shard_map/far/pallas_call | solution.py:499
  19.8 5.2 %collective-permute-start.4 = (f32[16,256]{1,0:T(8,128)S(1)}, f32[16,256]{1,0:T(8,128)S(1)}, u32[]{:S(2)}, u32[]{:S(2)}) collective-permute-start(f32[16,256]{1,0:T(8,128)S(1)} %get-tuple-element.46), channel_id=1, source_target_pairs={{0,4},{4,0},{8,12},{12,8},{16,20},{20,16},{24,28},{28,24},{1,5},{5... | collective-permute-start | bytes 49160 | tf_op jit(solution)/shard_map/ppermute | solution.py:44
  25.0 0.8 %collective-permute-done.4 = f32[16,256]{1,0:T(8,128)S(1)} collective-permute-done((f32[16,256]{1,0:T(8,128)S(1)}, f32[16,256]{1,0:T(8,128)S(1)}, u32[]{:S(2)}, u32[]{:S(2)}) %collective-permute-start.4) | collective-permute-done | bytes 16416 | tf_op jit(solution)/shard_map/ppermute | solution.py:44
  25.8 2.1 %collective-permute-start.5 = (f32[16,256]{1,0:T(8,128)S(1)}, f32[16,256]{1,0:T(8,128)S(1)}, u32[]{:S(2)}, u32[]{:S(2)}) collective-permute-start(f32[16,256]{1,0:T(8,128)S(1)} %multiply_add_fusion.1), channel_id=1, source_target_pairs={{0,8},{4,12},{8,0},{12,4},{16,24},{20,28},{24,16},{28,20},{1,9},{5... | collective-permute-start | bytes 49160 | tf_op jit(solution)/shard_map/ppermute | solution.py:44
  27.9 0.5 %collective-permute-start.6 = (f32[16,256]{1,0:T(8,128)S(1)}, f32[16,256]{1,0:T(8,128)S(1)}, u32[]{:S(2)}, u32[]{:S(2)}) collective-permute-start(f32[16,256]{1,0:T(8,128)S(1)} %multiply_add_fusion.1), channel_id=1, source_target_pairs={{0,16},{4,20},{8,24},{12,28},{16,0},{20,4},{24,8},{28,12},{1,17},{... | collective-permute-start | bytes 49160 | tf_op jit(solution)/shard_map/ppermute | solution.py:44
  28.4 1.2 %collective-permute-start.7 = (f32[16,256]{1,0:T(8,128)S(1)}, f32[16,256]{1,0:T(8,128)S(1)}, u32[]{:S(2)}, u32[]{:S(2)}) collective-permute-start(f32[16,256]{1,0:T(8,128)S(1)} %multiply_add_fusion.1), channel_id=1, source_target_pairs={{0,24},{4,28},{8,16},{12,20},{16,8},{20,12},{24,0},{28,4},{1,25},{... | collective-permute-start | bytes 49160 | tf_op jit(solution)/shard_map/ppermute | solution.py:44
  29.6 0.0 collective-permute-done.5
  29.6 2.0 %collective-permute-done.6 = f32[16,256]{1,0:T(8,128)S(1)} collective-permute-done((f32[16,256]{1,0:T(8,128)S(1)}, f32[16,256]{1,0:T(8,128)S(1)}, u32[]{:S(2)}, u32[]{:S(2)}) %collective-permute-start.6) | collective-permute-done | bytes 16416 | tf_op jit(solution)/shard_map/ppermute | solution.py:44
  31.7 1.4 %collective-permute-done.7 = f32[16,256]{1,0:T(8,128)S(1)} collective-permute-done((f32[16,256]{1,0:T(8,128)S(1)}, f32[16,256]{1,0:T(8,128)S(1)}, u32[]{:S(2)}, u32[]{:S(2)}) %collective-permute-start.7) | collective-permute-done | bytes 16416 | tf_op jit(solution)/shard_map/ppermute | solution.py:44
  33.0 1.4 %collective-permute-start.10 = (f32[16,256]{1,0:T(8,128)S(1)}, f32[16,256]{1,0:T(8,128)S(1)}, u32[]{:S(2)}, u32[]{:S(2)}) collective-permute-start(f32[16,256]{1,0:T(8,128)S(1)} %multiply_add_fusion), channel_id=1, source_target_pairs={{0,3},{1,2},{2,1},{3,0},{4,7},{5,6},{6,5},{7,4},{8,11},{9,10},{10,... | collective-permute-start | bytes 49160 | tf_op jit(solution)/shard_map/ppermute | solution.py:44
  34.4 1.1 %collective-permute-start.8 = (f32[16,256]{1,0:T(8,128)S(1)}, f32[16,256]{1,0:T(8,128)S(1)}, u32[]{:S(2)}, u32[]{:S(2)}) collective-permute-start(f32[16,256]{1,0:T(8,128)S(1)} %multiply_add_fusion), channel_id=1, source_target_pairs={{0,1},{1,0},{2,3},{3,2},{4,5},{5,4},{6,7},{7,6},{8,9},{9,8},{10,11... | collective-permute-start | bytes 49160 | tf_op jit(solution)/shard_map/ppermute | solution.py:44
  35.6 1.9 %collective-permute-start.9 = (f32[16,256]{1,0:T(8,128)S(1)}, f32[16,256]{1,0:T(8,128)S(1)}, u32[]{:S(2)}, u32[]{:S(2)}) collective-permute-start(f32[16,256]{1,0:T(8,128)S(1)} %multiply_add_fusion), channel_id=1, source_target_pairs={{0,2},{1,3},{2,0},{3,1},{4,6},{5,7},{6,4},{7,5},{8,10},{9,11},{10,... | collective-permute-start | bytes 49160 | tf_op jit(solution)/shard_map/ppermute | solution.py:44
  37.5 0.9 %tail.1 = (f32[16,16,256]{2,1,0:T(8,128)}, f32[16,16,256]{2,1,0:T(8,128)}) custom-call(f32[16,16,256]{2,1,0:T(8,128)S(1)} %get-tuple-element.42.refs_0_, f32[16,16,256]{2,1,0:T(8,128)S(1)} %get-tuple-element.43.refs_1_), custom_call_target="tpu_custom_call" | custom-call | tf_op jit(solution)/shard_map/tail/pallas_call | solution.py:511
  38.4 0.3 collective-permute-done.10
  38.6 0.0 collective-permute-done.8
  38.6 1.6 %collective-permute-done.9 = f32[16,256]{1,0:T(8,128)S(1)} collective-permute-done((f32[16,256]{1,0:T(8,128)S(1)}, f32[16,256]{1,0:T(8,128)S(1)}, u32[]{:S(2)}, u32[]{:S(2)}) %collective-permute-start.9) | collective-permute-done | bytes 16416 | tf_op jit(solution)/shard_map/ppermute | solution.py:44
  40.2 0.8 %copy.11 = f32[256,16]{1,0:T(8,128)} copy(f32[256,16]{0,1:T(8,128)S(1)} %add_bitcast_fusion) | data formatting | bytes 32768
  (3 shorter events, 0.0 us)
Async XLA Ops:
  2.1 6.6 %collective-permute-start = (f32[2,16,128]{2,1,0:T(8,128)S(1)}, f32[2,16,128]{2,1,0:T(8,128)S(1)}, u32[]{:S(2)}, u32[]{:S(2)}) collective-permute-start(f32[2,16,128]{2,1,0:T(8,128)S(1)} %get-tuple-element.27), channel_id=1, source_target_pairs={{1,2},{2,1},{5,6},{6,5},{9,10},{10,9},{13,14},{14,13},{17,18},{18,... | collective-permute-start | bytes 49160 | tf_op jit(solution)/shard_map/ppermute | solution.py:40
  2.7 7.7 %collective-permute-start.1 = (f32[2,16,128]{2,1,0:T(8,128)S(1)}, f32[2,16,128]{2,1,0:T(8,128)S(1)}, u32[]{:S(2)}, u32[]{:S(2)}) collective-permute-start(f32[2,16,128]{2,1,0:T(8,128)S(1)} %get-tuple-element.28), channel_id=1, source_target_pairs={{0,1},{1,0},{2,3},{3,2},{4,5},{5,4},{6,7},{7,6},{8,9},{9,8},{10,11... | collective-permute-start | bytes 49160 | tf_op jit(solution)/shard_map/ppermute | solution.py:40
  10.5 1.6 %collective-permute-start.3 = (f32[17,16,256]{2,1,0:T(8,128)S(1)}, f32[17,16,256]{2,1,0:T(8,128)S(1)}, u32[]{:S(2)}, u32[]{:S(2)}) collective-permute-start(f32[17,16,256]{2,1,0:T(8,128)S(1)} %get-tuple-element.30.refs_1_), channel_id=1, source_target_pairs={{0,4},{1,5},{2,6},{3,7},{4,0},{5,1},{6,2},{7,3},{8,12},{9,13},{10,... | collective-permute-start | bytes 835592 | tf_op jit(solution)/shard_map/ppermute | solution.py:40
  10.5 5.9 %collective-permute-start.2 = (f32[17,16,256]{2,1,0:T(8,128)S(1)}, f32[17,16,256]{2,1,0:T(8,128)S(1)}, u32[]{:S(2)}, u32[]{:S(2)}) collective-permute-start(f32[17,16,256]{2,1,0:T(8,128)S(1)} %get-tuple-element.29.refs_0_.refs_1_), channel_id=1, source_target_pairs={{4,8},{5,9},{6,10},{7,11},{8,4},{9,5},{10,6},{11,7},{12,16},{13,17... | collective-permute-start | bytes 835592 | tf_op jit(solution)/shard_map/ppermute | solution.py:40
  19.8 6.1 %collective-permute-start.4 = (f32[16,256]{1,0:T(8,128)S(1)}, f32[16,256]{1,0:T(8,128)S(1)}, u32[]{:S(2)}, u32[]{:S(2)}) collective-permute-start(f32[16,256]{1,0:T(8,128)S(1)} %get-tuple-element.46), channel_id=1, source_target_pairs={{0,4},{4,0},{8,12},{12,8},{16,20},{20,16},{24,28},{28,24},{1,5},{5... | collective-permute-start | bytes 49160 | tf_op jit(solution)/shard_map/ppermute | solution.py:44
  25.8 3.8 %collective-permute-start.5 = (f32[16,256]{1,0:T(8,128)S(1)}, f32[16,256]{1,0:T(8,128)S(1)}, u32[]{:S(2)}, u32[]{:S(2)}) collective-permute-start(f32[16,256]{1,0:T(8,128)S(1)} %multiply_add_fusion.1), channel_id=1, source_target_pairs={{0,8},{4,12},{8,0},{12,4},{16,24},{20,28},{24,16},{28,20},{1,9},{5... | collective-permute-start | bytes 49160 | tf_op jit(solution)/shard_map/ppermute | solution.py:44
  27.9 3.8 %collective-permute-start.6 = (f32[16,256]{1,0:T(8,128)S(1)}, f32[16,256]{1,0:T(8,128)S(1)}, u32[]{:S(2)}, u32[]{:S(2)}) collective-permute-start(f32[16,256]{1,0:T(8,128)S(1)} %multiply_add_fusion.1), channel_id=1, source_target_pairs={{0,16},{4,20},{8,24},{12,28},{16,0},{20,4},{24,8},{28,12},{1,17},{... | collective-permute-start | bytes 49160 | tf_op jit(solution)/shard_map/ppermute | solution.py:44
  28.4 4.6 %collective-permute-start.7 = (f32[16,256]{1,0:T(8,128)S(1)}, f32[16,256]{1,0:T(8,128)S(1)}, u32[]{:S(2)}, u32[]{:S(2)}) collective-permute-start(f32[16,256]{1,0:T(8,128)S(1)} %multiply_add_fusion.1), channel_id=1, source_target_pairs={{0,24},{4,28},{8,16},{12,20},{16,8},{20,12},{24,0},{28,4},{1,25},{... | collective-permute-start | bytes 49160 | tf_op jit(solution)/shard_map/ppermute | solution.py:44
  33.0 5.6 %collective-permute-start.10 = (f32[16,256]{1,0:T(8,128)S(1)}, f32[16,256]{1,0:T(8,128)S(1)}, u32[]{:S(2)}, u32[]{:S(2)}) collective-permute-start(f32[16,256]{1,0:T(8,128)S(1)} %multiply_add_fusion), channel_id=1, source_target_pairs={{0,3},{1,2},{2,1},{3,0},{4,7},{5,6},{6,5},{7,4},{8,11},{9,10},{10,... | collective-permute-start | bytes 49160 | tf_op jit(solution)/shard_map/ppermute | solution.py:44
  34.4 4.2 %collective-permute-start.8 = (f32[16,256]{1,0:T(8,128)S(1)}, f32[16,256]{1,0:T(8,128)S(1)}, u32[]{:S(2)}, u32[]{:S(2)}) collective-permute-start(f32[16,256]{1,0:T(8,128)S(1)} %multiply_add_fusion), channel_id=1, source_target_pairs={{0,1},{1,0},{2,3},{3,2},{4,5},{5,4},{6,7},{7,6},{8,9},{9,8},{10,11... | collective-permute-start | bytes 49160 | tf_op jit(solution)/shard_map/ppermute | solution.py:44
  35.6 4.6 %collective-permute-start.9 = (f32[16,256]{1,0:T(8,128)S(1)}, f32[16,256]{1,0:T(8,128)S(1)}, u32[]{:S(2)}, u32[]{:S(2)}) collective-permute-start(f32[16,256]{1,0:T(8,128)S(1)} %multiply_add_fusion), channel_id=1, source_target_pairs={{0,2},{1,3},{2,0},{3,1},{4,6},{5,7},{6,4},{7,5},{8,10},{9,11},{10,... | collective-permute-start | bytes 49160 | tf_op jit(solution)/shard_map/ppermute | solution.py:44
